TPU v7x, 32 devices: a whole 2x2x4 slice. The times are simulated.
32 devices in a mesh: dp: 16 (over z, y, x), fsdp: 2 (over core).
Axes of the slice: x: 2, y: 2, z: 4, core: 2. Of those that a mesh axis runs over, the one named last changes fastest.
Arguments:
- tokens: bfloat16 [32, 256, 1152], P(('dp', 'fsdp')), may hold values from -6 to 6
- condition: bfloat16 [32, 1152], P(('dp', 'fsdp')), may hold values from -6 to 6
- cotangent: bfloat16 [32, 256, 1152], P(('dp', 'fsdp')), may hold values from -6 to 6
- image_grids: int32 [32, 2], P(('dp', 'fsdp')), may hold values from 12 to 20, as said below
- noise_bins: int32 [32], P(('dp', 'fsdp')), may hold values from 0 to 15, as said below
- bin_weights: int32 [16], replicated, may hold values from 1 to 4
- w_qkv: bfloat16 [1152, 3456], P('dp', 'fsdp'), may hold values from -0.1875 to 0.1875
- b_query: float32 [1152], replicated, may hold values from -3 to 3
- b_value: float32 [1152], replicated, may hold values from -0.625 to 0.625
- w_proj: bfloat16 [1152, 1152], P('dp', 'fsdp'), may hold values from -1.5 to 1.5
- b_proj: float32 [1152], replicated, may hold values from -1.75 to 1.75
- w_fc1: bfloat16 [1152, 4608], P('dp', 'fsdp'), may hold values from -0.1875 to 0.1875
- b_fc1: float32 [4608], replicated, may hold values from -3 to 3
- w_fc2: bfloat16 [4608, 1152], P('dp', 'fsdp'), may hold values from -0.09375 to 0.09375
- b_fc2: float32 [1152], replicated, may hold values from -1.75 to 1.75
- w_ada: bfloat16 [6912, 1152], replicated, may hold values from -0.1875 to 0.1875
- b_ada: float32 [6912], replicated, may hold values from -1.75 to 1.75
Outputs:
- result: bfloat16 [32, 256, 1152], P(('dp', 'fsdp'))
- grad_tokens: bfloat16 [32, 256, 1152], P(('dp', 'fsdp'))
- grad_condition: float32 [32, 1152], P(('dp', 'fsdp'))
- grad_w_qkv: float32 [1152, 3456], P('dp', 'fsdp')
- grad_b_query: float32 [1152], replicated
- grad_b_value: float32 [1152], replicated
- grad_w_proj: float32 [1152, 1152], P('dp', 'fsdp')
- grad_b_proj: float32 [1152], replicated
- grad_w_fc1: float32 [1152, 4608], P('dp', 'fsdp')
- grad_b_fc1: float32 [4608], replicated
- grad_w_fc2: float32 [4608, 1152], P('dp', 'fsdp')
- grad_b_fc2: float32 [1152], replicated
- grad_w_ada: float32 [6912, 1152], P(('dp', 'fsdp'))
- grad_b_ada: float32 [6912], replicated
Inputs may be any that keep to these rules, and one draw needn't show every extreme that they name: `image_grids`: each row is a height and a width that sum to 32; an image's tokens are the first height * width of its 256 slots. `noise_bins`: bin ids never fall along the image slots, and every bin holds at least one image.
All inputs are finite; a program needn't handle non-finite values.
Results may differ from a plain program's by a relative error of at most 0.014.
The roundings to bfloat16 on the way count: a program that leaves them out, or rounds other values in their place, can miss the bound.
Values may be sent and summed in bfloat16 or wider, within the bound.
A program may use at most 256 MiB of HBM per device.

v0:
```python
import jax
import jax.numpy as jnp
from jax import lax
from jax.sharding import PartitionSpec as P

D = 1152
H = 16
HD = 72
BINS = 16
SEQ = 256


NEG_FILL = -1e30
NORM_EPS = 1e-06
GELU_COEF = 0.7978845608028654
CUBIC_COEF = 0.044715
ROWS_DIMS = (((0,), (0,)), ((), ()))
LAST_DIMS = (((1,), (1,)), ((), ()))


def gelu_tanh(values_in):
    return (
        0.5
        * values_in
        * (1.0 + jnp.tanh(GELU_COEF * (values_in + CUBIC_COEF * values_in * values_in * values_in)))
    )


def norm_rows(inputs):
    centered = inputs - jnp.mean(inputs, axis=-1, keepdims=True)
    inverse = lax.rsqrt(jnp.mean(centered * centered, axis=-1, keepdims=True) + NORM_EPS)
    return (centered * inverse, inverse)


def norm_back(grad_normed, normed, inverse):
    centered_grad = grad_normed - jnp.mean(grad_normed, axis=-1, keepdims=True)
    return inverse * (
        centered_grad - normed * jnp.mean(grad_normed * normed, axis=-1, keepdims=True)
    )


def collect_trunk(w_qkv, w_proj, w_fc1, w_fc2):
    paired = (
        lax.all_gather(w_qkv, "fsdp", axis=1, tiled=True),
        lax.all_gather(w_proj, "fsdp", axis=1, tiled=True),
        lax.all_gather(w_fc1, "fsdp", axis=1, tiled=True),
        lax.all_gather(w_fc2, "fsdp", axis=1, tiled=True),
    )
    return (
        lax.all_gather(paired[0], "dp", axis=0, tiled=True),
        lax.all_gather(paired[1], "dp", axis=0, tiled=True),
        lax.all_gather(paired[2], "dp", axis=0, tiled=True),
        lax.all_gather(paired[3], "dp", axis=0, tiled=True),
    )


def masked_scores(query, keys, valid_keys):
    scaled = jnp.einsum(
        "blhc,bmhc->bhlm", query, keys, preferred_element_type=jnp.float32
    ) * HD ** (-0.5)
    return jnp.where(valid_keys[:, None, None, :], scaled, NEG_FILL)


def shards(
    tokens,
    condition,
    cotangent,
    image_grids,
    noise_bins,
    bin_weights,
    w_qkv,
    b_query,
    b_value,
    w_proj,
    b_proj,
    w_fc1,
    b_fc1,
    w_fc2,
    b_fc2,
    w_ada,
    b_ada,
):
    images = tokens.shape[0]
    row_count = images * SEQ
    token_count = image_grids[:, 0] * image_grids[:, 1]
    valid_keys = lax.broadcasted_iota(jnp.int32, (images, SEQ), 1) < token_count[:, None]
    bin_table = (noise_bins[:, None] == lax.broadcasted_iota(jnp.int32, (images, BINS), 1)).astype(
        jnp.float32
    )
    local_counts = jnp.sum(bin_table * token_count[:, None].astype(jnp.float32), axis=0)
    counts = lax.psum(local_counts, ("dp", "fsdp"))
    bin_scale = bin_weights.astype(jnp.float32) * (jnp.sum(counts) / BINS) / counts
    image_scale = jnp.sum(bin_table * bin_scale[None, :], axis=1)
    full_qkv, full_proj, full_fc1, full_fc2 = collect_trunk(w_qkv, w_proj, w_fc1, w_fc2)
    cond_float = condition.astype(jnp.float32)
    silu_cond = jax.nn.silu(cond_float).astype(jnp.bfloat16)
    modul = lax.dot_general(silu_cond, w_ada, LAST_DIMS, preferred_element_type=jnp.float32) + b_ada
    pieces = [modul[:, None, part_index * D : (part_index + 1) * D] for part_index in range(6)]
    shift_one, scale_one, gate_one, shift_two, scale_two, gate_two = pieces
    token_float = tokens.astype(jnp.float32)
    normed_one, inverse_one = norm_rows(token_float)
    attn_in = (
        (normed_one * (1.0 + scale_one) + shift_one).astype(jnp.bfloat16).reshape(row_count, D)
    )
    bias_qkv = jnp.concatenate([b_query, jnp.zeros_like(b_query), b_value])
    qkv_all = (jnp.dot(attn_in, full_qkv, preferred_element_type=jnp.float32) + bias_qkv).astype(
        jnp.bfloat16
    )
    qkv_heads = qkv_all.reshape(images, SEQ, 3, H, HD)
    query, keys, values = (qkv_heads[:, :, 0], qkv_heads[:, :, 1], qkv_heads[:, :, 2])
    scores = masked_scores(query, keys, valid_keys)
    row_max = jnp.max(scores, axis=-1, keepdims=True)
    exponent = jnp.exp(scores - row_max)
    row_total = jnp.sum(exponent, axis=-1, keepdims=True)
    soft_probs = exponent / row_total
    log_total = row_max + jnp.log(row_total)
    attended = jnp.einsum(
        "bhlm,bmhc->blhc",
        soft_probs.astype(jnp.bfloat16),
        values,
        preferred_element_type=jnp.float32,
    )
    attended = attended.astype(jnp.bfloat16).reshape(row_count, D)
    attn_out = (jnp.dot(attended, full_proj, preferred_element_type=jnp.float32) + b_proj).reshape(
        images, SEQ, D
    )
    middle = token_float + gate_one * attn_out
    normed_two, inverse_two = norm_rows(middle)
    mlp_in = (normed_two * (1.0 + scale_two) + shift_two).astype(jnp.bfloat16).reshape(row_count, D)
    hidden = jnp.dot(mlp_in, full_fc1, preferred_element_type=jnp.float32) + b_fc1
    active = gelu_tanh(hidden).astype(jnp.bfloat16)
    branch = (jnp.dot(active, full_fc2, preferred_element_type=jnp.float32) + b_fc2).reshape(
        images, SEQ, D
    )
    result = (middle + gate_two * branch).astype(jnp.bfloat16)
    back_qkv, back_proj, back_fc1, back_fc2 = (full_qkv, full_proj, full_fc1, full_fc2)
    grad_out = (
        cotangent.astype(jnp.float32)
        * (valid_keys.astype(jnp.float32) * image_scale[:, None])[:, :, None]
    )
    d_gate_two = jnp.sum(grad_out * branch, axis=1)
    d_branch = (gate_two * grad_out).astype(jnp.bfloat16).reshape(row_count, D)
    grad_fc2 = lax.dot_general(active, d_branch, ROWS_DIMS, preferred_element_type=jnp.float32)
    bias_fc2 = jnp.sum(d_branch, axis=0, dtype=jnp.float32)
    d_active = lax.dot_general(d_branch, back_fc2, LAST_DIMS, preferred_element_type=jnp.float32)
    gelu_pull = jax.vjp(gelu_tanh, hidden)[1]
    d_hidden = gelu_pull(d_active)[0].astype(jnp.bfloat16)
    grad_fc1 = lax.dot_general(mlp_in, d_hidden, ROWS_DIMS, preferred_element_type=jnp.float32)
    bias_fc1 = jnp.sum(d_hidden, axis=0, dtype=jnp.float32)
    d_mlp_in = lax.dot_general(
        d_hidden, back_fc1, LAST_DIMS, preferred_element_type=jnp.float32
    ).reshape(images, SEQ, D)
    d_shift_two = jnp.sum(d_mlp_in, axis=1)
    d_scale_two = jnp.sum(d_mlp_in * normed_two, axis=1)
    d_middle = grad_out + norm_back(d_mlp_in * (1.0 + scale_two), normed_two, inverse_two)
    d_gate_one = jnp.sum(d_middle * attn_out, axis=1)
    d_attn = (gate_one * d_middle).astype(jnp.bfloat16).reshape(row_count, D)
    grad_proj = lax.dot_general(attended, d_attn, ROWS_DIMS, preferred_element_type=jnp.float32)
    bias_proj = jnp.sum(d_attn, axis=0, dtype=jnp.float32)
    d_attended = lax.dot_general(d_attn, back_proj, LAST_DIMS, preferred_element_type=jnp.float32)
    d_attended = d_attended.astype(jnp.bfloat16).reshape(images, SEQ, H, HD)
    soft_again = jnp.exp(masked_scores(query, keys, valid_keys) - log_total)
    grad_values = jnp.einsum(
        "bhlm,blhc->bmhc",
        soft_again.astype(jnp.bfloat16),
        d_attended,
        preferred_element_type=jnp.float32,
    )
    d_probs = jnp.einsum("blhc,bmhc->bhlm", d_attended, values, preferred_element_type=jnp.float32)
    d_scores = soft_again * (d_probs - jnp.sum(soft_again * d_probs, axis=-1, keepdims=True))
    d_scores = jnp.where(valid_keys[:, None, None, :], d_scores, 0.0).astype(jnp.bfloat16)
    grad_query = jnp.einsum(
        "bhlm,bmhc->blhc", d_scores, keys, preferred_element_type=jnp.float32
    ) * HD ** (-0.5)
    grad_keys = jnp.einsum(
        "bhlm,blhc->bmhc", d_scores, query, preferred_element_type=jnp.float32
    ) * HD ** (-0.5)
    d_qkv = (
        jnp.stack([grad_query, grad_keys, grad_values], axis=2)
        .astype(jnp.bfloat16)
        .reshape(row_count, 3 * D)
    )
    grad_qkv = lax.dot_general(attn_in, d_qkv, ROWS_DIMS, preferred_element_type=jnp.float32)
    bias_query = jnp.sum(d_qkv[:, :D], axis=0, dtype=jnp.float32)
    bias_value = jnp.sum(d_qkv[:, 2 * D :], axis=0, dtype=jnp.float32)
    d_attn_in = lax.dot_general(
        d_qkv, back_qkv, LAST_DIMS, preferred_element_type=jnp.float32
    ).reshape(images, SEQ, D)
    d_shift_one = jnp.sum(d_attn_in, axis=1)
    d_scale_one = jnp.sum(d_attn_in * normed_one, axis=1)
    grad_tokens = (
        d_middle + norm_back(d_attn_in * (1.0 + scale_one), normed_one, inverse_one)
    ).astype(jnp.bfloat16)
    d_modul = jnp.concatenate(
        [d_shift_one, d_scale_one, d_gate_one, d_shift_two, d_scale_two, d_gate_two], axis=1
    ).astype(jnp.bfloat16)
    silu_pull = jax.vjp(jax.nn.silu, cond_float)[1]
    grad_condition = silu_pull(jnp.dot(d_modul, w_ada, preferred_element_type=jnp.float32))[0]
    bias_ada = jnp.sum(d_modul, axis=0, dtype=jnp.float32)
    spread_dp = (
        lax.psum_scatter(grad_qkv, "dp", scatter_dimension=0, tiled=True),
        lax.psum_scatter(grad_proj, "dp", scatter_dimension=0, tiled=True),
        lax.psum_scatter(grad_fc1, "dp", scatter_dimension=0, tiled=True),
        lax.psum_scatter(grad_fc2, "dp", scatter_dimension=0, tiled=True),
    )
    owned = (
        lax.psum_scatter(
            spread_dp[0].astype(jnp.bfloat16), "fsdp", scatter_dimension=1, tiled=True
        ).astype(jnp.float32),
        lax.psum_scatter(
            spread_dp[1].astype(jnp.bfloat16), "fsdp", scatter_dimension=1, tiled=True
        ).astype(jnp.float32),
        lax.psum_scatter(
            spread_dp[2].astype(jnp.bfloat16), "fsdp", scatter_dimension=1, tiled=True
        ).astype(jnp.float32),
        lax.psum_scatter(
            spread_dp[3].astype(jnp.bfloat16), "fsdp", scatter_dimension=1, tiled=True
        ).astype(jnp.float32),
    )
    summed_bias = lax.psum(
        (bias_query, bias_value, bias_proj, bias_fc1, bias_fc2, bias_ada), ("dp", "fsdp")
    )
    share_rows = 6 * D // lax.axis_size(("dp", "fsdp"))
    own_start = lax.axis_index(("dp", "fsdp")) * share_rows
    columns = lax.dynamic_slice_in_dim(
        lax.all_gather(d_modul, ("dp", "fsdp"), axis=0, tiled=True), own_start, share_rows, 1
    )
    grad_ada = lax.dot_general(
        columns,
        lax.all_gather(silu_cond, ("dp", "fsdp"), axis=0, tiled=True),
        ROWS_DIMS,
        preferred_element_type=jnp.float32,
    )
    return (
        result,
        grad_tokens,
        grad_condition,
        owned[0],
        summed_bias[0],
        summed_bias[1],
        owned[1],
        summed_bias[2],
        owned[2],
        summed_bias[3],
        owned[3],
        summed_bias[4],
        grad_ada,
        summed_bias[5],
    )


def solution(mesh):
    in_specs = (
        P(("dp", "fsdp"), None, None),
        P(("dp", "fsdp"), None),
        P(("dp", "fsdp"), None, None),
        P(("dp", "fsdp"), None),
        P(("dp", "fsdp")),
        P(),
        P("dp", "fsdp"),
        P(),
        P(),
        P("dp", "fsdp"),
        P(),
        P("dp", "fsdp"),
        P(),
        P("dp", "fsdp"),
        P(),
        P(),
        P(),
    )
    out_specs = (
        P(("dp", "fsdp"), None, None),
        P(("dp", "fsdp"), None, None),
        P(("dp", "fsdp"), None),
        P("dp", "fsdp"),
        P(),
        P(),
        P("dp", "fsdp"),
        P(),
        P("dp", "fsdp"),
        P(),
        P("dp", "fsdp"),
        P(),
        P(("dp", "fsdp"), None),
        P(),
    )
    return jax.shard_map(shards, mesh=mesh, in_specs=in_specs, out_specs=out_specs, check_vma=False)
```

profile of v0, /device:TPU:16, one launch (start us, length us, event | category | flops | bytes accessed | tf_op | source)
XLA Modules:
  0.0 1596.9 jit_solution(9398244737780951491)
XLA Ops:
  23.8 42.0 %psum.49 = f32[16]{0:T(128)S(1)} all-reduce(f32[16]{0:T(128)S(1)} %compare_select_fusion.1), channel_id=1, replica_groups=mesh['dp'=16,'fsdp'=2] {'dp','fsdp'}, use_global_device_ids=true, to_apply=%region_6.7 | all-reduce | flops 16 | bytes 128 | tf_op jit(solution)/shard_map/psum | solution.py:91
  66.5 9.8 convolution_reduce_fusion
  80.7 39.7 %all-gather.10.cloned.1.call-done = bf16[1152,3456]{1,0:T(8,128)(2,1)} async-done(((bf16[72,3456]{1,0:T(8,128)(2,1)}), bf16[1152,3456]{1,0:T(8,128)(2,1)}) %all-gather.10.cloned.1.call-update) | async-done | bytes 7962640 | tf_op jit(solution)/shard_map/all_gather | solution.py:50
  120.4 7.2 fusion.1
  135.1 51.4 %all-gather.12.cloned.1.call-done = bf16[1152,1152]{1,0:T(8,128)(2,1)} async-done(((bf16[72,1152]{1,0:T(8,128)(2,1)}), bf16[1152,1152]{1,0:T(8,128)(2,1)}) %all-gather.12.cloned.1.call-update) | async-done | bytes 2654224 | tf_op jit(solution)/shard_map/all_gather | solution.py:51
  192.0 128.3 %all-gather.14.cloned.1.call-done = bf16[1152,4608]{1,0:T(8,128)(2,1)} async-done(((bf16[72,4608]{1,0:T(8,128)(2,1)}), bf16[1152,4608]{1,0:T(8,128)(2,1)}) %all-gather.14.cloned.1.call-update) | async-done | bytes 10616848 | tf_op jit(solution)/shard_map/all_gather | solution.py:52
  320.2 9.0 convolution_add_fusion
  329.3 125.2 %all-gather.16.cloned.1.call-done = bf16[4608,1152]{1,0:T(8,128)(2,1)} async-done(((bf16[288,1152]{1,0:T(8,128)(2,1)}), bf16[4608,1152]{1,0:T(8,128)(2,1)}) %all-gather.16.cloned.1.call-update) | async-done | bytes 10616848 | tf_op jit(solution)/shard_map/all_gather | solution.py:53
  454.4 10.6 convert_reduce_fusion
  465.0 8.8 fusion.98
  473.9 9.3 fusion.62
  500.9 8.6 fusion.43
  509.5 8.6 fusion.49
  522.1 8.1 fusion.86
  530.5 14.1 fusion.89
  544.7 12.1 fusion.95
  557.5 33.8 %all-gather.4 = bf16[32,1,1152]{2,1,0:T(2,128)(2,1)} all-gather(bf16[1,1,1152]{2,1,0:T(2,128)(2,1)S(1)} %copy-done.41), channel_id=1, replica_groups=mesh['dp'=16,'fsdp'=2] {'dp','fsdp'}, dimensions={0}, use_global_device_ids=true | all-gather | bytes 76032 | tf_op jit(solution)/shard_map/all_gather | solution.py:230
  591.2 39.3 %reduce-scatter.33.cloned.1.call-done = f32[72,1152]{1,0:T(8,128)} async-done(((f32[1152,1152]{1,0:T(8,128)}), f32[72,1152]{1,0:T(8,128)}) %reduce-scatter.33.cloned.1.call-update) | async-done | bytes 331792
  641.1 246.9 %reduce-scatter.31.cloned.1.call-done = f32[72,3456]{1,0:T(8,128)} async-done(((f32[1152,3456]{1,0:T(8,128)}), f32[72,3456]{1,0:T(8,128)}) %reduce-scatter.31.cloned.1.call-update) | async-done | bytes 995344
  898.2 307.3 %reduce-scatter.23.cloned.1.call-done = f32[288,1152]{1,0:T(8,128)} async-done(((f32[4608,1152]{1,0:T(8,128)}), f32[288,1152]{1,0:T(8,128)}) %reduce-scatter.23.cloned.1.call-update) | async-done | bytes 1327120 | tf_op jit(solution)/shard_map/reduce_scatter | solution.py:204
  1208.4 43.5 %all-gather.3 = bf16[32,1,6912]{2,1,0:T(2,128)(2,1)S(1)} all-gather(bf16[1,1,6912]{2,1,0:T(2,128)(2,1)S(1)} %bitcast.186), channel_id=1, replica_groups=mesh['dp'=16,'fsdp'=2] {'dp','fsdp'}, dimensions={0}, use_global_device_ids=true | all-gather | bytes 456192 | tf_op jit(solution)/shard_map/all_gather | solution.py:226
  1251.9 275.2 %reduce-scatter.19.cloned.1.call-done = f32[72,4608]{1,0:T(8,128)} async-done(((f32[1152,4608]{1,0:T(8,128)}), f32[72,4608]{1,0:T(8,128)}) %reduce-scatter.19.cloned.1.call-update) | async-done | bytes 1327120 | tf_op jit(solution)/shard_map/reduce_scatter | solution.py:203
  1531.4 41.0 %all-reduce.2 = (f32[1152]{0:T(1024)}, f32[1152]{0:T(1024)}, f32[1152]{0:T(1024)}, f32[4608]{0:T(1024)}, f32[1152]{0:T(1024)}, /*index=5*/f32[6912]{0:T(1024)}) all-reduce(f32[1152]{0:T(1024)S(1)} %get-tuple-element.19, f32[1152]{0:T(1024)S(1)} %get-tuple-element.18, ...), channel_id=1, replica_groups=mesh['dp'=16,'fsdp'=2] {'dp','fsdp'}, use_global_device_ids=true, to_apply=%region_23.24 | all-reduce | flops 16128 | bytes 115200 | tf_op jit(solution)/shard_map/psum | solution.py:220
  1573.7 8.3 fusion.78
  (213 shorter events, 91.2 us)
Async XLA Ops:
  7.2 113.2 %all-gather.10.cloned.1.call-start = ((), (), s32[]{:S(2)}) async-start(), calls=%async_computation.8 | async-start | bytes 8460288 | tf_op jit(solution)/shard_map/all_gather | solution.py:50
  11.4 175.1 %all-gather.12.cloned.1.call-start = ((), (), s32[]{:S(2)}) async-start(), calls=%async_computation.9 | async-start | bytes 2820096 | tf_op jit(solution)/shard_map/all_gather | solution.py:51
  14.4 305.9 %all-gather.14.cloned.1.call-start = ((), (), s32[]{:S(2)}) async-start(), calls=%async_computation.10 | async-start | bytes 11280384 | tf_op jit(solution)/shard_map/all_gather | solution.py:52
  16.9 437.6 %all-gather.16.cloned.1.call-start = ((), (), s32[]{:S(2)}) async-start(), calls=%async_computation.11 | async-start | bytes 11280384 | tf_op jit(solution)/shard_map/all_gather | solution.py:53
  21.2 609.3 %reduce-scatter.33.cloned.1.call-start = ((), (), s32[]{:S(2)}) async-start(), calls=%async_computation.19 | async-start | bytes 5640192
  489.6 398.4 %reduce-scatter.31.cloned.1.call-start = ((), (), s32[]{:S(2)}) async-start(), calls=%async_computation.18 | async-start | bytes 16920576
  530.2 675.3 %reduce-scatter.23.cloned.1.call-start = ((), (), s32[]{:S(2)}) async-start(), calls=%async_computation.14 | async-start | bytes 22560768 | tf_op jit(solution)/shard_map/reduce_scatter | solution.py:204
  544.6 982.5 %reduce-scatter.19.cloned.1.call-start = ((), (), s32[]{:S(2)}) async-start(), calls=%async_computation.12 | async-start | bytes 22560768 | tf_op jit(solution)/shard_map/reduce_scatter | solution.py:203
  556.8 1025.2 %reduce-scatter.27.cloned.1.call-start = ((), (), s32[]{:S(2)}) async-start(), calls=%async_computation.16 | async-start | bytes 442368
  632.4 951.3 %reduce-scatter.25.cloned.1.call-start = ((), (), s32[]{:S(2)}) async-start(), calls=%async_computation.15 | async-start | bytes 1327104
  641.1 253.5 %copy-start.3 = (f32[256,1152]{1,0:T(8,128)S(1)}, f32[256,1152]{1,0:T(8,128)}, u32[]{:S(2)}) copy-start(f32[256,1152]{1,0:T(8,128)} %get-tuple-element.54) | copy-start | bytes 3538948
  892.3 693.5 %reduce-scatter.29.cloned.1.call-start = ((), (), s32[]{:S(2)}) async-start(), calls=%async_computation.17 | async-start | bytes 1327104
  898.2 310.1 %copy-start.26 = (bf16[1,6912]{1,0:T(2,128)(2,1)S(1)}, bf16[1,6912]{1,0:T(2,128)(2,1)}, u32[]{:S(2)}) copy-start(bf16[1,6912]{1,0:T(2,128)(2,1)} %constant_dynamic-update-slice_fusion.5) | copy-start | bytes 41476
  898.2 310.1 %copy-start.45 = (bf16[1152]{0:T(1024)(128)(2,1)S(1)}, bf16[1152]{0:T(1024)(128)(2,1)}, u32[]{:S(2)}) copy-start(bf16[1152]{0:T(1024)(128)(2,1)} %get-tuple-element.16) | copy-start | bytes 6916
  898.2 310.1 %copy-start.32 = (bf16[1152]{0:T(1024)(128)(2,1)S(1)}, bf16[1152]{0:T(1024)(128)(2,1)}, u32[]{:S(2)}) copy-start(bf16[1152]{0:T(1024)(128)(2,1)} %get-tuple-element.47) | copy-start | bytes 6916
  898.2 310.2 %copy-start.44 = (bf16[1152]{0:T(1024)(128)(2,1)S(1)}, bf16[1152]{0:T(1024)(128)(2,1)}, u32[]{:S(2)}) copy-start(bf16[1152]{0:T(1024)(128)(2,1)} %get-tuple-element.20) | copy-start | bytes 6916
  898.2 310.2 %copy-start.43 = (bf16[1152]{0:T(1024)(128)(2,1)S(1)}, bf16[1152]{0:T(1024)(128)(2,1)}, u32[]{:S(2)}) copy-start(bf16[1152]{0:T(1024)(128)(2,1)} %get-tuple-element.46) | copy-start | bytes 6916
  898.2 310.2 %copy-start.42 = (bf16[1152]{0:T(1024)(128)(2,1)S(1)}, bf16[1152]{0:T(1024)(128)(2,1)}, u32[]{:S(2)}) copy-start(bf16[1152]{0:T(1024)(128)(2,1)} %get-tuple-element.43) | copy-start | bytes 6916
  1208.2 379.7 %reduce-scatter.21.cloned.1.call-start = ((), (), s32[]{:S(2)}) async-start(), calls=%async_computation.13 | async-start | bytes 995328 | tf_op jit(solution)/shard_map/reduce_scatter | solution.py:213
  1251.9 277.8 %copy-start.21 = (bf16[6912]{0:T(1024)(128)(2,1)S(1)}, bf16[6912]{0:T(1024)(128)(2,1)}, u32[]{:S(2)}) copy-start(bf16[6912]{0:T(1024)(128)(2,1)} %custom-call.1) | copy-start | bytes 41476
  1251.9 279.5 %copy-start.33 = (f32[1152]{0:T(1024)S(1)}, f32[1152]{0:T(1024)}, u32[]{:S(2)}) copy-start(f32[1152]{0:T(1024)} %get-tuple-element.38) | copy-start | bytes 13828
  1251.9 279.5 %copy-start.34 = (f32[1152]{0:T(1024)S(1)}, f32[1152]{0:T(1024)}, u32[]{:S(2)}) copy-start(f32[1152]{0:T(1024)} %get-tuple-element.49) | copy-start | bytes 13828
  1251.9 279.5 %copy-start.40 = (f32[4608]{0:T(1024)S(1)}, f32[4608]{0:T(1024)}, u32[]{:S(2)}) copy-start(f32[4608]{0:T(1024)} %get-tuple-element.57) | copy-start | bytes 55300
  1251.9 320.6 %copy-start.12 = (bf16[32,1,1152]{2,1,0:T(2,128)(2,1)S(1)}, bf16[32,1,1152]{2,1,0:T(2,128)(2,1)}, u32[]{:S(2)}) copy-start(bf16[32,1,1152]{2,1,0:T(2,128)(2,1)} %all-gather.4) | copy-start | bytes 221188
  (41 other events, 655.9 us)
Sparse Core Ops, SparseCore 0:
  11.5 108.8 all-gather.9
  123.7 62.7 all-gather.11
  189.3 130.9 all-gather.13
  323.5 130.9 all-gather.15
  489.7 140.7 reduce-scatter.32
  636.2 251.7 reduce-scatter.30
  894.0 311.4 reduce-scatter.22
  1211.5 315.5 reduce-scatter.18
  1529.9 7.9 reduce-scatter.26
  1540.0 9.3 reduce-scatter.24
  1551.7 9.3 reduce-scatter.28
  1563.8 9.1 reduce-scatter.20
where the time goes:
time: 1600 us
  waiting for transfers between devices  1210 us (76%)
  blocking collectives  169 us (11%)
  matrix products  143 us (9%)
  other arithmetic  26.5 us (2%)
  local copies, waits for them, and re-layouts  25.2 us (2%)
  between operations  17.7 us (1%)
    reduce_scatter x1, waiting for transfers between devices, shards(): lax.psum_scatter(grad_fc2, 'dp', scatter_dimension=0, tiled=True)  307 us
    unnamed x17, waiting for transfers between devices  286 us
    reduce_scatter x1, waiting for transfers between devices, shards(): lax.psum_scatter(grad_fc1, 'dp', scatter_dimension=0, tiled=True)  275 us
    all_gather x1, waiting for transfers between devices, collect_trunk(): lax.all_gather(paired[2], 'dp', axis=0, tiled=True)  128 us
    all_gather x1, waiting for transfers between devices, collect_trunk(): lax.all_gather(paired[3], 'dp', axis=0, tiled=True)  125 us
    all_gather x1, waiting for transfers between devices, collect_trunk(): lax.all_gather(paired[1], 'dp', axis=0, tiled=True)  51.4 us
    all_gather x1, blocking collectives, shards(): lax.all_gather(d_modul, ('dp', 'fsdp'), axis=0, tiled=True)  43.5 us
    psum x1, blocking collectives, shards(): counts = lax.psum(local_counts, ('dp', 'fsdp'))  42 us
  transfers between devices with their start and end apart: 12, of which 8 were waited for; matrix products, arithmetic and copies ran while one was open for 10% of the time, Pallas kernels for 0%

commit v1 on v0

v1 whole, which is shorter than its diff:
```python
import functools

import jax
import jax.numpy as jnp
from jax import lax
from jax.experimental import pallas as pl
from jax.experimental.pallas import tpu as pltpu
from jax.sharding import PartitionSpec as P

D = 1152
H = 16
HD = 72
BINS = 16
SEQ = 256


NEG_FILL = -1e30
NORM_EPS = 1e-06
GELU_COEF = 0.7978845608028654
CUBIC_COEF = 0.044715
ROWS_DIMS = (((0,), (0,)), ((), ()))
LAST_DIMS = (((1,), (1,)), ((), ()))


def gelu_tanh(values_in):
    return (
        0.5
        * values_in
        * (1.0 + jnp.tanh(GELU_COEF * (values_in + CUBIC_COEF * values_in * values_in * values_in)))
    )


def norm_rows(inputs):
    centered = inputs - jnp.mean(inputs, axis=-1, keepdims=True)
    inverse = lax.rsqrt(jnp.mean(centered * centered, axis=-1, keepdims=True) + NORM_EPS)
    return (centered * inverse, inverse)


def norm_back(grad_normed, normed, inverse):
    centered_grad = grad_normed - jnp.mean(grad_normed, axis=-1, keepdims=True)
    return inverse * (
        centered_grad - normed * jnp.mean(grad_normed * normed, axis=-1, keepdims=True)
    )


VMEM_LIMIT = 66_000_000
ANY = pl.BlockSpec(memory_space=pl.ANY)
VMEM = pl.BlockSpec(memory_space=pltpu.VMEM)
ZS = 4
OFFSETS = (0, -1, 1, -2, 2, -3, 3)


class Place:
    def __init__(self):
        self.i = lax.axis_index("dp")
        self.c = lax.axis_index("fsdp")
        self.z = self.i // 4
        self.q = self.i % 4
        self.y = self.q // 2
        self.x = self.q % 2
        self.to_y = 2 * (1 - 2 * self.y)
        self.to_x = 1 - 2 * self.x

    def partners(self, level):
        odd = level % 2
        first = odd * self.to_x + (1 - odd) * self.to_y
        return first, self.to_x + self.to_y - first

    def greet(self):
        barrier = pltpu.get_barrier_semaphore()

        def signal(i, c):
            pl.semaphore_signal(
                barrier,
                inc=1,
                device_id={"dp": i, "fsdp": c},
                device_id_type=pl.DeviceIdType.MESH,
            )

        signal(self.i, 1 - self.c)
        signal(self.i + self.to_y, self.c)
        signal(self.i + self.to_x, self.c)
        up, down = self.z < ZS - 1, self.z > 0
        pl.when(up)(lambda: signal(self.i + 4, self.c))
        pl.when(down)(lambda: signal(self.i - 4, self.c))
        pl.semaphore_wait(barrier, 3 + up.astype(jnp.int32) + down.astype(jnp.int32))


def remote(src, dst, send, recv, i, c):
    return pltpu.make_async_remote_copy(
        src_ref=src,
        dst_ref=dst,
        send_sem=send,
        recv_sem=recv,
        device_id={"dp": i, "fsdp": c},
        device_id_type=pl.DeviceIdType.MESH,
    )


def gather_sems(count):
    dma = pltpu.SemaphoreType.DMA
    return [
        dma((count, 16)),
        dma((count, 16)),
        dma((count, 2, ZS)),
        dma((count, ZS, 3)),
        dma((count, 16)),
        dma((count,)),
    ]


class Gather:
    def __init__(self, at, k, shard, own, sib, sems):
        self.at, self.k, self.shard, self.own, self.sib = at, k, shard, own, sib
        self.recv, self.core, self.line, self.pair, self.over, self.local = sems

    def send(self, src, j, sem, i):
        return remote(src, self.own.at[j], sem, self.recv.at[self.k, j], i, self.at.c)

    def across(self, src, j):
        at, k = self.at, self.k
        return remote(
            src, self.sib.at[j], self.over.at[k, j], self.core.at[k, j], at.i, 1 - at.c
        )

    def arrived(self, j):
        at = self.at
        remote(
            self.own.at[j],
            self.own.at[j],
            self.over.at[self.k, j],
            self.recv.at[self.k, j],
            at.i,
            1 - at.c,
        ).wait_recv()

    def pieces(self, level):
        first, second = self.at.partners(level)
        column = level * 4 + self.at.q
        return first, second, column

    def guard(self, off, run):
        level = self.at.z + off
        if off == 0:
            run(level)
        else:
            pl.when((level >= 0) & (level < ZS))(lambda: run(level))

    def column_copies(self, off, level):
        at, k = self.at, self.k
        first, second, j = self.pieces(level)
        src = self.shard if off == 0 else self.own.at[j]
        always = [
            self.send(src, j, self.pair.at[k, level, 0], at.i + first),
            self.send(src, j, self.pair.at[k, level, 1], at.i + second),
            self.across(src, j),
        ]
        up = self.send(src, j, self.line.at[k, 0, level], at.i + 4) if off <= 0 else None
        down = self.send(src, j, self.line.at[k, 1, level], at.i - 4) if off >= 0 else None
        return always, up, down

    def column(self, off):
        def run(level):
            if off:
                self.arrived(level * 4 + self.at.q)
            always, up, down = self.column_copies(off, level)
            if up is not None:
                pl.when(self.at.z < ZS - 1)(up.start)
            if down is not None:
                pl.when(self.at.z > 0)(down.start)
            for copy in always:
                copy.start()
            if off == 0:
                self.keep().start()

        self.guard(off, run)

    def keep(self):
        return pltpu.make_async_copy(
            self.shard, self.own.at[self.at.i], self.local.at[self.k]
        )

    def relay_copies(self, level):
        first, second, column = self.pieces(level)
        j = column + first
        return (
            self.send(self.own.at[j], j, self.pair.at[self.k, level, 2], self.at.i + second),
            self.across(self.own.at[j], j),
        )

    def relay(self, off):
        def run(level):
            first, _, column = self.pieces(level)
            self.arrived(column + first)
            for copy in self.relay_copies(level):
                copy.start()

        self.guard(off, run)

    def last_copies(self, level):
        first, second, column = self.pieces(level)
        return [(j, self.across(self.own.at[j], j)) for j in (column + second, column + first + second)]

    def last(self, off):
        def run(level):
            for j, copy in self.last_copies(level):
                self.arrived(j)
                copy.start()

        self.guard(off, run)

    def finish(self):
        at = self.at
        self.keep().wait()
        for off in OFFSETS:

            def run(level, off=off):
                always, up, down = self.column_copies(off, level)
                if up is not None:
                    pl.when(at.z < ZS - 1)(up.wait_send)
                if down is not None:
                    pl.when(at.z > 0)(down.wait_send)
                for copy in always:
                    copy.wait_send()
                for copy in self.relay_copies(level):
                    copy.wait_send()
                for _, copy in self.last_copies(level):
                    copy.wait_send()

            self.guard(off, run)

        @pl.loop(0, 16)
        def _(j):
            self.across(self.sib.at[j], j).wait_recv()

    def events(self, start, span):
        out = []
        for off in OFFSETS:
            far = abs(off)
            out.append((start + span * 0.15 * far, functools.partial(self.column, off)))
            out.append((start + span * (0.3 + 0.2 * far), functools.partial(self.relay, off)))
            out.append((start + span * (0.6 + 0.2 * far), functools.partial(self.last, off)))
        return out


def gather_kernel(count, *refs):
    shards, own, sib = refs[:count], refs[count : 2 * count], refs[2 * count : 3 * count]
    sems = refs[3 * count :]
    at = Place()
    at.greet()
    steps, start = [], 0.0
    jobs = []
    for k in range(count):
        job = Gather(at, k, shards[k], own[k], sib[k], sems)
        jobs.append(job)
        span = float(shards[k].shape[0] * shards[k].shape[1])
        steps += job.events(start, span)
        start += span
    for _, action in sorted(steps, key=lambda item: item[0]):
        action()
    for job in jobs:
        job.finish()


def gather_all(shards):
    count = len(shards)
    spread = [jax.ShapeDtypeStruct((16,) + s.shape, s.dtype) for s in shards]
    outs = pl.pallas_call(
        functools.partial(gather_kernel, count),
        out_shape=spread + spread,
        in_specs=[VMEM] * count,
        out_specs=[ANY] * (2 * count),
        scratch_shapes=gather_sems(count),
        compiler_params=pltpu.CompilerParams(
            collective_id=0, has_side_effects=True, vmem_limit_bytes=16_000_000
        ),
        name="gather_all",
    )(*shards)
    return outs[:count], outs[count:]


def total(*values):
    out = values[0].astype(jnp.float32)
    for value in values[1:]:
        out = out + value.astype(jnp.float32)
    return out


class Scatter:
    def __init__(self, at, k, mine, other, result, bufs, sems):
        self.at, self.k = at, k
        self.mine, self.other, self.result = mine, other, result
        self.held, self.cross, self.near, self.far, self.line = bufs
        (
            self.load_sem,
            self.cross_send,
            self.cross_recv,
            self.near_send,
            self.near_recv,
            self.far_send,
            self.far_recv,
            self.line_send,
            self.line_recv,
        ) = sems

    def load(self):
        return pltpu.make_async_copy(self.mine, self.held, self.load_sem.at[self.k])

    def cross_copy(self, level):
        at, k = self.at, self.k
        rows = pl.ds(level * 4, 4)
        return remote(
            self.other.at[rows],
            self.cross.at[rows],
            self.cross_send.at[k, level],
            self.cross_recv.at[k, level],
            at.i,
            1 - at.c,
        )

    def near_copies(self, level):
        at, k = self.at, self.k
        first, second = at.partners(level)
        column = level * 4 + at.q
        return [
            remote(
                self.held.at[j],
                self.near.at[level, slot],
                self.near_send.at[k, level, slot],
                self.near_recv.at[k, level, slot],
                at.i + second,
                at.c,
            )
            for slot, j in enumerate((column + second, column + first + second))
        ]

    def far_copy(self, level):
        at, k = self.at, self.k
        first, _ = at.partners(level)
        j = level * 4 + at.q + first
        return remote(
            self.held.at[j],
            self.far.at[level],
            self.far_send.at[k, level],
            self.far_recv.at[k, level],
            at.i + first,
            at.c,
        )

    def line_copy(self, way, level):
        at, k = self.at, self.k
        j = level * 4 + at.q
        return remote(
            self.held.at[j],
            self.line.at[way, level],
            self.line_send.at[k, way, level],
            self.line_recv.at[k, way, level],
            at.i + (4 if way == 0 else -4),
            at.c,
        )

    def begin(self):
        self.load().start()

        @pl.loop(0, ZS)
        def _(level):
            self.cross_copy(level).start()

        zeros = jnp.zeros(self.line.shape[2:], self.line.dtype)

        @pl.when(self.at.z == 0)
        def _():
            @pl.loop(0, ZS)
            def _(level):
                self.line[0, level] = zeros

        @pl.when(self.at.z == ZS - 1)
        def _():
            @pl.loop(0, ZS)
            def _(level):
                self.line[1, level] = zeros

    def stage_near(self):
        self.load().wait()

        @pl.loop(0, ZS)
        def _(level):
            first, second = self.at.partners(level)
            column = level * 4 + self.at.q
            self.cross_copy(level).wait_recv()
            copies = self.near_copies(level)
            for copy, j in zip(copies, (column + second, column + first + second)):
                self.held[j] = total(self.held[j], self.cross[j]).astype(jnp.bfloat16)
                copy.start()

    def stage_far(self):
        @pl.loop(0, ZS)
        def _(level):
            first, _ = self.at.partners(level)
            j = level * 4 + self.at.q + first
            for copy in self.near_copies(level):
                copy.wait_recv()
            self.held[j] = total(self.held[j], self.cross[j], self.near[level, 1]).astype(
                jnp.bfloat16
            )
            self.far_copy(level).start()

    def stage_line(self):
        z = self.at.z

        def pass_on(way, level):
            j = level * 4 + self.at.q
            self.far_copy(level).wait_recv()
            if way == 0:
                pl.when(z > 0)(self.line_copy(0, level).wait_recv)
            else:
                pl.when(z < ZS - 1)(self.line_copy(1, level).wait_recv)
            self.held[j] = total(
                self.held[j],
                self.cross[j],
                self.near[level, 0],
                self.far[level],
                self.line[way, level],
            ).astype(jnp.bfloat16)
            self.line_copy(way, level).start()

        @pl.loop(0, ZS - 1)
        def _(back):
            level = ZS - 1 - back
            pl.when(level > z)(lambda: pass_on(0, level))
            low = back
            pl.when(low < z)(lambda: pass_on(1, low))

    def stage_own(self):
        z = self.at.z
        j = self.at.i
        self.far_copy(z).wait_recv()
        pl.when(z > 0)(self.line_copy(0, z).wait_recv)
        pl.when(z < ZS - 1)(self.line_copy(1, z).wait_recv)
        self.result[...] = total(
            self.held[j],
            self.cross[j],
            self.near[z, 0],
            self.far[z],
            self.line[0, z],
            self.line[1, z],
        )

    def finish(self):
        z = self.at.z

        @pl.loop(0, ZS)
        def _(level):
            self.cross_copy(level).wait_send()
            for copy in self.near_copies(level):
                copy.wait_send()
            self.far_copy(level).wait_send()
            pl.when(level > z)(self.line_copy(0, level).wait_send)
            pl.when(level < z)(self.line_copy(1, level).wait_send)


def scatter_kernel(count, *refs):
    refs = list(refs)

    def take(n):
        out = refs[:n]
        del refs[:n]
        return out

    mine, other, note = take(count), take(count), take(1)[0]
    results = take(count)
    note_own, note_sib = take(2)
    bufs = [take(5) for _ in range(count)]
    sems, note_sems = take(9), take(6)
    at = Place()
    at.greet()
    jobs = [
        Scatter(at, k, mine[k], other[k], results[k], bufs[k], sems) for k in range(count)
    ]
    word = Gather(at, 0, note, note_own, note_sib, note_sems)
    whisper = [action for _, action in sorted(word.events(0.0, 1.0), key=lambda item: item[0])]
    for job in jobs:
        job.begin()

    def speak(n):
        for action in whisper[:n]:
            action()
        del whisper[:n]

    speak(1)
    jobs[0].stage_near()
    speak(5)
    for k in range(count):
        if k + 1 < count:
            jobs[k + 1].stage_near()
        jobs[k].stage_far()
        speak(5)
        if k:
            jobs[k - 1].stage_own()
        jobs[k].stage_line()
    speak(len(whisper))
    jobs[-1].stage_own()
    for job in jobs:
        job.finish()
    word.finish()


def scatter_all(mine, other, note):
    count = len(mine)
    shapes = [g.shape[1:] for g in mine]
    spread = jax.ShapeDtypeStruct((16,) + note.shape, note.dtype)
    scratch = []
    for shape in shapes:
        for lead in ((16,), (16,), (ZS, 2), (ZS,), (2, ZS)):
            scratch.append(pltpu.VMEM(lead + shape, jnp.bfloat16))
    dma = pltpu.SemaphoreType.DMA
    scratch += [
        dma((count,)),
        dma((count, ZS)),
        dma((count, ZS)),
        dma((count, ZS, 2)),
        dma((count, ZS, 2)),
        dma((count, ZS)),
        dma((count, ZS)),
        dma((count, 2, ZS)),
        dma((count, 2, ZS)),
    ]
    outs = pl.pallas_call(
        functools.partial(scatter_kernel, count),
        out_shape=[jax.ShapeDtypeStruct(s, jnp.float32) for s in shapes] + [spread, spread],
        in_specs=[ANY] * (2 * count) + [VMEM],
        out_specs=[VMEM] * count + [ANY, ANY],
        scratch_shapes=scratch + gather_sems(1),
        compiler_params=pltpu.CompilerParams(
            collective_id=1, has_side_effects=True, vmem_limit_bytes=VMEM_LIMIT
        ),
        name="scatter_all",
    )(*mine, *other, note)
    return outs[:count], outs[count], outs[count + 1]


def gather_plain(shards):
    own = [lax.all_gather(s, "dp", axis=0) for s in shards]
    pair = [lax.all_gather(g, "fsdp", axis=0) for g in own]
    other = 1 - lax.axis_index("fsdp")
    return own, [lax.dynamic_index_in_dim(p, other, 0, keepdims=False) for p in pair]


def scatter_plain(mine, other, note):
    c = lax.axis_index("fsdp")
    results = []
    for own, sib in zip(mine, other):
        pair = jnp.where(c == 0, jnp.stack([own, sib]), jnp.stack([sib, own]))
        half = lax.psum_scatter(pair, "fsdp", scatter_dimension=0, tiled=False)
        results.append(
            lax.psum_scatter(
                half.astype(jnp.float32), "dp", scatter_dimension=0, tiled=False
            )
        )
    own, sib = gather_plain([note])
    return results, own[0], sib[0]


def masked_scores(query, keys, valid_keys):
    scaled = jnp.einsum(
        "blhc,bmhc->bhlm", query, keys, preferred_element_type=jnp.float32
    ) * HD ** (-0.5)
    return jnp.where(valid_keys[:, None, None, :], scaled, NEG_FILL)


def shards(
    fast,
    tokens,
    condition,
    cotangent,
    image_grids,
    noise_bins,
    bin_weights,
    w_qkv,
    b_query,
    b_value,
    w_proj,
    b_proj,
    w_fc1,
    b_fc1,
    w_fc2,
    b_fc2,
    w_ada,
    b_ada,
):
    images = tokens.shape[0]
    row_count = images * SEQ
    core = lax.axis_index("fsdp")

    def join(own, sib):
        return jnp.where(
            core == 0,
            jnp.concatenate([own, sib], axis=-1),
            jnp.concatenate([sib, own], axis=-1),
        )

    def split(full):
        half = full.shape[-1] // 2
        low, high = full[..., :half], full[..., half:]
        return jnp.where(core == 0, low, high), jnp.where(core == 0, high, low)

    token_count = image_grids[:, 0] * image_grids[:, 1]
    valid_keys = lax.broadcasted_iota(jnp.int32, (images, SEQ), 1) < token_count[:, None]
    bin_table = (noise_bins[:, None] == lax.broadcasted_iota(jnp.int32, (images, BINS), 1)).astype(
        jnp.float32
    )
    local_counts = jnp.sum(bin_table * token_count[:, None].astype(jnp.float32), axis=0)
    cond_float = condition.astype(jnp.float32)
    silu_cond = jax.nn.silu(cond_float).astype(jnp.bfloat16)
    lanes = 128
    head = jnp.concatenate([local_counts, jnp.zeros((lanes - BINS,), jnp.float32)])[None]
    facts = jnp.concatenate(
        [
            head,
            silu_cond.astype(jnp.float32).reshape(-1, lanes),
            jnp.zeros((6, lanes), jnp.float32),
        ]
    )
    gather = gather_all if fast else gather_plain
    scatter = scatter_all if fast else scatter_plain
    own, sib = gather([facts, w_qkv, w_proj, w_fc1, w_fc2])
    flat = lambda w: w.reshape(-1, w.shape[-1])
    qkv_own, proj_own, fc1_own, fc2_own = [flat(w) for w in own[1:]]
    qkv_sib, proj_sib, fc1_sib, fc2_sib = [flat(w) for w in sib[1:]]
    counts = (jnp.sum(own[0], axis=0) + jnp.sum(sib[0], axis=0))[0, :BINS]
    bin_scale = bin_weights.astype(jnp.float32) * (jnp.sum(counts) / BINS) / counts
    image_scale = jnp.sum(bin_table * bin_scale[None, :], axis=1)

    def times(left, right):
        return jnp.dot(left, right, preferred_element_type=jnp.float32)

    def times_t(left, right):
        return lax.dot_general(left, right, LAST_DIMS, preferred_element_type=jnp.float32)

    def outer(left, right):
        return lax.dot_general(left, right, ROWS_DIMS, preferred_element_type=jnp.float32)

    modul = lax.dot_general(silu_cond, w_ada, LAST_DIMS, preferred_element_type=jnp.float32) + b_ada
    pieces = [modul[:, None, part_index * D : (part_index + 1) * D] for part_index in range(6)]
    shift_one, scale_one, gate_one, shift_two, scale_two, gate_two = pieces
    token_float = tokens.astype(jnp.float32)
    normed_one, inverse_one = norm_rows(token_float)
    attn_in = (
        (normed_one * (1.0 + scale_one) + shift_one).astype(jnp.bfloat16).reshape(row_count, D)
    )
    bias_qkv = jnp.concatenate([b_query, jnp.zeros_like(b_query), b_value])
    qkv_all = (join(times(attn_in, qkv_own), times(attn_in, qkv_sib)) + bias_qkv).astype(
        jnp.bfloat16
    )
    qkv_heads = qkv_all.reshape(images, SEQ, 3, H, HD)
    query, keys, values = (qkv_heads[:, :, 0], qkv_heads[:, :, 1], qkv_heads[:, :, 2])
    scores = masked_scores(query, keys, valid_keys)
    row_max = jnp.max(scores, axis=-1, keepdims=True)
    exponent = jnp.exp(scores - row_max)
    row_total = jnp.sum(exponent, axis=-1, keepdims=True)
    soft_probs = exponent / row_total
    log_total = row_max + jnp.log(row_total)
    attended = jnp.einsum(
        "bhlm,bmhc->blhc",
        soft_probs.astype(jnp.bfloat16),
        values,
        preferred_element_type=jnp.float32,
    )
    attended = attended.astype(jnp.bfloat16).reshape(row_count, D)
    attn_out = (join(times(attended, proj_own), times(attended, proj_sib)) + b_proj).reshape(
        images, SEQ, D
    )
    middle = token_float + gate_one * attn_out
    normed_two, inverse_two = norm_rows(middle)
    mlp_in = (normed_two * (1.0 + scale_two) + shift_two).astype(jnp.bfloat16).reshape(row_count, D)
    bias_own, bias_sib = split(b_fc1)
    hidden_own = times(mlp_in, fc1_own) + bias_own
    hidden_sib = times(mlp_in, fc1_sib) + bias_sib
    active = join(
        gelu_tanh(hidden_own).astype(jnp.bfloat16), gelu_tanh(hidden_sib).astype(jnp.bfloat16)
    )
    branch = (join(times(active, fc2_own), times(active, fc2_sib)) + b_fc2).reshape(
        images, SEQ, D
    )
    result = (middle + gate_two * branch).astype(jnp.bfloat16)
    grad_out = (
        cotangent.astype(jnp.float32)
        * (valid_keys.astype(jnp.float32) * image_scale[:, None])[:, :, None]
    )
    d_gate_two = jnp.sum(grad_out * branch, axis=1)
    d_branch = (gate_two * grad_out).astype(jnp.bfloat16).reshape(row_count, D)
    d_branch_own, d_branch_sib = split(d_branch)
    fc2_mine, fc2_other = outer(active, d_branch_own), outer(active, d_branch_sib)
    bias_fc2 = jnp.sum(d_branch, axis=0, dtype=jnp.float32)
    d_active = times_t(d_branch_own, fc2_own) + times_t(d_branch_sib, fc2_sib)
    d_active_own, d_active_sib = split(d_active)
    d_hidden_own = jax.vjp(gelu_tanh, hidden_own)[1](d_active_own)[0].astype(jnp.bfloat16)
    d_hidden_sib = jax.vjp(gelu_tanh, hidden_sib)[1](d_active_sib)[0].astype(jnp.bfloat16)
    fc1_mine, fc1_other = outer(mlp_in, d_hidden_own), outer(mlp_in, d_hidden_sib)
    bias_fc1 = join(
        jnp.sum(d_hidden_own, axis=0, dtype=jnp.float32),
        jnp.sum(d_hidden_sib, axis=0, dtype=jnp.float32),
    )
    d_mlp_in = (times_t(d_hidden_own, fc1_own) + times_t(d_hidden_sib, fc1_sib)).reshape(
        images, SEQ, D
    )
    d_shift_two = jnp.sum(d_mlp_in, axis=1)
    d_scale_two = jnp.sum(d_mlp_in * normed_two, axis=1)
    d_middle = grad_out + norm_back(d_mlp_in * (1.0 + scale_two), normed_two, inverse_two)
    d_gate_one = jnp.sum(d_middle * attn_out, axis=1)
    d_attn = (gate_one * d_middle).astype(jnp.bfloat16).reshape(row_count, D)
    d_attn_own, d_attn_sib = split(d_attn)
    proj_mine, proj_other = outer(attended, d_attn_own), outer(attended, d_attn_sib)
    bias_proj = jnp.sum(d_attn, axis=0, dtype=jnp.float32)
    d_attended = times_t(d_attn_own, proj_own) + times_t(d_attn_sib, proj_sib)
    d_attended = d_attended.astype(jnp.bfloat16).reshape(images, SEQ, H, HD)
    soft_again = jnp.exp(masked_scores(query, keys, valid_keys) - log_total)
    grad_values = jnp.einsum(
        "bhlm,blhc->bmhc",
        soft_again.astype(jnp.bfloat16),
        d_attended,
        preferred_element_type=jnp.float32,
    )
    d_probs = jnp.einsum("blhc,bmhc->bhlm", d_attended, values, preferred_element_type=jnp.float32)
    d_scores = soft_again * (d_probs - jnp.sum(soft_again * d_probs, axis=-1, keepdims=True))
    d_scores = jnp.where(valid_keys[:, None, None, :], d_scores, 0.0).astype(jnp.bfloat16)
    grad_query = jnp.einsum(
        "bhlm,bmhc->blhc", d_scores, keys, preferred_element_type=jnp.float32
    ) * HD ** (-0.5)
    grad_keys = jnp.einsum(
        "bhlm,blhc->bmhc", d_scores, query, preferred_element_type=jnp.float32
    ) * HD ** (-0.5)
    d_qkv = (
        jnp.stack([grad_query, grad_keys, grad_values], axis=2)
        .astype(jnp.bfloat16)
        .reshape(row_count, 3 * D)
    )
    d_qkv_own, d_qkv_sib = split(d_qkv)
    qkv_mine, qkv_other = outer(attn_in, d_qkv_own), outer(attn_in, d_qkv_sib)
    bias_query = jnp.sum(d_qkv[:, :D], axis=0, dtype=jnp.float32)
    bias_value = jnp.sum(d_qkv[:, 2 * D :], axis=0, dtype=jnp.float32)
    d_attn_in = (times_t(d_qkv_own, qkv_own) + times_t(d_qkv_sib, qkv_sib)).reshape(
        images, SEQ, D
    )
    d_shift_one = jnp.sum(d_attn_in, axis=1)
    d_scale_one = jnp.sum(d_attn_in * normed_one, axis=1)
    grad_tokens = (
        d_middle + norm_back(d_attn_in * (1.0 + scale_one), normed_one, inverse_one)
    ).astype(jnp.bfloat16)
    d_modul = jnp.concatenate(
        [d_shift_one, d_scale_one, d_gate_one, d_shift_two, d_scale_two, d_gate_two], axis=1
    ).astype(jnp.bfloat16)
    silu_pull = jax.vjp(jax.nn.silu, cond_float)[1]
    grad_condition = silu_pull(jnp.dot(d_modul, w_ada, preferred_element_type=jnp.float32))[0]
    biases = [bias_query, bias_value, bias_proj, bias_fc1, bias_fc2]
    note = jnp.concatenate(
        biases + [d_modul.astype(jnp.float32).reshape(-1), jnp.zeros((2 * lanes,), jnp.float32)]
    ).reshape(-1, lanes)

    def blocks(grad, shard):
        return grad.astype(jnp.bfloat16).reshape((-1,) + shard.shape)

    owners = [w_fc1, w_fc2, w_qkv, w_proj]
    mine = [blocks(g, w) for g, w in zip([fc1_mine, fc2_mine, qkv_mine, proj_mine], owners)]
    other = [blocks(g, w) for g, w in zip([fc1_other, fc2_other, qkv_other, proj_other], owners)]
    (grad_fc1, grad_fc2, grad_qkv, grad_proj), note_own, note_sib = scatter(mine, other, note)
    total_note = (jnp.sum(note_own, axis=0) + jnp.sum(note_sib, axis=0)).reshape(-1)
    summed, start = [], 0
    for vector in biases + [b_ada]:
        summed.append(total_note[start : start + vector.shape[0]])
        start += vector.shape[0]
    first = start - b_ada.shape[0]
    share_rows = 6 * D // lax.axis_size(("dp", "fsdp"))
    own_start = first + lax.axis_index(("dp", "fsdp")) * share_rows
    notes = jnp.concatenate([note_own, note_sib]).reshape(-1, note.size)
    silus = jnp.concatenate([own[0], sib[0]])[:, 1:10].reshape(-1, D)
    columns = lax.dynamic_slice_in_dim(notes, own_start, share_rows, 1)
    grad_ada = lax.dot_general(
        columns.astype(jnp.bfloat16),
        silus.astype(jnp.bfloat16),
        ROWS_DIMS,
        preferred_element_type=jnp.float32,
    )
    return (
        result,
        grad_tokens,
        grad_condition,
        grad_qkv,
        summed[0],
        summed[1],
        grad_proj,
        summed[2],
        grad_fc1,
        summed[3],
        grad_fc2,
        summed[4],
        grad_ada,
        summed[5],
    )


def solution(mesh):
    in_specs = (
        P(("dp", "fsdp"), None, None),
        P(("dp", "fsdp"), None),
        P(("dp", "fsdp"), None, None),
        P(("dp", "fsdp"), None),
        P(("dp", "fsdp")),
        P(),
        P("dp", "fsdp"),
        P(),
        P(),
        P("dp", "fsdp"),
        P(),
        P("dp", "fsdp"),
        P(),
        P("dp", "fsdp"),
        P(),
        P(),
        P(),
    )
    out_specs = (
        P(("dp", "fsdp"), None, None),
        P(("dp", "fsdp"), None, None),
        P(("dp", "fsdp"), None),
        P("dp", "fsdp"),
        P(),
        P(),
        P("dp", "fsdp"),
        P(),
        P("dp", "fsdp"),
        P(),
        P("dp", "fsdp"),
        P(),
        P(("dp", "fsdp"), None),
        P(),
    )
    return jax.shard_map(
        functools.partial(shards, dict(mesh.shape) == {"dp": 16, "fsdp": 2}),
        mesh=mesh,
        in_specs=in_specs,
        out_specs=out_specs,
        check_vma=False,
    )
```

time: 1600 us -> 625 us (0.39)
  waiting for transfers between devices: 1210 us -> 0 us
  Pallas kernels: 0 us -> 371 us
  blocking collectives: 169 us -> 0 us
  local copies, waits for them, and re-layouts: 25.2 us -> 78.9 us
    reduce_scatter x3 -> x0, waiting for transfers between devices: 582 us -> none  [the longest x1 307 us: shards(): lax.psum_scatter(grad_fc2, 'dp', scatter_dimension=0, tiled=True)]
    pallas_call x0 -> x2, Pallas kernels: none -> 371 us  [the longest x1 215 us: scatter_all(): pl.pallas_call(functools.partial(scatter_kernel, count), out_shape=[jax.S...]
    all_gather x4 -> x0, waiting for transfers between devices: 345 us -> none  [the longest x1 128 us: collect_trunk(): lax.all_gather(paired[2], 'dp', axis=0, tiled=True)]
    unnamed x17 -> x0, waiting for transfers between devices: 286 us -> none
    all_gather x6 -> x0, blocking collectives: 86.4 us -> none  [the longest x1 43.5 us: shards(): lax.all_gather(d_modul, ('dp', 'fsdp'), axis=0, tiled=True)]
    psum x2 -> x0, blocking collectives: 83 us -> none  [the longest x1 42 us: shards(): counts = lax.psum(local_counts, ('dp', 'fsdp'))]
    convert_element_type x1 -> x6, local copies, waits for them, and re-layouts: 2.62 us -> 35.4 us  [blocks(): return grad.astype(jnp.bfloat16).reshape((-1,) + shard.shape)]
    unnamed x125 -> x244, local copies, waits for them, and re-layouts: 18.4 us -> 37.8 us
  transfers between devices with their start and end apart: 12 -> 0, of which waited for: 8 -> 0; matrix products, arithmetic and copies ran while one was open for 10% -> 0% of each run, Pallas kernels for 0% -> 0%
where the time goes in v1:
time: 625 us; the launch traced here: 617 us
  Pallas kernels  371 us (59%)
  matrix products  131 us (21%)
  local copies, waits for them, and re-layouts  78.9 us (13%)
  other arithmetic  31 us (5%)
    pallas_call x1, Pallas kernels, scatter_all(): pl.pallas_call(functools.partial(scatter_kernel, count), out_shape=[jax.S...  215 us
    pallas_call x1, Pallas kernels, gather_all(): pl.pallas_call(functools.partial(gather_kernel, count), out_shape=spread...  155 us
    unnamed x244, local copies, waits for them, and re-layouts  37.8 us
    convert_element_type x6, local copies, waits for them, and re-layouts, blocks(): return grad.astype(jnp.bfloat16).reshape((-1,) + shard.shape)  35.4 us
    dot_general x8, matrix products, outer(): lax.dot_general(left, right, ROWS_DIMS, preferred_element_type=jnp.float32)  31.2 us
    dot_general x8, matrix products, times(): return jnp.dot(left, right, preferred_element_type=jnp.float32)  29.6 us
    dot_general x8, matrix products, times_t(): lax.dot_general(left, right, LAST_DIMS, preferred_element_type=jnp.float32)  23.8 us

profile of v1, /device:TPU:16, one launch (start us, length us, event | category | flops | bytes accessed | tf_op | source)
XLA Modules:
  0.0 616.8 jit_solution(5434023960216119938)
XLA Ops:
  7.2 155.5 %gather_all.1 = (f32[16,16,128]{2,1,0:T(8,128)S(1)}, bf16[16,72,1728]{2,1,0:T(8,128)(2,1)S(1)}, bf16[16,72,576]{2,1,0:T(8,128)(2,1)S(1)}, bf16[16,72,2304]{2,1,0...) custom-call(f32[16,128]{1,0:T(8,128)S(1)} %maximum_maximum_fusion.re, ...), custom_call_target="tpu_custom_call" | custom-call | tf_op jit(solution)/shard_map/gather_all/pallas_call | solution.py:268
  175.1 11.3 %convolution_reduce_fusion = f32[6912]{0:T(1024)S(1)} fusion(bf16[6912,1152]{1,0:T(8,128)(2,1)} %param.32, f32[1,1152]{1,0:T(1,128)S(1)} %get-tuple-element.102, bf16[1,1152]{1,0:T(2,128)(2,1)S(1)} %copy-done.65), kind=kOutput, calls=%fused_computation.120 | convolution fusion | flops 15928704 | bytes 15959808 | tf_op jit(solution)/shard_map/dot_general | solution.py:643
  187.1 3.4 fusion.108
  193.8 5.5 maximum_select_fusion
  220.7 5.0 fusion.92
  225.8 4.3 convolution_add_fusion
  230.2 10.5 %convert_reduce_fusion = (f32[2304]{0:T(1024)}, bf16[256,2304]{1,0:T(8,128)(2,1)}, f32[2304]{0:T(1024)}, bf16[256,2304]{1,0:T(8,128)(2,1)S(1)}, bf16[256,2304]{1,0:T(8,128)(2,1)}, /*index=5*/bf16[256,2304]{1,0:T(8,128)(2,1)}) fusion(f32[256,4608]{1,0:T(8,128)} %convolution_add_fusion, pred[]{:T(512)S(6)} %eq.11, f32[256,2304]{1,0:T(8,128)} %convolution_add_fusion.2, ...), kind=kOutput, calls=%fused_computation.50 | convolution fusion | flops 1393749504 | bytes 17722368 | tf_op jit(solution)/shard_map/dot_general | solution.py:635
  243.4 4.9 convolution_bitcast_fusion.2
  259.1 3.9 fusion.87
  263.1 8.6 %fusion.59 = bf16[1,256,1,16,72]{1,4,3,2,0:T(8,128)(2,1)} fusion(f32[16,256,256]{1,2,0:T(8,128)} %fusion.87, f32[16,256,256]{1,2,0:T(8,128)} %copy-done.14, f32[16,256]{1,0:T(8,128)S(1)} %log_add_fusion, pred[256]{0:T(512)(128)(4,1)S(1)} %copy-done.96, bf16[1,256,3,16,72]{1,4,3,2,0:T(8,128)(2,1)S(1)} %copy-done.26), kind=kOutput, calls=%fused_computation.83 | convolution fusion | flops 158929152 | bytes 17990144 | tf_op jit(solution)/shard_map/bhlm,bmhc->blhc/dot_general | solution.py:727
  271.6 8.4 %fusion.62 = bf16[1,256,1,16,72]{1,4,3,2,0:T(8,128)(2,1)} fusion(f32[16,256,256]{1,2,0:T(8,128)} %fusion.87, f32[16,256,256]{1,2,0:T(8,128)} %copy-done.14, f32[16,256]{1,0:T(8,128)S(1)} %log_add_fusion, pred[256]{0:T(512)(128)(4,1)S(1)} %copy-done.96, bf16[1,256,3,16,72]{1,4,3,2,0:T(8,128)(2,1)S(1)} %copy-done.26), kind=kOutput, calls=%fused_computation.84 | convolution fusion | flops 158929152 | bytes 17990144 | tf_op jit(solution)/shard_map/bhlm,blhc->bmhc/dot_general | solution.py:730
  290.4 3.6 fusion.88
  294.0 3.6 fusion.75
  303.0 3.8 multiply_reduce_fusion.2
  319.5 6.4 %convolution_convert_fusion.2 = bf16[4608,576]{0,1:T(8,128)(2,1)} fusion(pred[]{:T(512)S(6)} %eq.11, bf16[256,1152]{0,1:T(8,128)(2,1)S(1)} %copy-done.42, bf16[256,2304]{1,0:T(8,128)(2,1)} %get-tuple-element.106, bf16[256,2304]{1,0:T(8,128)(2,1)} %get-tuple-element.105), kind=kOutput, calls=%fused_computation.3 | convolution fusion | flops 1372372992 | bytes 8258560 | tf_op jit(solution)/shard_map/dot_general | solution.py:641
  326.0 8.4 %copy.65 = bf16[4608,576]{1,0:T(8,128)(2,1)} copy(bf16[4608,576]{0,1:T(8,128)(2,1)} %convolution_convert_fusion.2) | data formatting | bytes 10616832 | tf_op jit(solution)/shard_map/convert_element_type | solution.py:761
  334.4 5.1 convolution_convert_fusion
  344.2 5.6 convolution_convert_fusion.3
  349.8 8.4 %copy.62 = bf16[4608,576]{1,0:T(8,128)(2,1)} copy(bf16[4608,576]{0,1:T(8,128)(2,1)} %convolution_convert_fusion.3) | data formatting | bytes 10616832 | tf_op jit(solution)/shard_map/convert_element_type | solution.py:761
  361.5 6.5 %copy.63 = bf16[1152,1728]{1,0:T(8,128)(2,1)} copy(bf16[1152,1728]{0,1:T(8,128)(2,1)} %convolution_convert_fusion.5) | data formatting | bytes 7962624 | tf_op jit(solution)/shard_map/convert_element_type | solution.py:761
  371.4 6.5 %copy.66 = bf16[1152,1728]{1,0:T(8,128)(2,1)} copy(bf16[1152,1728]{0,1:T(8,128)(2,1)} %convolution_convert_fusion.4) | data formatting | bytes 7962624 | tf_op jit(solution)/shard_map/convert_element_type | solution.py:761
  377.9 3.9 convolution_convert_fusion.1
  381.8 215.2 %scatter_all.1 = (f32[72,2304]{1,0:T(8,128)}, f32[288,576]{1,0:T(8,128)}, f32[72,1728]{1,0:T(8,128)}, f32[72,576]{1,0:T(8,128)}, f32[16,128,128]{2,1,0:T(8,128)}, /*index=5*/f32[16,128,128]{2,1,0:T(8,128)}) custom-call(bf16[16,72,2304]{2,1,0:T(8,128)(2,1)} %bitcast.198, bf16[16,288,576]{2,1,0:T(8,128)(2,1)} %bitcast.200, bf16[16,72,1728]{2,1,0:T(8,128)(2,1)} %bitcast.201, ...), custom_call_target="tpu_custom_call" | custom-call | tf_op jit(solution)/shard_map/scatter_all/pallas_call | solution.py:528
  602.9 8.4 %fusion.96 = f32[1,1152]{1,0:T(1,128)} fusion(f32[1,1152]{1,0:T(1,128)S(1)} %copy-done.68, bf16[1,1152]{1,0:T(2,128)(2,1)S(1)} %copy-done.66, bf16[6912,1]{0,1:T(2,128)(2,1)S(1)} %reshape.820, bf16[6912,1152]{1,0:T(8,128)(2,1)} %param.32), kind=kOutput, calls=%fused_computation.162 | convolution fusion | flops 15933312 | bytes 15950592 | tf_op jit(solution)/shard_map/dot_general | solution.py:754
  (326 shorter events, 105.5 us)
Async XLA Ops:
  2.2 188.2 %copy-start.81 = (f32[256]{0:T(256)}, f32[256]{0:T(256)S(1)}, u32[]{:S(2)}) copy-start(f32[256]{0:T(256)S(1)} %broadcast_multiply_fusion.5) | copy-start | bytes 3076
  2.5 188.0 %copy-start.91 = (f32[256]{0:T(256)}, f32[256]{0:T(256)S(1)}, u32[]{:S(2)}) copy-start(f32[256]{0:T(256)S(1)} %add_rsqrt_fusion.1) | copy-start | bytes 3076
  5.1 181.3 %copy-start.67 = (f32[1,1152]{1,0:T(1,128)}, f32[1,1152]{1,0:T(1,128)S(1)}, u32[]{:S(2)}) copy-start(f32[1,1152]{1,0:T(1,128)S(1)} %get-tuple-element.102) | copy-start | bytes 13828
  175.1 12.0 %copy-start.10 = (bf16[16,72,1728]{2,1,0:T(8,128)(2,1)}, bf16[16,72,1728]{2,1,0:T(8,128)(2,1)S(1)}, u32[]{:S(2)}) copy-start(bf16[16,72,1728]{2,1,0:T(8,128)(2,1)S(1)} %get-tuple-element.31) | copy-start | bytes 11943940
  175.1 11.3 %copy-start.75 = (f32[6912]{0:T(1024)S(1)}, f32[6912]{0:T(1024)}, u32[]{:S(2)}) copy-start(f32[6912]{0:T(1024)} %param.33) | copy-start | bytes 82948
  175.1 12.0 %copy-start.20 = (bf16[1,256,1152]{1,2,0:T(8,128)(2,1)S(1)}, bf16[1,256,1152]{1,2,0:T(8,128)(2,1)}, u32[]{:S(2)}) copy-start(bf16[1,256,1152]{1,2,0:T(8,128)(2,1)} %copy-done.19) | copy-start | bytes 1769476
  187.1 21.2 %copy-start.59 = (f32[1152]{0:T(1024)}, f32[1152]{0:T(1024)S(1)}, u32[]{:S(2)}) copy-start(f32[1152]{0:T(1024)S(1)} %get-tuple-element.89) | copy-start | bytes 13828
  187.1 21.9 %copy-start.55 = (f32[1152]{0:T(1024)}, f32[1152]{0:T(1024)S(1)}, u32[]{:S(2)}) copy-start(f32[1152]{0:T(1024)S(1)} %get-tuple-element.86) | copy-start | bytes 13828
  220.7 9.4 %slice-start.8 = ((s8[5308416]{0:T(1024)(128)(4,1)}), s8[4194304]{0:T(1024)(128)(4,1)S(1)}, s32[]{:S(2)}) async-start(s8[5308416]{0:T(1024)(128)(4,1)} %bitcast.189), calls=%async_computation.8 | async-start | bytes 8388608
  225.8 14.9 %slice-start.2 = ((s8[5308416]{0:T(1024)(128)(4,1)}), s8[1114112]{0:T(1024)(128)(4,1)S(1)}, s32[]{:S(2)}) async-start(s8[5308416]{0:T(1024)(128)(4,1)} %bitcast.174), calls=%async_computation.2 | async-start | bytes 2228224
  225.8 22.4 %slice-start.6 = ((s8[5898240]{0:T(1024)(128)(4,1)}), s8[4194304]{0:T(1024)(128)(4,1)S(1)}, s32[]{:S(2)}) async-start(s8[5898240]{0:T(1024)(128)(4,1)} %bitcast.186), calls=%async_computation.6 | async-start | bytes 8388608
  230.1 10.6 %slice-start.3 = ((s8[5308416]{0:T(1024)(128)(4,1)}), s8[4194304]{0:T(1024)(128)(4,1)S(1)}, s32[]{:S(2)}) async-start(s8[5308416]{0:T(1024)(128)(4,1)} %bitcast.174), calls=%async_computation.3 | async-start | bytes 8388608
  230.1 18.1 %slice-start.7 = ((s8[5898240]{0:T(1024)(128)(4,1)}), s8[1703936]{0:T(1024)(128)(4,1)S(1)}, s32[]{:S(2)}) async-start(s8[5898240]{0:T(1024)(128)(4,1)} %bitcast.186), calls=%async_computation.7 | async-start | bytes 3407872
  263.0 8.6 %copy-start.63 = (f32[16,256]{1,0:T(8,128)}, f32[16,256]{1,0:T(8,128)S(1)}, u32[]{:S(2)}) copy-start(f32[16,256]{1,0:T(8,128)S(1)} %log_add_fusion) | copy-start | bytes 49156
  294.0 9.0 %copy-start.32 = (f32[1,256,576]{1,2,0:T(8,128)S(1)}, f32[1,256,576]{1,2,0:T(8,128)}, u32[]{:S(2)}) copy-start(f32[1,256,576]{1,2,0:T(8,128)} %copy-done.31) | copy-start | bytes 1769476
  294.0 9.0 %copy-start.34 = (f32[1,256,576]{1,2,0:T(8,128)S(1)}, f32[1,256,576]{1,2,0:T(8,128)}, u32[]{:S(2)}) copy-start(f32[1,256,576]{1,2,0:T(8,128)} %copy-done.33) | copy-start | bytes 1769476
  294.0 8.9 %copy-start.70 = (f32[1152]{0:T(1024)S(1)}, f32[1152]{0:T(1024)}, u32[]{:S(2)}) copy-start(f32[1152]{0:T(1024)} %param.27) | copy-start | bytes 13828
  303.0 12.2 %copy-start.24 = (bf16[16,72,256]{2,1,0:T(8,128)(2,1)S(1)}, bf16[16,72,256]{2,1,0:T(8,128)(2,1)}, u32[]{:S(2)}) copy-start(bf16[16,72,256]{2,1,0:T(8,128)(2,1)} %copy-done.23) | copy-start | bytes 1769476
  303.0 12.2 %copy-start.28 = (bf16[256,1152]{0,1:T(8,128)(2,1)S(1)}, bf16[256,1152]{0,1:T(8,128)(2,1)}, u32[]{:S(2)}) copy-start(bf16[256,1152]{0,1:T(8,128)(2,1)} %copy-done.27) | copy-start | bytes 1769476
  349.8 8.4 %copy-start.83 = (f32[256]{0:T(256)S(1)}, f32[256]{0:T(256)}, u32[]{:S(2)}) copy-start(f32[256]{0:T(256)} %copy-done.81) | copy-start | bytes 3076
  349.8 8.4 %copy-start.88 = (f32[1152]{0:T(1024)S(1)}, f32[1152]{0:T(1024)}, u32[]{:S(2)}) copy-start(f32[1152]{0:T(1024)} %copy-done.87) | copy-start | bytes 13828
  349.8 8.4 %copy-start.93 = (f32[256]{0:T(256)S(1)}, f32[256]{0:T(256)}, u32[]{:S(2)}) copy-start(f32[256]{0:T(256)} %copy-done.91) | copy-start | bytes 3076
  602.9 8.4 %copy-start.40 = (bf16[1,256,1152]{1,2,0:T(8,128)(2,1)S(1)}, bf16[1,256,1152]{1,2,0:T(8,128)(2,1)}, u32[]{:S(2)}) copy-start(bf16[1,256,1152]{1,2,0:T(8,128)(2,1)} %get-tuple-element.112) | copy-start | bytes 1769476
  602.9 9.5 %copy-start.50 = (bf16[1,256,1152]{1,2,0:T(8,128)(2,1)S(1)}, bf16[1,256,1152]{1,2,0:T(8,128)(2,1)}, u32[]{:S(2)}) copy-start(bf16[1,256,1152]{1,2,0:T(8,128)(2,1)} %get-tuple-element.108) | copy-start | bytes 1769476
  (89 other events, 303.1 us)

commit v2 on v1

--- a/solution.py
+++ b/solution.py
@@ -47,7 +47,149 @@
 ANY = pl.BlockSpec(memory_space=pl.ANY)
 VMEM = pl.BlockSpec(memory_space=pltpu.VMEM)
 ZS = 4
+TILE = 256
+MID = ((72, 1728), (72, 576))
+ORDER = (
+    ("near", 0, 1),
+    ("near", 0, 0),
+    ("near", 1, 0),
+    ("near", 2, 0),
+    ("line", 0, 0),
+    ("far", 1, 0),
+    ("line", 0, 1),
+    ("near", 3, 0),
+    ("near", 2, 1),
+    ("near", 1, 1),
+    ("line", 2, 0),
+    ("line", 1, 0),
+    ("line", 0, 2),
+    ("far", 3, 0),
+    ("line", 2, 1),
+    ("line", 2, 2),
+    ("far", 1, 1),
+    ("near", 3, 1),
+    ("line", 3, 0),
+    ("line", 1, 1),
+    ("far", 0, 0),
+    ("far", 3, 1),
+    ("line", 1, 2),
+    ("line", 3, 1),
+    ("line", 3, 2),
+    ("own", 1, 0),
+    ("own", 0, 0),
+    ("far", 2, 0),
+    ("own", 2, 0),
+    ("own", 3, 0),
+)
 OFFSETS = (0, -1, 1, -2, 2, -3, 3)
+GATHER_MID = (3, 4)
+GATHER_ORDER = (
+    ("column", 1, 0),
+    ("column", 2, 0),
+    ("column", 0, 0),
+    ("column", 1, 1),
+    ("column", 3, 0),
+    ("column", 2, 1),
+    ("column", 1, -1),
+    ("column", 0, 1),
+    ("column", 2, -1),
+    ("relay", 1, 0),
+    ("column", 4, 0),
+    ("column", 2, 2),
+    ("column", 1, -2),
+    ("column", 0, 2),
+    ("column", 2, -2),
+    ("column", 1, -3),
+    ("column", 1, 2),
+    ("relay", 1, 1),
+    ("relay", 3, 0),
+    ("column", 1, 3),
+    ("relay", 4, 0),
+    ("relay", 1, -1),
+    ("relay", 0, 1),
+    ("column", 2, 3),
+    ("column", 3, 1),
+    ("column", 4, -1),
+    ("column", 0, -1),
+    ("relay", 1, 2),
+    ("relay", 1, 3),
+    ("relay", 2, -1),
+    ("relay", 2, 1),
+    ("relay", 3, -1),
+    ("last", 1, 0),
+    ("relay", 1, -3),
+    ("last", 1, 1),
+    ("column", 0, -2),
+    ("relay", 1, -2),
+    ("relay", 4, 1),
+    ("last", 1, -1),
+    ("column", 0, 3),
+    ("column", 2, -3),
+    ("column", 3, -1),
+    ("relay", 3, 1),
+    ("relay", 0, -1),
+    ("relay", 2, -2),
+    ("relay", 4, 2),
+    ("relay", 2, 0),
+    ("last", 1, 2),
+    ("relay", 2, 3),
+    ("last", 4, 0),
+    ("relay", 4, -1),
+    ("last", 1, 3),
+    ("last", 1, -3),
+    ("column", 4, 1),
+    ("relay", 0, 2),
+    ("last", 1, -2),
+    ("relay", 3, -2),
+    ("column", 0, -3),
+    ("relay", 2, 2),
+    ("last", 2, 2),
+    ("last", 2, -1),
+    ("relay", 4, -2),
+    ("last", 2, 0),
+    ("relay", 0, 3),
+    ("last", 2, 1),
+    ("relay", 4, 3),
+    ("last", 2, -2),
+    ("last", 2, 3),
+    ("relay", 2, -3),
+    ("relay", 3, -3),
+    ("relay", 0, 0),
+    ("column", 3, 2),
+    ("last", 2, -3),
+    ("column", 3, 3),
+    ("relay", 3, 2),
+    ("column", 4, -2),
+    ("last", 0, 1),
+    ("column", 4, 2),
+    ("relay", 3, 3),
+    ("relay", 0, -3),
+    ("column", 3, -2),
+    ("relay", 4, -3),
+    ("last", 3, 1),
+    ("last", 3, 2),
+    ("last", 3, -1),
+    ("column", 4, -3),
+    ("column", 4, 3),
+    ("last", 4, -1),
+    ("last", 0, -3),
+    ("column", 3, -3),
+    ("last", 4, 2),
+    ("last", 0, 2),
+    ("last", 4, -2),
+    ("last", 0, 3),
+    ("last", 0, -1),
+    ("relay", 0, -2),
+    ("last", 3, -2),
+    ("last", 4, 1),
+    ("last", 3, 3),
+    ("last", 0, -2),
+    ("last", 3, 0),
+    ("last", 4, -3),
+    ("last", 4, 3),
+    ("last", 3, -3),
+    ("last", 0, 0),
+)
 
 
 class Place:
@@ -102,7 +244,7 @@
     return [
         dma((count, 16)),
         dma((count, 16)),
-        dma((count, 2, ZS)),
+        dma((count, 2, ZS, 2)),
         dma((count, ZS, 3)),
         dma((count, 16)),
         dma((count,)),
@@ -110,7 +252,8 @@
 
 
 class Gather:
-    def __init__(self, at, k, shard, own, sib, sems):
+    def __init__(self, at, k, shard, own, sib, sems, mid=False):
+        self.mid = mid
         self.at, self.k, self.shard, self.own, self.sib = at, k, shard, own, sib
         self.recv, self.core, self.line, self.pair, self.over, self.local = sems
 
@@ -146,29 +289,38 @@
         else:
             pl.when((level >= 0) & (level < ZS))(lambda: run(level))
 
+    def line_copies(self, off, level, slot, src, j):
+        at, k = self.at, self.k
+        out = []
+        if off <= 0:
+            copy = self.send(src, j, self.line.at[k, 0, level, slot], at.i + 4)
+            out.append((at.z < ZS - 1, copy))
+        if off >= 0:
+            copy = self.send(src, j, self.line.at[k, 1, level, slot], at.i - 4)
+            out.append((at.z > 0, copy))
+        return out
+
     def column_copies(self, off, level):
         at, k = self.at, self.k
         first, second, j = self.pieces(level)
         src = self.shard if off == 0 else self.own.at[j]
-        always = [
-            self.send(src, j, self.pair.at[k, level, 0], at.i + first),
-            self.send(src, j, self.pair.at[k, level, 1], at.i + second),
-            self.across(src, j),
-        ]
-        up = self.send(src, j, self.line.at[k, 0, level], at.i + 4) if off <= 0 else None
-        down = self.send(src, j, self.line.at[k, 1, level], at.i - 4) if off >= 0 else None
-        return always, up, down
+        lines = self.line_copies(off, level, 0, src, j)
+        near = [self.send(src, j, self.pair.at[k, level, 0], at.i + first)]
+        rest = [self.send(src, j, self.pair.at[k, level, 1], at.i + second), self.across(src, j)]
+        if not self.mid:
+            return [], lines, near + rest
+        return (near if off == 0 else []), lines, rest
 
     def column(self, off):
         def run(level):
             if off:
                 self.arrived(level * 4 + self.at.q)
-            always, up, down = self.column_copies(off, level)
-            if up is not None:
-                pl.when(self.at.z < ZS - 1)(up.start)
-            if down is not None:
-                pl.when(self.at.z > 0)(down.start)
-            for copy in always:
+            before, lines, after = self.column_copies(off, level)
+            for copy in before:
+                copy.start()
+            for where, copy in lines:
+                pl.when(where)(copy.start)
+            for copy in after:
                 copy.start()
             if off == 0:
                 self.keep().start()
@@ -180,19 +332,24 @@
             self.shard, self.own.at[self.at.i], self.local.at[self.k]
         )
 
-    def relay_copies(self, level):
+    def relay_copies(self, off, level):
         first, second, column = self.pieces(level)
         j = column + first
-        return (
-            self.send(self.own.at[j], j, self.pair.at[self.k, level, 2], self.at.i + second),
-            self.across(self.own.at[j], j),
-        )
+        src = self.own.at[j]
+        lines = self.line_copies(off, level, 1, src, j) if self.mid else []
+        return lines, [
+            self.send(src, j, self.pair.at[self.k, level, 2], self.at.i + second),
+            self.across(src, j),
+        ]
 
     def relay(self, off):
         def run(level):
             first, _, column = self.pieces(level)
             self.arrived(column + first)
-            for copy in self.relay_copies(level):
+            lines, after = self.relay_copies(off, level)
+            for where, copy in lines:
+                pl.when(where)(copy.start)
+            for copy in after:
                 copy.start()
 
         self.guard(off, run)
@@ -215,14 +372,11 @@
         for off in OFFSETS:
 
             def run(level, off=off):
-                always, up, down = self.column_copies(off, level)
-                if up is not None:
-                    pl.when(at.z < ZS - 1)(up.wait_send)
-                if down is not None:
-                    pl.when(at.z > 0)(down.wait_send)
-                for copy in always:
-                    copy.wait_send()
-                for copy in self.relay_copies(level):
+                before, lines, after = self.column_copies(off, level)
+                more, relays = self.relay_copies(off, level)
+                for where, copy in lines + more:
+                    pl.when(where)(copy.wait_send)
+                for copy in before + after + relays:
                     copy.wait_send()
                 for _, copy in self.last_copies(level):
                     copy.wait_send()
@@ -248,16 +402,11 @@
     sems = refs[3 * count :]
     at = Place()
     at.greet()
-    steps, start = [], 0.0
-    jobs = []
-    for k in range(count):
-        job = Gather(at, k, shards[k], own[k], sib[k], sems)
-        jobs.append(job)
-        span = float(shards[k].shape[0] * shards[k].shape[1])
-        steps += job.events(start, span)
-        start += span
-    for _, action in sorted(steps, key=lambda item: item[0]):
-        action()
+    jobs = [
+        Gather(at, k, shards[k], own[k], sib[k], sems, k in GATHER_MID) for k in range(count)
+    ]
+    for step, k, off in GATHER_ORDER:
+        getattr(jobs[k], step)(off)
     for job in jobs:
         job.finish()
 
@@ -279,6 +428,11 @@
     return outs[:count], outs[count:]
 
 
+def blocked(shape):
+    rows, cols = shape
+    return (rows, cols) if rows % 16 == 0 else (rows // 8, 8, cols)
+
+
 def total(*values):
     out = values[0].astype(jnp.float32)
     for value in values[1:]:
@@ -287,14 +441,15 @@
 
 
 class Scatter:
-    def __init__(self, at, k, mine, other, result, bufs, sems):
+    def __init__(self, at, k, ins, result, bufs, sems):
         self.at, self.k = at, k
-        self.mine, self.other, self.result = mine, other, result
-        self.held, self.cross, self.near, self.far, self.line = bufs
+        self.left, self.right, self.away = ins
+        self.result = result
+        self.left_sib, self.right_sib, self.held, self.near, self.far, self.line = bufs
+        self.mid = self.line.shape[2] == 2
         (
-            self.load_sem,
-            self.cross_send,
-            self.cross_recv,
+            self.swap_send,
+            self.swap_recv,
             self.near_send,
             self.near_recv,
             self.far_send,
@@ -303,20 +458,15 @@
             self.line_recv,
         ) = sems
 
-    def load(self):
-        return pltpu.make_async_copy(self.mine, self.held, self.load_sem.at[self.k])
-
-    def cross_copy(self, level):
+    def swaps(self):
         at, k = self.at, self.k
-        rows = pl.ds(level * 4, 4)
-        return remote(
-            self.other.at[rows],
-            self.cross.at[rows],
-            self.cross_send.at[k, level],
-            self.cross_recv.at[k, level],
-            at.i,
-            1 - at.c,
-        )
+        pairs = ((self.left, self.left_sib), (self.away, self.right_sib))
+        return [
+            remote(
+                src, dst, self.swap_send.at[k, s], self.swap_recv.at[k, s], at.i, 1 - at.c
+            )
+            for s, (src, dst) in enumerate(pairs)
+        ]
 
     def near_copies(self, level):
         at, k = self.at, self.k
@@ -338,125 +488,188 @@
         at, k = self.at, self.k
         first, _ = at.partners(level)
         j = level * 4 + at.q + first
+        slot = 0 if self.mid else level
         return remote(
             self.held.at[j],
-            self.far.at[level],
-            self.far_send.at[k, level],
-            self.far_recv.at[k, level],
+            self.far.at[slot],
+            self.far_send.at[k, slot],
+            self.far_recv.at[k, slot],
             at.i + first,
             at.c,
         )
 
-    def line_copy(self, way, level):
+    def line_copies(self, way, level):
         at, k = self.at, self.k
-        j = level * 4 + at.q
-        return remote(
-            self.held.at[j],
-            self.line.at[way, level],
-            self.line_send.at[k, way, level],
-            self.line_recv.at[k, way, level],
-            at.i + (4 if way == 0 else -4),
-            at.c,
-        )
+        first, _ = at.partners(level)
+        column = level * 4 + at.q
+        return [
+            remote(
+                self.held.at[j],
+                self.line.at[way, level, slot],
+                self.line_send.at[k, way, level, slot],
+                self.line_recv.at[k, way, level, slot],
+                at.i + (4 if way == 0 else -4),
+                at.c,
+            )
+            for slot, j in enumerate((column, column + first)[: 2 if self.mid else 1])
+        ]
+
+    def line_arrived(self, way, level):
+        for copy in self.line_copies(way, level):
+            if way == 0:
+                pl.when(self.at.z > 0)(copy.wait_recv)
+            else:
+                pl.when(self.at.z < ZS - 1)(copy.wait_recv)
 
     def begin(self):
-        self.load().start()
-
-        @pl.loop(0, ZS)
-        def _(level):
-            self.cross_copy(level).start()
-
-        zeros = jnp.zeros(self.line.shape[2:], self.line.dtype)
+        for copy in self.swaps():
+            copy.start()
+
+        zeros = jnp.zeros(self.line.shape[3:], self.line.dtype)
 
         @pl.when(self.at.z == 0)
         def _():
             @pl.loop(0, ZS)
             def _(level):
-                self.line[0, level] = zeros
+                for slot in range(self.line.shape[2]):
+                    self.line[0, level, slot] = zeros
 
         @pl.when(self.at.z == ZS - 1)
         def _():
             @pl.loop(0, ZS)
             def _(level):
-                self.line[1, level] = zeros
-
-    def stage_near(self):
-        self.load().wait()
-
-        @pl.loop(0, ZS)
-        def _(level):
-            first, second = self.at.partners(level)
-            column = level * 4 + self.at.q
-            self.cross_copy(level).wait_recv()
-            copies = self.near_copies(level)
-            for copy, j in zip(copies, (column + second, column + first + second)):
-                self.held[j] = total(self.held[j], self.cross[j]).astype(jnp.bfloat16)
+                for slot in range(self.line.shape[2]):
+                    self.line[1, level, slot] = zeros
+
+    def multiply(self, level):
+        cols = self.held.shape[-1]
+        rows = self.left.shape[0] // 16
+        group = max(1, 288 // rows)
+        height = group * rows
+        wide = cols // TILE
+
+        def block(part, columns):
+            where = pl.ds(pl.multiple_of((level * 4 + part * group) * rows, 32), height)
+            value = jnp.dot(
+                self.left[where, :], self.right[:, columns], preferred_element_type=jnp.float32
+            ) + jnp.dot(
+                self.left_sib[where, :],
+                self.right_sib[:, columns],
+                preferred_element_type=jnp.float32,
+            )
+            for g in range(group):
+                piece = value[g * rows : (g + 1) * rows]
+                if len(self.held.shape) == 4:
+                    piece = piece.reshape((rows // 8, 8, piece.shape[-1]))
+                self.held[level * 4 + part * group + g, ..., columns] = piece.astype(jnp.bfloat16)
+
+        @pl.loop(0, 4 // group)
+        def _(part):
+            @pl.loop(0, wide)
+            def _(t):
+                block(part, pl.ds(pl.multiple_of(t * TILE, TILE), TILE))
+
+            if cols % TILE:
+                block(part, pl.ds(wide * TILE, cols % TILE))
+
+    def ready(self):
+        for copy in self.swaps():
+            copy.wait_recv()
+
+    def stage_near(self, pair):
+        @pl.loop(0, 2)
+        def _(t):
+            level = (1 - pair) * 3 * t + pair * (1 + t)
+            self.multiply(level)
+            for copy in self.near_copies(level):
                 copy.start()
 
-    def stage_far(self):
-        @pl.loop(0, ZS)
-        def _(level):
-            first, _ = self.at.partners(level)
-            j = level * 4 + self.at.q + first
+    def stage_far(self, pair):
+        if self.mid:
+            self.far_mid()
+        else:
+            pl.loop(0, 2)(lambda t: self.far_level((1 - pair) * 3 * t + pair * (1 + t)))
+
+    def far_level(self, level):
+        first, _ = self.at.partners(level)
+        j = level * 4 + self.at.q + first
+        for copy in self.near_copies(level):
+            copy.wait_recv()
+        self.held[j] = total(self.held[j], self.near[level, 1]).astype(jnp.bfloat16)
+        self.far_copy(level).start()
+
+    def far_mid(self):
+        level = self.at.z
+        first, _ = self.at.partners(level)
+        j = level * 4 + self.at.q + first
+        for copy in self.near_copies(level):
+            copy.wait_recv()
+        self.line_arrived(0, level)
+        self.line_arrived(1, level)
+        self.held[j] = total(
+            self.held[j], self.near[level, 1], self.line[0, level, 1], self.line[1, level, 1]
+        ).astype(jnp.bfloat16)
+        self.far_copy(level).start()
+
+    def pass_on(self, way, level):
+        first, _ = self.at.partners(level)
+        column = level * 4 + self.at.q
+        if self.mid:
             for copy in self.near_copies(level):
                 copy.wait_recv()
-            self.held[j] = total(self.held[j], self.cross[j], self.near[level, 1]).astype(
-                jnp.bfloat16
-            )
-            self.far_copy(level).start()
-
-    def stage_line(self):
+        else:
+            self.far_copy(level).wait_recv()
+        self.line_arrived(way, level)
+        copies = self.line_copies(way, level)
+        for slot, copy in enumerate(copies):
+            j = column + slot * first
+            values = [self.held[j], self.near[level, slot], self.line[way, level, slot]]
+            if not self.mid:
+                values.append(self.far[level])
+            self.held[j] = total(*values).astype(jnp.bfloat16)
+            copy.start()
+
+    def stage_line(self, back):
         z = self.at.z
-
-        def pass_on(way, level):
-            j = level * 4 + self.at.q
-            self.far_copy(level).wait_recv()
-            if way == 0:
-                pl.when(z > 0)(self.line_copy(0, level).wait_recv)
-            else:
-                pl.when(z < ZS - 1)(self.line_copy(1, level).wait_recv)
-            self.held[j] = total(
-                self.held[j],
-                self.cross[j],
-                self.near[level, 0],
-                self.far[level],
-                self.line[way, level],
-            ).astype(jnp.bfloat16)
-            self.line_copy(way, level).start()
-
-        @pl.loop(0, ZS - 1)
-        def _(back):
-            level = ZS - 1 - back
-            pl.when(level > z)(lambda: pass_on(0, level))
-            low = back
-            pl.when(low < z)(lambda: pass_on(1, low))
-
-    def stage_own(self):
+        if back < ZS - 1:
+            up, down = ZS - 1 - back, back
+            pl.when(z < up)(lambda: self.pass_on(0, up))
+            pl.when(z > down)(lambda: self.pass_on(1, down))
+
+    def stage_own(self, _):
         z = self.at.z
         j = self.at.i
         self.far_copy(z).wait_recv()
-        pl.when(z > 0)(self.line_copy(0, z).wait_recv)
-        pl.when(z < ZS - 1)(self.line_copy(1, z).wait_recv)
-        self.result[...] = total(
+        if not self.mid:
+            self.line_arrived(0, z)
+            self.line_arrived(1, z)
+        whole = total(
             self.held[j],
-            self.cross[j],
             self.near[z, 0],
-            self.far[z],
-            self.line[0, z],
-            self.line[1, z],
+            self.far[0 if self.mid else z],
+            self.line[0, z, 0],
+            self.line[1, z, 0],
         )
+        self.result[...] = whole.reshape(self.result.shape)
 
     def finish(self):
         z = self.at.z
+        for copy in self.swaps():
+            copy.wait_send()
+
+        if self.mid:
+            self.far_copy(z).wait_send()
 
         @pl.loop(0, ZS)
         def _(level):
-            self.cross_copy(level).wait_send()
             for copy in self.near_copies(level):
                 copy.wait_send()
-            self.far_copy(level).wait_send()
-            pl.when(level > z)(self.line_copy(0, level).wait_send)
-            pl.when(level < z)(self.line_copy(1, level).wait_send)
+            if not self.mid:
+                self.far_copy(level).wait_send()
+            for way in (0, 1):
+                beyond = level > z if way == 0 else level < z
+                for copy in self.line_copies(way, level):
+                    pl.when(beyond)(copy.wait_send)
 
 
 def scatter_kernel(count, *refs):
@@ -467,16 +680,15 @@
         del refs[:n]
         return out
 
-    mine, other, note = take(count), take(count), take(1)[0]
+    ins = [take(3) for _ in range(count)]
+    note = take(1)[0]
     results = take(count)
     note_own, note_sib = take(2)
-    bufs = [take(5) for _ in range(count)]
-    sems, note_sems = take(9), take(6)
+    bufs = [take(6) for _ in range(count)]
+    sems, note_sems = take(8), take(6)
     at = Place()
     at.greet()
-    jobs = [
-        Scatter(at, k, mine[k], other[k], results[k], bufs[k], sems) for k in range(count)
-    ]
+    jobs = [Scatter(at, k, ins[k], results[k], bufs[k], sems) for k in range(count)]
     word = Gather(at, 0, note, note_own, note_sib, note_sems)
     whisper = [action for _, action in sorted(word.events(0.0, 1.0), key=lambda item: item[0])]
     for job in jobs:
@@ -488,54 +700,54 @@
         del whisper[:n]
 
     speak(1)
-    jobs[0].stage_near()
-    speak(5)
-    for k in range(count):
-        if k + 1 < count:
-            jobs[k + 1].stage_near()
-        jobs[k].stage_far()
-        speak(5)
-        if k:
-            jobs[k - 1].stage_own()
-        jobs[k].stage_line()
+    seen = set()
+    for stage, k, part in ORDER:
+        if k not in seen:
+            jobs[k].ready()
+            seen.add(k)
+        getattr(jobs[k], "stage_" + stage)(part)
+        speak(1)
     speak(len(whisper))
-    jobs[-1].stage_own()
     for job in jobs:
         job.finish()
     word.finish()
 
 
-def scatter_all(mine, other, note):
-    count = len(mine)
-    shapes = [g.shape[1:] for g in mine]
+def scatter_all(terms, note):
+    count = len(terms)
     spread = jax.ShapeDtypeStruct((16,) + note.shape, note.dtype)
-    scratch = []
-    for shape in shapes:
-        for lead in ((16,), (16,), (ZS, 2), (ZS,), (2, ZS)):
-            scratch.append(pltpu.VMEM(lead + shape, jnp.bfloat16))
+    scratch, operands = [], []
+    for left, right, away, shard in terms:
+        operands += [left, right, away]
+        scratch.append(pltpu.VMEM(left.shape, jnp.bfloat16))
+        scratch.append(pltpu.VMEM(right.shape, jnp.bfloat16))
+        mid = shard.shape in MID
+        piece = blocked(shard.shape)
+        for lead in ((16,), (ZS, 2), (1 if mid else ZS,), (2, ZS, 2 if mid else 1)):
+            scratch.append(pltpu.VMEM(lead + piece, jnp.bfloat16))
     dma = pltpu.SemaphoreType.DMA
     scratch += [
-        dma((count,)),
-        dma((count, ZS)),
-        dma((count, ZS)),
+        dma((count, 2)),
+        dma((count, 2)),
         dma((count, ZS, 2)),
         dma((count, ZS, 2)),
         dma((count, ZS)),
         dma((count, ZS)),
-        dma((count, 2, ZS)),
-        dma((count, 2, ZS)),
+        dma((count, 2, ZS, 2)),
+        dma((count, 2, ZS, 2)),
     ]
     outs = pl.pallas_call(
         functools.partial(scatter_kernel, count),
-        out_shape=[jax.ShapeDtypeStruct(s, jnp.float32) for s in shapes] + [spread, spread],
-        in_specs=[ANY] * (2 * count) + [VMEM],
+        out_shape=[jax.ShapeDtypeStruct(t[3].shape, jnp.float32) for t in terms]
+        + [spread, spread],
+        in_specs=[VMEM, VMEM, ANY] * count + [VMEM],
         out_specs=[VMEM] * count + [ANY, ANY],
         scratch_shapes=scratch + gather_sems(1),
         compiler_params=pltpu.CompilerParams(
             collective_id=1, has_side_effects=True, vmem_limit_bytes=VMEM_LIMIT
         ),
         name="scatter_all",
-    )(*mine, *other, note)
+    )(*operands, note)
     return outs[:count], outs[count], outs[count + 1]
 
 
@@ -546,10 +758,16 @@
     return own, [lax.dynamic_index_in_dim(p, other, 0, keepdims=False) for p in pair]
 
 
-def scatter_plain(mine, other, note):
+def scatter_plain(terms, note):
     c = lax.axis_index("fsdp")
     results = []
-    for own, sib in zip(mine, other):
+    for left, right, away, shard in terms:
+        own, sib = [
+            jnp.dot(left, half, preferred_element_type=jnp.float32)
+            .astype(jnp.bfloat16)
+            .reshape((-1,) + shard.shape)
+            for half in (right, away)
+        ]
         pair = jnp.where(c == 0, jnp.stack([own, sib]), jnp.stack([sib, own]))
         half = lax.psum_scatter(pair, "fsdp", scatter_dimension=0, tiled=False)
         results.append(
@@ -637,9 +855,6 @@
     def times_t(left, right):
         return lax.dot_general(left, right, LAST_DIMS, preferred_element_type=jnp.float32)
 
-    def outer(left, right):
-        return lax.dot_general(left, right, ROWS_DIMS, preferred_element_type=jnp.float32)
-
     modul = lax.dot_general(silu_cond, w_ada, LAST_DIMS, preferred_element_type=jnp.float32) + b_ada
     pieces = [modul[:, None, part_index * D : (part_index + 1) * D] for part_index in range(6)]
     shift_one, scale_one, gate_one, shift_two, scale_two, gate_two = pieces
@@ -690,13 +905,11 @@
     d_gate_two = jnp.sum(grad_out * branch, axis=1)
     d_branch = (gate_two * grad_out).astype(jnp.bfloat16).reshape(row_count, D)
     d_branch_own, d_branch_sib = split(d_branch)
-    fc2_mine, fc2_other = outer(active, d_branch_own), outer(active, d_branch_sib)
     bias_fc2 = jnp.sum(d_branch, axis=0, dtype=jnp.float32)
     d_active = times_t(d_branch_own, fc2_own) + times_t(d_branch_sib, fc2_sib)
     d_active_own, d_active_sib = split(d_active)
     d_hidden_own = jax.vjp(gelu_tanh, hidden_own)[1](d_active_own)[0].astype(jnp.bfloat16)
     d_hidden_sib = jax.vjp(gelu_tanh, hidden_sib)[1](d_active_sib)[0].astype(jnp.bfloat16)
-    fc1_mine, fc1_other = outer(mlp_in, d_hidden_own), outer(mlp_in, d_hidden_sib)
     bias_fc1 = join(
         jnp.sum(d_hidden_own, axis=0, dtype=jnp.float32),
         jnp.sum(d_hidden_sib, axis=0, dtype=jnp.float32),
@@ -710,7 +923,6 @@
     d_gate_one = jnp.sum(d_middle * attn_out, axis=1)
     d_attn = (gate_one * d_middle).astype(jnp.bfloat16).reshape(row_count, D)
     d_attn_own, d_attn_sib = split(d_attn)
-    proj_mine, proj_other = outer(attended, d_attn_own), outer(attended, d_attn_sib)
     bias_proj = jnp.sum(d_attn, axis=0, dtype=jnp.float32)
     d_attended = times_t(d_attn_own, proj_own) + times_t(d_attn_sib, proj_sib)
     d_attended = d_attended.astype(jnp.bfloat16).reshape(images, SEQ, H, HD)
@@ -736,7 +948,6 @@
         .reshape(row_count, 3 * D)
     )
     d_qkv_own, d_qkv_sib = split(d_qkv)
-    qkv_mine, qkv_other = outer(attn_in, d_qkv_own), outer(attn_in, d_qkv_sib)
     bias_query = jnp.sum(d_qkv[:, :D], axis=0, dtype=jnp.float32)
     bias_value = jnp.sum(d_qkv[:, 2 * D :], axis=0, dtype=jnp.float32)
     d_attn_in = (times_t(d_qkv_own, qkv_own) + times_t(d_qkv_sib, qkv_sib)).reshape(
@@ -757,13 +968,13 @@
         biases + [d_modul.astype(jnp.float32).reshape(-1), jnp.zeros((2 * lanes,), jnp.float32)]
     ).reshape(-1, lanes)
 
-    def blocks(grad, shard):
-        return grad.astype(jnp.bfloat16).reshape((-1,) + shard.shape)
-
-    owners = [w_fc1, w_fc2, w_qkv, w_proj]
-    mine = [blocks(g, w) for g, w in zip([fc1_mine, fc2_mine, qkv_mine, proj_mine], owners)]
-    other = [blocks(g, w) for g, w in zip([fc1_other, fc2_other, qkv_other, proj_other], owners)]
-    (grad_fc1, grad_fc2, grad_qkv, grad_proj), note_own, note_sib = scatter(mine, other, note)
+    terms = [
+        (attended.T, d_attn_own, d_attn_sib, w_proj),
+        (active.T, d_branch_own, d_branch_sib, w_fc2),
+        (attn_in.T, d_qkv_own, d_qkv_sib, w_qkv),
+        (mlp_in.T, d_hidden_own, d_hidden_sib, w_fc1),
+    ]
+    (grad_proj, grad_fc2, grad_qkv, grad_fc1), note_own, note_sib = scatter(terms, note)
     total_note = (jnp.sum(note_own, axis=0) + jnp.sum(note_sib, axis=0)).reshape(-1)
     summed, start = [], 0
     for vector in biases + [b_ada]:

time: 625 us -> 478 us (0.76)
  Pallas kernels: 371 us -> 293 us
  local copies, waits for them, and re-layouts: 78.9 us -> 41 us
  matrix products: 131 us -> 104 us
    pallas_call x1, Pallas kernels: 215 us -> 160 us  [scatter_all(): pl.pallas_call(functools.partial(scatter_kernel, count), out_shape=[jax.S...]
    convert_element_type x6 -> x0, local copies, waits for them, and re-layouts: 35.4 us -> none  [blocks(): return grad.astype(jnp.bfloat16).reshape((-1,) + shard.shape)]
    dot_general x8 -> x0, matrix products: 31.2 us -> none  [outer(): lax.dot_general(left, right, ROWS_DIMS, preferred_element_type=jnp.float32)]
    pallas_call x1, Pallas kernels: 155 us -> 132 us  [gather_all(): pl.pallas_call(functools.partial(gather_kernel, count), out_shape=spread...]
    unnamed x244 -> x250, local copies, waits for them, and re-layouts: 37.8 us -> 29.5 us
where the time goes in v2:
time: 478 us; the launch traced here: 473 us
  Pallas kernels  293 us (61%)
  matrix products  104 us (22%)
  local copies, waits for them, and re-layouts  41 us (9%)
  other arithmetic  30.2 us (6%)
  between operations  5.23 us (1%)
    pallas_call x1, Pallas kernels, scatter_all(): pl.pallas_call(functools.partial(scatter_kernel, count), out_shape=[jax.S...  160 us
    pallas_call x1, Pallas kernels, gather_all(): pl.pallas_call(functools.partial(gather_kernel, count), out_shape=spread...  132 us
    dot_general x8, matrix products, times(): return jnp.dot(left, right, preferred_element_type=jnp.float32)  29.9 us
    unnamed x250, local copies, waits for them, and re-layouts  29.5 us
    dot_general x8, matrix products, times_t(): lax.dot_general(left, right, LAST_DIMS, preferred_element_type=jnp.float32)  27.7 us
    dot_general x1, matrix products, shards(): lax.dot_general(silu_cond, w_ada, LAST_DIMS, preferred_element_type=jnp.f...  11.3 us

profile of v2, /device:TPU:16, one launch (start us, length us, event | category | flops | bytes accessed | tf_op | source)
XLA Modules:
  0.0 472.9 jit_solution(1946829729737750292)
XLA Ops:
  7.2 132.1 %gather_all.1 = (f32[16,16,128]{2,1,0:T(8,128)S(1)}, bf16[16,72,1728]{2,1,0:T(8,128)(2,1)S(1)}, bf16[16,72,576]{2,1,0:T(8,128)(2,1)S(1)}, bf16[16,72,2304]{2,1,0...) custom-call(f32[16,128]{1,0:T(8,128)S(1)} %maximum_maximum_fusion.re, ...), custom_call_target="tpu_custom_call" | custom-call | tf_op jit(solution)/shard_map/gather_all/pallas_call | solution.py:417
  139.3 2.5 copy-done
  141.8 2.5 copy-done.1
  151.5 11.3 %convolution_reduce_fusion = f32[6912]{0:T(1024)S(1)} fusion(bf16[6912,1152]{1,0:T(8,128)(2,1)} %param.32, f32[1,1152]{1,0:T(1,128)S(1)} %get-tuple-element.102, bf16[1,1152]{1,0:T(2,128)(2,1)S(1)} %copy-done.64), kind=kOutput, calls=%fused_computation.112 | convolution fusion | flops 15928704 | bytes 15959808 | tf_op jit(solution)/shard_map/dot_general | solution.py:858
  163.6 3.4 fusion.87
  167.0 3.4 fusion.89
  170.4 5.4 %maximum_select_fusion = f32[256,3456]{0,1:T(8,128)} fusion(f32[256,1728]{0,1:T(8,128)} %fusion.87, f32[256,1728]{0,1:T(8,128)} %fusion.89, pred[]{:T(512)S(6)} %eq.11), kind=kLoop, calls=%fused_computation.12 | loop fusion | flops 2654208 | bytes 7077889 | tf_op jit(solution)/shard_map/jit(_where)/select_n | solution.py:814
  176.1 2.5 add_convert_fusion
  186.2 3.4 convolution_add_fusion.2
  196.5 7.2 %fusion.124 = f32[256,4608]{1,0:T(8,128)} fusion(bf16[256,576]{0,1:T(8,128)(2,1)S(1)} %get-tuple-element.121, bf16[4608,576]{1,0:T(8,128)(2,1)} %bitcast.175), kind=kOutput, calls=%fused_computation.204 | convolution fusion | flops 1358954496 | bytes 10321920 | tf_op jit(solution)/shard_map/dot_general | solution.py:856
  203.8 6.8 %convolution_add_fusion = f32[256,4608]{1,0:T(8,128)} fusion(f32[256,4608]{1,0:T(8,128)} %fusion.124, bf16[256,576]{0,1:T(8,128)(2,1)S(1)} %get-tuple-element.120, bf16[4608,576]{1,0:T(8,128)(2,1)S(1)} %bitcast.185), kind=kOutput, calls=%fused_computation.1 | convolution fusion | flops 1360134144 | bytes 15040512 | tf_op jit(solution)/shard_map/dot_general | solution.py:856
  210.7 10.7 %convert_reduce_fusion = (f32[2304]{0:T(1024)}, bf16[256,2304]{1,0:T(8,128)(2,1)}, f32[2304]{0:T(1024)}, bf16[256,2304]{1,0:T(8,128)(2,1)S(1)}, bf16[256,2304]{1,0:T(8,128)(2,1)}, /*index=5*/bf16[256,2304]{1,0:T(8,128)(2,1)}) fusion(f32[256,4608]{1,0:T(8,128)} %convolution_add_fusion, pred[]{:T(512)S(6)} %eq.11, f32[256,2304]{1,0:T(8,128)} %convolution_add_fusion.2, ...), kind=kOutput, calls=%fused_computation.42 | convolution fusion | flops 1395224064 | bytes 18323456 | tf_op jit(solution)/shard_map/dot_general | solution.py:853
  221.4 2.7 fusion.125
  224.1 4.9 %convolution_bitcast_fusion.2 = f32[1,256,576]{1,2,0:T(8,128)S(1)} fusion(bf16[4608,576]{1,0:T(8,128)(2,1)S(1)} %bitcast.186, bf16[256,2304]{1,0:T(8,128)(2,1)} %get-tuple-element.106, bf16[256,2304]{1,0:T(8,128)(2,1)} %get-tuple-element.105, pred[]{:T(512)S(6)} %eq.11), kind=kOutput, calls=%fused_computation.78 | convolution fusion | flops 1369571328 | bytes 8257537 | tf_op jit(solution)/shard_map/dot_general | solution.py:853
  231.5 3.2 multiply_reduce_fusion.1
  241.5 2.7 fusion.91
  244.3 8.9 %fusion.59 = bf16[1,256,1,16,72]{1,4,3,2,0:T(8,128)(2,1)} fusion(f32[16,256,256]{1,2,0:T(8,128)} %fusion.91, f32[16,256,256]{1,2,0:T(8,128)} %copy-done.14, f32[16,256]{1,0:T(8,128)S(1)} %log_add_fusion, pred[256]{0:T(512)(128)(4,1)S(1)} %copy-done.101, bf16[1,256,3,16,72]{1,4,3,2,0:T(8,128)(2,1)S(1)} %copy-done.23), kind=kOutput, calls=%fused_computation.75 | convolution fusion | flops 158929152 | bytes 17990144 | tf_op jit(solution)/shard_map/bhlm,bmhc->blhc/dot_general | solution.py:939
  253.1 8.7 %fusion.62 = bf16[1,256,1,16,72]{1,4,3,2,0:T(8,128)(2,1)} fusion(f32[16,256,256]{1,2,0:T(8,128)} %fusion.91, f32[16,256,256]{1,2,0:T(8,128)} %copy-done.14, f32[16,256]{1,0:T(8,128)S(1)} %log_add_fusion, pred[256]{0:T(512)(128)(4,1)S(1)} %copy-done.101, bf16[1,256,3,16,72]{1,4,3,2,0:T(8,128)(2,1)S(1)} %copy-done.23), kind=kOutput, calls=%fused_computation.76 | convolution fusion | flops 158929152 | bytes 17990144 | tf_op jit(solution)/shard_map/bhlm,blhc->bmhc/dot_general | solution.py:942
  261.8 3.1 fusion.65
  269.0 4.1 fusion.127
  276.9 4.0 multiply_reduce_fusion.2
  283.3 2.8 fusion.110
  292.2 160.5 %scatter_all.1 = (f32[72,576]{1,0:T(8,128)}, f32[288,576]{1,0:T(8,128)}, f32[72,1728]{1,0:T(8,128)}, f32[72,2304]{1,0:T(8,128)}, f32[16,128,128]{2,1,0:T(8,128)}, /*index=5*/f32[16,128,128]{2,1,0:T(8,128)}) custom-call(bf16[1152,256]{1,0:T(8,128)(2,1)} %bitcast.206, bf16[256,576]{1,0:T(8,128)(2,1)} %copy.64.refs_1_, bf16[256,576]{1,0:T(8,128)(2,1)} %copy.65.refs_2_, ...), custom_call_target="tpu_custom_call" | custom-call | tf_op jit(solution)/shard_map/scatter_all/pallas_call | solution.py:739
  458.8 8.4 %fusion.97 = f32[1,1152]{1,0:T(1,128)} fusion(f32[1,1152]{1,0:T(1,128)S(1)} %copy-done.67, bf16[1,1152]{1,0:T(2,128)(2,1)S(1)} %copy-done.65, bf16[6912,1]{0,1:T(2,128)(2,1)S(1)} %reshape.788, bf16[6912,1152]{1,0:T(8,128)(2,1)} %param.32), kind=kOutput, calls=%fused_computation.155 | convolution fusion | flops 15933312 | bytes 15950592 | tf_op jit(solution)/shard_map/dot_general | solution.py:965
  (328 shorter events, 62.6 us)
Async XLA Ops:
  2.2 164.7 %copy-start.91 = (f32[256]{0:T(256)}, f32[256]{0:T(256)S(1)}, u32[]{:S(2)}) copy-start(f32[256]{0:T(256)S(1)} %broadcast_multiply_fusion.5) | copy-start | bytes 3076
  2.5 164.5 %copy-start.97 = (f32[256]{0:T(256)}, f32[256]{0:T(256)S(1)}, u32[]{:S(2)}) copy-start(f32[256]{0:T(256)S(1)} %add_rsqrt_fusion.1) | copy-start | bytes 3076
  5.1 157.7 %copy-start.66 = (f32[1,1152]{1,0:T(1,128)}, f32[1,1152]{1,0:T(1,128)S(1)}, u32[]{:S(2)}) copy-start(f32[1,1152]{1,0:T(1,128)S(1)} %get-tuple-element.102) | copy-start | bytes 13828
  151.5 12.0 %copy-start.10 = (bf16[16,72,1728]{2,1,0:T(8,128)(2,1)}, bf16[16,72,1728]{2,1,0:T(8,128)(2,1)S(1)}, u32[]{:S(2)}) copy-start(bf16[16,72,1728]{2,1,0:T(8,128)(2,1)S(1)} %get-tuple-element.31) | copy-start | bytes 11943940
  151.5 11.3 %copy-start.79 = (f32[6912]{0:T(1024)S(1)}, f32[6912]{0:T(1024)}, u32[]{:S(2)}) copy-start(f32[6912]{0:T(1024)} %param.33) | copy-start | bytes 82948
  151.5 12.0 %copy-start.19 = (bf16[1,256,1152]{1,2,0:T(8,128)(2,1)S(1)}, bf16[1,256,1152]{1,2,0:T(8,128)(2,1)}, u32[]{:S(2)}) copy-start(bf16[1,256,1152]{1,2,0:T(8,128)(2,1)} %copy-done.18) | copy-start | bytes 1769476
  163.5 21.1 %copy-start.59 = (f32[1152]{0:T(1024)}, f32[1152]{0:T(1024)S(1)}, u32[]{:S(2)}) copy-start(f32[1152]{0:T(1024)S(1)} %get-tuple-element.89) | copy-start | bytes 13828
  163.5 22.6 %copy-start.54 = (f32[1152]{0:T(1024)}, f32[1152]{0:T(1024)S(1)}, u32[]{:S(2)}) copy-start(f32[1152]{0:T(1024)S(1)} %get-tuple-element.86) | copy-start | bytes 13828
  163.5 22.6 %copy-start.70 = (f32[1152]{0:T(1024)}, f32[1152]{0:T(1024)S(1)}, u32[]{:S(2)}) copy-start(f32[1152]{0:T(1024)S(1)} %get-tuple-element.85) | copy-start | bytes 13828
  196.5 7.3 %copy-start.30 = (bf16[256,576]{0,1:T(8,128)(2,1)}, bf16[256,576]{0,1:T(8,128)(2,1)S(1)}, u32[]{:S(2)}) copy-start(bf16[256,576]{0,1:T(8,128)(2,1)S(1)} %get-tuple-element.121) | copy-start | bytes 884740
  196.5 7.2 %copy-start.38 = (bf16[256,576]{0,1:T(8,128)(2,1)}, bf16[256,576]{0,1:T(8,128)(2,1)S(1)}, u32[]{:S(2)}) copy-start(bf16[256,576]{0,1:T(8,128)(2,1)S(1)} %get-tuple-element.120) | copy-start | bytes 884740
  196.5 7.2 %slice-start.2 = ((s8[5898240]{0:T(1024)(128)(4,1)}), s8[4194304]{0:T(1024)(128)(4,1)S(1)}, s32[]{:S(2)}) async-start(s8[5898240]{0:T(1024)(128)(4,1)} %bitcast.183), calls=%async_computation.2 | async-start | bytes 8388608
  196.5 7.2 %slice-start.3 = ((s8[5898240]{0:T(1024)(128)(4,1)}), s8[1703936]{0:T(1024)(128)(4,1)S(1)}, s32[]{:S(2)}) async-start(s8[5898240]{0:T(1024)(128)(4,1)} %bitcast.183), calls=%async_computation.3 | async-start | bytes 3407872
  196.5 14.1 %slice-start.4 = ((s8[5308416]{0:T(1024)(128)(4,1)}), s8[4194304]{0:T(1024)(128)(4,1)S(1)}, s32[]{:S(2)}) async-start(s8[5308416]{0:T(1024)(128)(4,1)} %bitcast.187), calls=%async_computation.4 | async-start | bytes 8388608
  203.7 6.9 %slice-start.5 = ((s8[5308416]{0:T(1024)(128)(4,1)}), s8[1114112]{0:T(1024)(128)(4,1)S(1)}, s32[]{:S(2)}) async-start(s8[5308416]{0:T(1024)(128)(4,1)} %bitcast.187), calls=%async_computation.5 | async-start | bytes 2228224
  203.8 6.9 %copy-start.16 = (f32[1,256,1152]{1,2,0:T(8,128)S(1)}, f32[1,256,1152]{1,2,0:T(8,128)}, u32[]{:S(2)}) copy-start(f32[1,256,1152]{1,2,0:T(8,128)} %copy-done.15) | copy-start | bytes 3538948
  203.8 6.9 %copy-start.55 = (f32[1152]{0:T(1024)S(1)}, f32[1152]{0:T(1024)}, u32[]{:S(2)}) copy-start(f32[1152]{0:T(1024)} %copy-done.54) | copy-start | bytes 13828
  203.8 6.9 %copy-start.71 = (f32[1152]{0:T(1024)S(1)}, f32[1152]{0:T(1024)}, u32[]{:S(2)}) copy-start(f32[1152]{0:T(1024)} %copy-done.70) | copy-start | bytes 13828
  203.8 17.6 %slice-start.8 = ((s8[5308416]{0:T(1024)(128)(4,1)}), s8[4194304]{0:T(1024)(128)(4,1)S(1)}, s32[]{:S(2)}) async-start(s8[5308416]{0:T(1024)(128)(4,1)} %bitcast.194), calls=%async_computation.8 | async-start | bytes 8388608
  203.8 25.1 %slice-start = ((s8[5898240]{0:T(1024)(128)(4,1)}), s8[4194304]{0:T(1024)(128)(4,1)S(1)}, s32[]{:S(2)}) async-start(s8[5898240]{0:T(1024)(128)(4,1)} %bitcast.176), calls=%async_computation | async-start | bytes 8388608
  210.7 10.7 %slice-start.9 = ((s8[5308416]{0:T(1024)(128)(4,1)}), s8[1114112]{0:T(1024)(128)(4,1)S(1)}, s32[]{:S(2)}) async-start(s8[5308416]{0:T(1024)(128)(4,1)} %bitcast.194), calls=%async_computation.9 | async-start | bytes 2228224
  210.7 18.3 %slice-start.1 = ((s8[5898240]{0:T(1024)(128)(4,1)}), s8[1703936]{0:T(1024)(128)(4,1)S(1)}, s32[]{:S(2)}) async-start(s8[5898240]{0:T(1024)(128)(4,1)} %bitcast.176), calls=%async_computation.1 | async-start | bytes 3407872
  458.7 8.4 %copy-start.40 = (bf16[1,256,1152]{1,2,0:T(8,128)(2,1)S(1)}, bf16[1,256,1152]{1,2,0:T(8,128)(2,1)}, u32[]{:S(2)}) copy-start(bf16[1,256,1152]{1,2,0:T(8,128)(2,1)} %get-tuple-element.116) | copy-start | bytes 1769476
  458.7 9.5 %copy-start.49 = (bf16[1,256,1152]{1,2,0:T(8,128)(2,1)S(1)}, bf16[1,256,1152]{1,2,0:T(8,128)(2,1)}, u32[]{:S(2)}) copy-start(bf16[1,256,1152]{1,2,0:T(8,128)(2,1)} %get-tuple-element.112) | copy-start | bytes 1769476
  (91 other events, 290.7 us)

commit v3 on v2

--- a/solution.py
+++ b/solution.py
@@ -43,152 +43,198 @@
     )
 
 
-VMEM_LIMIT = 66_000_000
+VMEM_LIMIT = 67_000_000
 ANY = pl.BlockSpec(memory_space=pl.ANY)
 VMEM = pl.BlockSpec(memory_space=pltpu.VMEM)
 ZS = 4
 TILE = 256
-MID = ((72, 1728), (72, 576))
+MID = (1,)
 ORDER = (
-    ("near", 0, 1),
-    ("near", 0, 0),
-    ("near", 1, 0),
-    ("near", 2, 0),
-    ("line", 0, 0),
-    ("far", 1, 0),
-    ("line", 0, 1),
-    ("near", 3, 0),
-    ("near", 2, 1),
-    ("near", 1, 1),
-    ("line", 2, 0),
-    ("line", 1, 0),
-    ("line", 0, 2),
-    ("far", 3, 0),
-    ("line", 2, 1),
-    ("line", 2, 2),
-    ("far", 1, 1),
-    ("near", 3, 1),
-    ("line", 3, 0),
-    ("line", 1, 1),
-    ("far", 0, 0),
-    ("far", 3, 1),
-    ("line", 1, 2),
-    ("line", 3, 1),
-    ("line", 3, 2),
-    ("own", 1, 0),
-    ("own", 0, 0),
-    ("far", 2, 0),
-    ("own", 2, 0),
-    ("own", 3, 0),
+    (0, 1, 0),
+    (0, 0, 0),
+    (2, 1, 0),
+    (1, 0, 0),
+    (0, 0, 1),
+    (0, 1, 1),
+    (2, 0, 0),
+    (1, 0, 1),
+    (2, 1, 1),
+    (2, 1, 2),
+    (2, 0, 1),
+    (1, 1, 0),
+    (2, 0, 2),
+    (3, 1, 0),
+    (3, 0, 0),
 )
+BACK_MID = ()
+BACK_ORDER = (
+    (0, -1, 0),
+    (1, -1, 0),
+    (0, 0, 0),
+    (0, 0, 1),
+    (1, -1, 1),
+    (1, -1, 2),
+    (2, -1, 0),
+    (0, 1, 0),
+    (3, -1, 0),
+    (4, -1, 0),
+    (5, -1, 0),
+    (5, -1, 1),
+    (1, 0, 0),
+    (1, 0, 1),
+    (5, -1, 2),
+    (1, 1, 0),
+    (0, 1, 1),
+    (2, 0, 0),
+    (2, 0, 1),
+    (5, -1, 3),
+    (1, 1, 1),
+    (2, 1, 0),
+    (6, -1, 0),
+    (2, 0, 2),
+    (3, 0, 0),
+    (2, 1, 1),
+    (2, 1, 2),
+    (7, -1, 0),
+    (8, -1, 0),
+    (3, 1, 0),
+)
+BACK_TASKS = ("seed", "widen", "mix", "centre", "project", "attend", "part", "query", "leave")
 OFFSETS = (0, -1, 1, -2, 2, -3, 3)
-GATHER_MID = (3, 4)
+STEPS = ("column", "relay", "last")
+TASKS = ("start", "mod", "ln", "load", "query", "attend", "project", "mid", "widen", "narrow", "last")
+WEIGHTS = ("qkv", "proj", "fc1", "fc2")
+STAGES = ("near", "far", "line", "own")
+GATHER_MID = (3,)
 GATHER_ORDER = (
-    ("column", 1, 0),
-    ("column", 2, 0),
-    ("column", 0, 0),
-    ("column", 1, 1),
-    ("column", 3, 0),
-    ("column", 2, 1),
-    ("column", 1, -1),
-    ("column", 0, 1),
-    ("column", 2, -1),
-    ("relay", 1, 0),
-    ("column", 4, 0),
-    ("column", 2, 2),
-    ("column", 1, -2),
-    ("column", 0, 2),
-    ("column", 2, -2),
-    ("column", 1, -3),
-    ("column", 1, 2),
-    ("relay", 1, 1),
-    ("relay", 3, 0),
-    ("column", 1, 3),
-    ("relay", 4, 0),
-    ("relay", 1, -1),
-    ("relay", 0, 1),
-    ("column", 2, 3),
-    ("column", 3, 1),
-    ("column", 4, -1),
-    ("column", 0, -1),
-    ("relay", 1, 2),
-    ("relay", 1, 3),
-    ("relay", 2, -1),
-    ("relay", 2, 1),
-    ("relay", 3, -1),
-    ("last", 1, 0),
-    ("relay", 1, -3),
-    ("last", 1, 1),
-    ("column", 0, -2),
-    ("relay", 1, -2),
-    ("relay", 4, 1),
-    ("last", 1, -1),
-    ("column", 0, 3),
-    ("column", 2, -3),
-    ("column", 3, -1),
-    ("relay", 3, 1),
-    ("relay", 0, -1),
-    ("relay", 2, -2),
-    ("relay", 4, 2),
-    ("relay", 2, 0),
-    ("last", 1, 2),
-    ("relay", 2, 3),
-    ("last", 4, 0),
-    ("relay", 4, -1),
-    ("last", 1, 3),
-    ("last", 1, -3),
-    ("column", 4, 1),
-    ("relay", 0, 2),
-    ("last", 1, -2),
-    ("relay", 3, -2),
-    ("column", 0, -3),
-    ("relay", 2, 2),
-    ("last", 2, 2),
-    ("last", 2, -1),
-    ("relay", 4, -2),
-    ("last", 2, 0),
-    ("relay", 0, 3),
-    ("last", 2, 1),
-    ("relay", 4, 3),
-    ("last", 2, -2),
-    ("last", 2, 3),
-    ("relay", 2, -3),
-    ("relay", 3, -3),
-    ("relay", 0, 0),
-    ("column", 3, 2),
-    ("last", 2, -3),
-    ("column", 3, 3),
-    ("relay", 3, 2),
-    ("column", 4, -2),
-    ("last", 0, 1),
-    ("column", 4, 2),
-    ("relay", 3, 3),
-    ("relay", 0, -3),
-    ("column", 3, -2),
-    ("relay", 4, -3),
-    ("last", 3, 1),
-    ("last", 3, 2),
-    ("last", 3, -1),
-    ("column", 4, -3),
-    ("column", 4, 3),
-    ("last", 4, -1),
-    ("last", 0, -3),
-    ("column", 3, -3),
-    ("last", 4, 2),
-    ("last", 0, 2),
-    ("last", 4, -2),
-    ("last", 0, 3),
-    ("last", 0, -1),
-    ("relay", 0, -2),
-    ("last", 3, -2),
-    ("last", 4, 1),
-    ("last", 3, 3),
-    ("last", 0, -2),
-    ("last", 3, 0),
-    ("last", 4, -3),
-    ("last", 4, 3),
-    ("last", 3, -3),
-    ("last", 0, 0),
+    (0, 0, 0),
+    (0, 1, 0),
+    (0, 2, 0),
+    (0, 1, -1),
+    (0, 1, 1),
+    (0, 3, 0),
+    (0, 1, -2),
+    (0, 0, -1),
+    (0, 1, 2),
+    (0, 2, 1),
+    (0, -1, 0),
+    (0, 1, 3),
+    (0, 1, -3),
+    (1, 1, 0),
+    (0, 2, -1),
+    (1, 2, 0),
+    (0, 2, 2),
+    (0, 0, -2),
+    (0, 2, -2),
+    (0, 3, 1),
+    (0, 2, -3),
+    (1, -1, 0),
+    (1, 1, -3),
+    (0, 0, 1),
+    (0, 4, 0),
+    (2, 1, -3),
+    (1, 2, 1),
+    (0, 3, 2),
+    (0, 0, -3),
+    (1, 1, 3),
+    (1, 1, 1),
+    (1, 3, 0),
+    (0, 3, -1),
+    (1, 2, -1),
+    (0, 0, 2),
+    (1, 1, -1),
+    (1, 0, 0),
+    (1, 0, -3),
+    (1, 3, -1),
+    (1, 1, -2),
+    (1, 0, -2),
+    (2, 1, 3),
+    (2, 1, 0),
+    (2, 0, -3),
+    (1, 1, 2),
+    (1, 3, -2),
+    (0, 4, -1),
+    (1, 2, -3),
+    (0, 4, 1),
+    (1, 2, -2),
+    (1, -1, 1),
+    (2, -1, 0),
+    (1, 3, -3),
+    (2, 0, -2),
+    (0, 4, -2),
+    (0, 2, 3),
+    (1, 3, 1),
+    (1, 2, 2),
+    (2, 1, 2),
+    (2, 0, 0),
+    (1, 3, 2),
+    (2, 1, -1),
+    (0, 0, 3),
+    (2, 1, 1),
+    (2, 1, -2),
+    (0, 4, 2),
+    (2, 3, 0),
+    (0, 4, -3),
+    (3, -1, 0),
+    (2, 2, -3),
+    (1, 4, 0),
+    (4, -1, 0),
+    (4, -1, 1),
+    (1, 3, 3),
+    (0, 3, -2),
+    (1, 0, 2),
+    (1, 2, 3),
+    (2, 3, -1),
+    (5, -1, 0),
+    (5, -1, 1),
+    (2, 2, 0),
+    (1, 4, -2),
+    (0, 3, -3),
+    (0, 3, 3),
+    (1, 4, -1),
+    (2, 2, 1),
+    (1, 0, 3),
+    (5, -1, 2),
+    (2, 2, 2),
+    (2, 2, 3),
+    (5, -1, 3),
+    (2, 2, -1),
+    (2, 2, -2),
+    (0, 4, 3),
+    (3, -1, 1),
+    (1, 4, -3),
+    (2, 0, 3),
+    (2, 0, 2),
+    (2, 3, -3),
+    (2, 3, 3),
+    (1, 4, 2),
+    (1, 4, 1),
+    (2, 4, 0),
+    (2, 3, 2),
+    (6, -1, 0),
+    (2, 3, 1),
+    (6, -1, 1),
+    (1, 4, 3),
+    (2, 3, -2),
+    (7, -1, 0),
+    (3, -1, 2),
+    (8, -1, 0),
+    (1, 0, 1),
+    (2, 4, -1),
+    (2, 4, 1),
+    (8, -1, 1),
+    (2, 4, 2),
+    (2, 4, -2),
+    (2, 4, -3),
+    (8, -1, 2),
+    (2, 4, 3),
+    (1, 0, -1),
+    (2, 0, 1),
+    (3, -1, 3),
+    (2, 0, -1),
+    (9, -1, 0),
+    (9, -1, 1),
+    (10, -1, 0),
 )
 
 
@@ -257,20 +303,24 @@
         self.at, self.k, self.shard, self.own, self.sib = at, k, shard, own, sib
         self.recv, self.core, self.line, self.pair, self.over, self.local = sems
 
+    def block(self, ref, j):
+        rows = self.shard.shape[0]
+        return ref.at[pl.ds(pl.multiple_of(j * rows, 8), rows)]
+
     def send(self, src, j, sem, i):
-        return remote(src, self.own.at[j], sem, self.recv.at[self.k, j], i, self.at.c)
+        return remote(src, self.block(self.own, j), sem, self.recv.at[self.k, j], i, self.at.c)
 
     def across(self, src, j):
         at, k = self.at, self.k
         return remote(
-            src, self.sib.at[j], self.over.at[k, j], self.core.at[k, j], at.i, 1 - at.c
+            src, self.block(self.sib, j), self.over.at[k, j], self.core.at[k, j], at.i, 1 - at.c
         )
 
     def arrived(self, j):
         at = self.at
         remote(
-            self.own.at[j],
-            self.own.at[j],
+            self.block(self.own, j),
+            self.block(self.own, j),
             self.over.at[self.k, j],
             self.recv.at[self.k, j],
             at.i,
@@ -303,7 +353,7 @@
     def column_copies(self, off, level):
         at, k = self.at, self.k
         first, second, j = self.pieces(level)
-        src = self.shard if off == 0 else self.own.at[j]
+        src = self.shard if off == 0 else self.block(self.own, j)
         lines = self.line_copies(off, level, 0, src, j)
         near = [self.send(src, j, self.pair.at[k, level, 0], at.i + first)]
         rest = [self.send(src, j, self.pair.at[k, level, 1], at.i + second), self.across(src, j)]
@@ -329,13 +379,13 @@
 
     def keep(self):
         return pltpu.make_async_copy(
-            self.shard, self.own.at[self.at.i], self.local.at[self.k]
+            self.shard, self.block(self.own, self.at.i), self.local.at[self.k]
         )
 
     def relay_copies(self, off, level):
         first, second, column = self.pieces(level)
         j = column + first
-        src = self.own.at[j]
+        src = self.block(self.own, j)
         lines = self.line_copies(off, level, 1, src, j) if self.mid else []
         return lines, [
             self.send(src, j, self.pair.at[self.k, level, 2], self.at.i + second),
@@ -356,7 +406,7 @@
 
     def last_copies(self, level):
         first, second, column = self.pieces(level)
-        return [(j, self.across(self.own.at[j], j)) for j in (column + second, column + first + second)]
+        return [(j, self.across(self.block(self.own, j), j)) for j in (column + second, column + first + second)]
 
     def last(self, off):
         def run(level):
@@ -366,9 +416,15 @@
 
         self.guard(off, run)
 
+    def complete(self):
+        self.keep().wait()
+
+        @pl.loop(0, 16)
+        def _(j):
+            self.across(self.block(self.sib, j), j).wait_recv()
+
     def finish(self):
         at = self.at
-        self.keep().wait()
         for off in OFFSETS:
 
             def run(level, off=off):
@@ -383,10 +439,6 @@
 
             self.guard(off, run)
 
-        @pl.loop(0, 16)
-        def _(j):
-            self.across(self.sib.at[j], j).wait_recv()
-
     def events(self, start, span):
         out = []
         for off in OFFSETS:
@@ -397,35 +449,293 @@
         return out
 
 
+def spread_rows(rows):
+    def over(step):
+        @pl.loop(0, rows // 32)
+        def _(part):
+            step(pl.ds(pl.multiple_of(part * 32, 32), 32))
+
+    return over
+
+
+def flip(source, out):
+    @pl.loop(0, source.shape[-1] // 128)
+    def _(t):
+        part = pl.ds(pl.multiple_of(t * 128, 128), 128)
+        out[part, :] = source[:, part].astype(jnp.float32).T.astype(jnp.bfloat16)
+
+
+def by_tiles(left, right, emit):
+    width = right.shape[-1]
+
+    @pl.loop(0, width // TILE)
+    def _(t):
+        columns = pl.ds(pl.multiple_of(t * TILE, TILE), TILE)
+        emit(columns, jnp.dot(left[...], right[:, columns], preferred_element_type=jnp.float32))
+
+    if width % TILE:
+        columns = pl.ds(width // TILE * TILE, width % TILE)
+        emit(columns, jnp.dot(left[...], right[:, columns], preferred_element_type=jnp.float32))
+
+
+class Forward:
+    def __init__(self, at, ins, outs, scratch, jobs):
+        self.at, self.jobs = at, jobs
+        (
+            self.tokens,
+            self.silu,
+            self.w_ada,
+            self.b_ada,
+            self.valid,
+            self.b_qkv,
+            self.b_proj,
+            self.b_fc1,
+            self.b_fc2,
+        ) = ins
+        (
+            self.modul,
+            self.attn_in_t,
+            self.qkv,
+            self.lse,
+            self.attended_t,
+            self.attn_out,
+            self.middle,
+            self.mlp_in_t,
+            self.hidden,
+            self.active_t,
+            self.branch,
+            self.result,
+        ) = outs
+        self.ada, self.loose = scratch[:2]
+        self.weights = dict(zip(WEIGHTS, scratch[2:6]))
+        self.attn_in, self.attended, self.mlp_in, self.active = scratch[6:10]
+        self.ada_sem, self.load_sem = scratch[10:]
+
+    def ada_copy(self, part):
+        slot = part % 2
+        rows = pl.ds(pl.multiple_of(part * D, D), D)
+        return pltpu.make_async_copy(
+            self.w_ada.at[rows], self.ada.at[slot], self.ada_sem.at[slot]
+        )
+
+    def start(self, _):
+        self.ada_copy(0).start()
+        self.lse[...] = jnp.zeros(self.lse.shape, jnp.float32)
+        self.attended[...] = jnp.zeros(self.attended.shape, jnp.bfloat16)
+
+    def mod(self, half):
+        @pl.loop(half * 3, half * 3 + 3)
+        def _(part):
+            pl.when(part < 5)(lambda: self.ada_copy(part + 1).start())
+            self.ada_copy(part).wait()
+            value = lax.dot_general(
+                self.silu[...],
+                self.ada[part % 2],
+                LAST_DIMS,
+                preferred_element_type=jnp.float32,
+            )
+            self.modul[part] = value[:8] + self.b_ada[part]
+
+    def piece(self, index):
+        return self.modul[index, 0:1, :]
+
+    def ln(self, _):
+        @spread_rows(SEQ)
+        def _(rows):
+            normed, _ = norm_rows(self.tokens[rows, :].astype(jnp.float32))
+            self.attn_in[rows, :] = (normed * (1.0 + self.piece(1)) + self.piece(0)).astype(
+                jnp.bfloat16
+            )
+
+        flip(self.attn_in, self.attn_in_t)
+
+    def load_copies(self, name):
+        k = WEIGHTS.index(name)
+        job, held, c = self.jobs[k + 1], self.weights[name], self.at.c
+        return [
+            pltpu.make_async_copy(job.own, held.at[c], self.load_sem.at[k, 0]),
+            pltpu.make_async_copy(job.sib, held.at[1 - c], self.load_sem.at[k, 1]),
+        ]
+
+    def load(self, k):
+        name = WEIGHTS[k]
+        self.jobs[k + 1].complete()
+        for copy in self.load_copies(name):
+            copy.start()
+
+    def loaded(self, name):
+        for copy in self.load_copies(name):
+            copy.wait()
+
+    def loosely(self, columns, value):
+        self.loose[:, columns] = value
+
+    def merge(self, out, bias, start):
+        width = out.shape[-1] - start
+
+        @spread_rows(SEQ)
+        def _(rows):
+            value = pltpu.roll(self.loose[rows, :width], 64, 1) + bias[0:1, start:]
+            before = out[rows, start : start + 128].astype(jnp.float32)
+            lane = lax.broadcasted_iota(jnp.int32, before.shape, 1)
+            seam = jnp.where(lane < 64, before, value[:, :128])
+            out[rows, start : start + 128] = seam.astype(out.dtype)
+            out[rows, start + 128 :] = value[:, 128:].astype(out.dtype)
+
+    def product(self, left, name, half, out, bias):
+        if half == 0:
+            self.loaded(name)
+
+            def emit(columns, value):
+                out[:, columns] = (value + bias[0:1, columns]).astype(out.dtype)
+
+            by_tiles(left, self.weights[name].at[0], emit)
+        else:
+            by_tiles(left, self.weights[name].at[1], self.loosely)
+            self.merge(out, bias, out.shape[-1] // 256 * 128)
+
+    def query(self, half):
+        self.product(self.attn_in, "qkv", half, self.qkv, self.b_qkv)
+
+    def attend(self, part):
+        @pl.loop(part * 4, part * 4 + 4)
+        def _(head):
+            begin = head * HD
+            tile = begin // 128
+            tile = tile - tile // 8
+            first = pl.multiple_of(tile * 128, 128)
+            window = pl.ds(first, 256)
+            lane = lax.broadcasted_iota(jnp.int32, (SEQ, 256), 1) + tile * 128
+            inside = (lane >= begin) & (lane < begin + HD)
+            query = jnp.where(inside, self.qkv[:, window].astype(jnp.float32), 0.0)
+            keys = self.qkv[:, pl.ds(pl.multiple_of(D + tile * 128, 128), 256)]
+            values = self.qkv[:, pl.ds(pl.multiple_of(2 * D + tile * 128, 128), 256)]
+            scores = lax.dot_general(
+                query.astype(jnp.bfloat16), keys, LAST_DIMS, preferred_element_type=jnp.float32
+            ) * HD ** (-0.5)
+            scores = jnp.where(self.valid[0:1, :] > 0.5, scores, NEG_FILL)
+            row_max = jnp.max(scores, axis=1, keepdims=True)
+            exponent = jnp.exp(scores - row_max)
+            row_total = jnp.sum(exponent, axis=1, keepdims=True)
+            probs = (exponent / row_total).astype(jnp.bfloat16)
+            value = jnp.dot(probs, values, preferred_element_type=jnp.float32)
+            before = self.attended[:, window].astype(jnp.float32)
+            self.attended[:, window] = jnp.where(inside, value, before).astype(jnp.bfloat16)
+            column = lax.broadcasted_iota(jnp.int32, (SEQ, 128), 1)
+            self.lse[...] = jnp.where(
+                column == head, row_max + jnp.log(row_total), self.lse[...]
+            )
+
+    def project(self, half):
+        self.product(self.attended, "proj", half, self.attn_out, self.b_proj)
+        if half:
+            flip(self.attended, self.attended_t)
+
+    def mid(self, _):
+        @spread_rows(SEQ)
+        def _(rows):
+            middle = (
+                self.tokens[rows, :].astype(jnp.float32) + self.piece(2) * self.attn_out[rows, :]
+            )
+            self.middle[rows, :] = middle
+            normed, _ = norm_rows(middle)
+            self.mlp_in[rows, :] = (normed * (1.0 + self.piece(4)) + self.piece(3)).astype(
+                jnp.bfloat16
+            )
+
+        flip(self.mlp_in, self.mlp_in_t)
+
+    def widen(self, part):
+        if part == 0:
+            self.loaded("fc1")
+        weight = self.weights["fc1"]
+
+        @pl.loop(part * 6, part * 6 + 6)
+        def _(t):
+            columns = pl.ds(pl.multiple_of(t * TILE, TILE), TILE)
+            within = pl.ds(pl.multiple_of(t % 9 * TILE, TILE), TILE)
+            hidden = (
+                jnp.dot(
+                    self.mlp_in[...],
+                    weight[t // 9, :, within],
+                    preferred_element_type=jnp.float32,
+                )
+                + self.b_fc1[0:1, columns]
+            )
+            self.hidden[:, columns] = hidden
+            active = gelu_tanh(hidden)
+            self.active[:, columns] = active.astype(jnp.bfloat16)
+            self.active_t[columns, :] = active.T.astype(jnp.bfloat16)
+
+    def narrow(self, half):
+        self.product(self.active, "fc2", half, self.branch, self.b_fc2)
+
+    def last(self, _):
+        @spread_rows(SEQ)
+        def _(rows):
+            self.result[rows, :] = (
+                self.middle[rows, :] + self.piece(5) * self.branch[rows, :]
+            ).astype(jnp.bfloat16)
+
+
 def gather_kernel(count, *refs):
-    shards, own, sib = refs[:count], refs[count : 2 * count], refs[2 * count : 3 * count]
-    sems = refs[3 * count :]
+    refs = list(refs)
+
+    def take(n):
+        out = refs[:n]
+        del refs[:n]
+        return out
+
+    shards, ins = take(count), take(9)
+    own, sib, outs = take(count), take(count), take(12)
+    sems, scratch = take(6), take(12)
     at = Place()
     at.greet()
     jobs = [
         Gather(at, k, shards[k], own[k], sib[k], sems, k in GATHER_MID) for k in range(count)
     ]
+    forward = Forward(at, ins, outs, scratch, jobs)
     for step, k, off in GATHER_ORDER:
-        getattr(jobs[k], step)(off)
+        getattr(forward if k < 0 else jobs[k], (TASKS if k < 0 else STEPS)[step])(off)
+    jobs[0].complete()
     for job in jobs:
         job.finish()
 
 
-def gather_all(shards):
+def gather_all(shards, ins):
     count = len(shards)
-    spread = [jax.ShapeDtypeStruct((16,) + s.shape, s.dtype) for s in shards]
+    spread = [jax.ShapeDtypeStruct((16 * s.shape[0], s.shape[1]), s.dtype) for s in shards]
+    kinds = [
+        ((6, 8, D), jnp.float32),
+        ((D, SEQ), jnp.bfloat16),
+        ((SEQ, 3 * D), jnp.bfloat16),
+        ((SEQ, 128), jnp.float32),
+        ((D, SEQ), jnp.bfloat16),
+        ((SEQ, D), jnp.float32),
+        ((SEQ, D), jnp.float32),
+        ((D, SEQ), jnp.bfloat16),
+        ((SEQ, 4 * D), jnp.float32),
+        ((4 * D, SEQ), jnp.bfloat16),
+        ((SEQ, D), jnp.float32),
+        ((SEQ, D), jnp.bfloat16),
+    ]
+    dma = pltpu.SemaphoreType.DMA
     outs = pl.pallas_call(
         functools.partial(gather_kernel, count),
-        out_shape=spread + spread,
-        in_specs=[VMEM] * count,
-        out_specs=[ANY] * (2 * count),
-        scratch_shapes=gather_sems(count),
+        out_shape=spread + spread + [jax.ShapeDtypeStruct(*kind) for kind in kinds],
+        in_specs=[VMEM] * count + [VMEM, VMEM, ANY] + [VMEM] * 6,
+        out_specs=[ANY] * (2 * count) + [VMEM] * len(kinds),
+        scratch_shapes=gather_sems(count)
+        + [pltpu.VMEM((2, D, D), jnp.bfloat16), pltpu.VMEM((SEQ, 1792), jnp.float32)]
+        + [pltpu.VMEM((2,) + s.shape, s.dtype) for s in spread[1:]]
+        + [pltpu.VMEM((SEQ, width), jnp.bfloat16) for width in (D, D, D, 4 * D)]
+        + [dma((2,)), dma((4, 2))],
         compiler_params=pltpu.CompilerParams(
-            collective_id=0, has_side_effects=True, vmem_limit_bytes=16_000_000
+            collective_id=0, has_side_effects=True, vmem_limit_bytes=VMEM_LIMIT
         ),
         name="gather_all",
-    )(*shards)
-    return outs[:count], outs[count:]
+    )(*shards, *ins)
+    return outs[:count], outs[count : 2 * count], outs[2 * count :]
 
 
 def blocked(shape):
@@ -443,7 +753,8 @@
 class Scatter:
     def __init__(self, at, k, ins, result, bufs, sems):
         self.at, self.k = at, k
-        self.left, self.right, self.away = ins
+        self.left, halves = ins
+        self.right, self.away = halves.at[at.c], halves.at[1 - at.c]
         self.result = result
         self.left_sib, self.right_sib, self.held, self.near, self.far, self.line = bufs
         self.mid = self.line.shape[2] == 2
@@ -521,10 +832,10 @@
             else:
                 pl.when(self.at.z < ZS - 1)(copy.wait_recv)
 
-    def begin(self):
-        for copy in self.swaps():
-            copy.start()
-
+    def begin(self, part):
+        self.swaps()[part].start()
+
+    def clear(self):
         zeros = jnp.zeros(self.line.shape[3:], self.line.dtype)
 
         @pl.when(self.at.z == 0)
@@ -672,7 +983,236 @@
                     pl.when(beyond)(copy.wait_send)
 
 
-def scatter_kernel(count, *refs):
+def fold(value):
+    rows, cols = value.shape
+    return jnp.sum(value.reshape(rows // 8, 8, cols), axis=0)
+
+
+def halve(out, rows, value):
+    width = out.shape[-1]
+    rest = value[:, width // 128 * 128 :]
+    out[0, rows, :] = value[:, :width].astype(jnp.bfloat16)
+    rest = pltpu.roll(rest, rest.shape[-1] - 64, 1)
+    out[1, rows, :] = rest[:, :width].astype(jnp.bfloat16)
+
+
+class Backward:
+    def __init__(self, at, ins, outs, scratch, jobs):
+        self.at, self.jobs = at, jobs
+        (
+            self.modul,
+            self.weight,
+            self.cotangent,
+            self.branch,
+            self.hidden,
+            self.middle,
+            self.attn_out,
+            self.lse,
+            self.qkv,
+            self.valid,
+            self.tokens,
+        ) = ins[:11]
+        self.own, self.sib = ins[11:15], ins[15:19]
+        self.d_attn, self.d_split, self.grad_tokens, self.sums, self.sums_fc1 = outs
+        (
+            self.d_branch,
+            self.d_hidden,
+            self.flow,
+            self.d_middle,
+            self.d_attended,
+            self.d_qkv,
+            self.slim,
+            self.wide,
+            self.long,
+            self.slim_sem,
+            self.wide_sem,
+            self.long_sem,
+        ) = scratch
+
+    def piece(self, index):
+        return self.modul[index, 0:1, :]
+
+    def fetches(self, k, t):
+        if k in (1, 3):
+            buffer, sem = self.slim.at[t % 2], self.slim_sem.at[t % 2]
+        else:
+            buffer, sem = (self.long, self.long_sem) if k == 0 else (self.wide, self.wide_sem)
+        rows = pl.ds(pl.multiple_of(t * 384, 384), 384)
+        return [
+            pltpu.make_async_copy(self.own[k].at[rows], buffer.at[self.at.c], sem.at[0]),
+            pltpu.make_async_copy(self.sib[k].at[rows], buffer.at[1 - self.at.c], sem.at[1]),
+        ]
+
+    def fetch(self, k, t):
+        for copy in self.fetches(k, t):
+            copy.start()
+
+    def fetched(self, k, t):
+        for copy in self.fetches(k, t):
+            copy.wait()
+
+    def back(self, halves, buffer):
+        return lax.dot_general(
+            halves[0], buffer[0], LAST_DIMS, preferred_element_type=jnp.float32
+        ) + lax.dot_general(halves[1], buffer[1], LAST_DIMS, preferred_element_type=jnp.float32)
+
+    def seed(self, _):
+        self.fetch(3, 0)
+        self.fetch(2, 0)
+        self.fetch(0, 0)
+        self.sums[...] = jnp.zeros(self.sums.shape, jnp.float32)
+        self.d_qkv[...] = jnp.zeros(self.d_qkv.shape, jnp.bfloat16)
+
+        @spread_rows(SEQ)
+        def _(rows):
+            grad = self.cotangent[rows, :].astype(jnp.float32) * self.weight[rows, 0:1]
+            d_branch = (self.piece(5) * grad).astype(jnp.bfloat16).astype(jnp.float32)
+            self.sums[5] += fold(grad * self.branch[rows, :])
+            self.sums[9] += fold(d_branch)
+            halve(self.d_branch, rows, d_branch)
+
+        self.jobs[0].begin(1)
+
+    def widen(self, part):
+        @pl.loop(part * 4, part * 4 + 4)
+        def _(t):
+            pl.when(t < 11)(lambda: self.fetch(3, t + 1))
+            self.fetched(3, t)
+            columns = pl.ds(pl.multiple_of(t * 384, 384), 384)
+            within = pl.ds(pl.multiple_of(t % 6 * 384, 384), 384)
+            d_active = self.back(self.d_branch, self.slim.at[t % 2])
+            pull = jax.vjp(gelu_tanh, self.hidden[:, columns])[1]
+            d_hidden = pull(d_active)[0].astype(jnp.bfloat16)
+            self.d_hidden[t // 6, :, within] = d_hidden
+            self.sums_fc1[:, columns] = fold(d_hidden.astype(jnp.float32))
+
+        if part == 2:
+            self.jobs[1].begin(1)
+            self.fetch(1, 0)
+
+    def mix(self, _):
+        @pl.loop(0, 3)
+        def _(t):
+            self.fetched(2, t)
+            columns = pl.ds(pl.multiple_of(t * 384, 384), 384)
+            self.flow[:, columns] = self.back(self.d_hidden, self.wide)
+            pl.when(t < 2)(lambda: self.fetch(2, t + 1))
+
+    def centre(self, _):
+        @spread_rows(SEQ)
+        def _(rows):
+            grad = self.cotangent[rows, :].astype(jnp.float32) * self.weight[rows, 0:1]
+            normed, inverse = norm_rows(self.middle[rows, :])
+            d_mlp = self.flow[rows, :]
+            self.sums[3] += fold(d_mlp)
+            self.sums[4] += fold(d_mlp * normed)
+            d_middle = grad + norm_back(d_mlp * (1.0 + self.piece(4)), normed, inverse)
+            self.d_middle[rows, :] = d_middle
+            self.sums[2] += fold(d_middle * self.attn_out[rows, :])
+            d_attn = (self.piece(2) * d_middle).astype(jnp.bfloat16).astype(jnp.float32)
+            self.sums[8] += fold(d_attn)
+            halve(self.d_attn, rows, d_attn)
+
+    def project(self, _):
+        @pl.loop(0, 3)
+        def _(t):
+            pl.when(t < 2)(lambda: self.fetch(1, t + 1))
+            self.fetched(1, t)
+            columns = pl.ds(pl.multiple_of(t * 384, 384), 384)
+            self.d_attended[:, columns] = self.back(self.d_attn, self.slim.at[t % 2]).astype(
+                jnp.bfloat16
+            )
+
+    def attend(self, part):
+        @pl.loop(part * 4, part * 4 + 4)
+        def _(head):
+            begin = head * HD
+            tile = begin // 128
+            tile = tile - tile // 8
+            spots = [
+                pl.ds(pl.multiple_of(kind * D + tile * 128, 128), 256) for kind in range(3)
+            ]
+            lane = lax.broadcasted_iota(jnp.int32, (SEQ, 256), 1) + tile * 128
+            inside = (lane >= begin) & (lane < begin + HD)
+
+            def only(ref, spot):
+                return jnp.where(inside, ref[:, spot].astype(jnp.float32), 0.0).astype(
+                    jnp.bfloat16
+                )
+
+            query, d_out = only(self.qkv, spots[0]), only(self.d_attended, spots[0])
+            keys, values = self.qkv[:, spots[1]], self.qkv[:, spots[2]]
+            column = lax.broadcasted_iota(jnp.int32, (SEQ, 128), 1)
+            log_total = jnp.sum(
+                jnp.where(column == head, self.lse[...], 0.0), axis=1, keepdims=True
+            )
+            is_valid = self.valid[0:1, :] > 0.5
+            scores = lax.dot_general(
+                query, keys, LAST_DIMS, preferred_element_type=jnp.float32
+            ) * HD ** (-0.5)
+            probs = jnp.exp(jnp.where(is_valid, scores, NEG_FILL) - log_total)
+            d_probs = lax.dot_general(
+                d_out, values, LAST_DIMS, preferred_element_type=jnp.float32
+            )
+            inner = jnp.sum(probs * d_probs, axis=1, keepdims=True)
+            d_scores = jnp.where(is_valid, probs * (d_probs - inner), 0.0).astype(jnp.bfloat16)
+            grads = (
+                jnp.dot(d_scores, keys, preferred_element_type=jnp.float32) * HD ** (-0.5),
+                lax.dot_general(d_scores, query, ROWS_DIMS, preferred_element_type=jnp.float32)
+                * HD ** (-0.5),
+                lax.dot_general(
+                    probs.astype(jnp.bfloat16),
+                    d_out,
+                    ROWS_DIMS,
+                    preferred_element_type=jnp.float32,
+                ),
+            )
+            for spot, grad in zip(spots, grads):
+                before = self.d_qkv[:, spot].astype(jnp.float32)
+                self.d_qkv[:, spot] = jnp.where(inside, grad, before).astype(jnp.bfloat16)
+
+    def part(self, _):
+        @spread_rows(SEQ)
+        def _(rows):
+            value = self.d_qkv[rows, :].astype(jnp.float32)
+            self.sums[6] += fold(value[:, :D])
+            self.sums[7] += fold(value[:, 2 * D :])
+            halve(self.d_split, rows, value)
+
+    def query(self, _):
+        @pl.loop(0, 3)
+        def _(t):
+            self.fetched(0, t)
+            columns = pl.ds(pl.multiple_of(t * 384, 384), 384)
+            self.flow[:, columns] = self.back(self.d_split, self.long)
+            pl.when(t < 2)(lambda: self.fetch(0, t + 1))
+
+    def leave(self, _):
+        @spread_rows(SEQ)
+        def _(rows):
+            normed, inverse = norm_rows(self.tokens[rows, :].astype(jnp.float32))
+            d_in = self.flow[rows, :]
+            self.sums[0] += fold(d_in)
+            self.sums[1] += fold(d_in * normed)
+            self.grad_tokens[rows, :] = (
+                self.d_middle[rows, :] + norm_back(d_in * (1.0 + self.piece(1)), normed, inverse)
+            ).astype(jnp.bfloat16)
+
+
+def scatter_bufs(terms):
+    scratch = []
+    for left, halves, shard, mid in terms:
+        piece = blocked(shard.shape)
+        scratch.append(pltpu.VMEM(left.shape, jnp.bfloat16))
+        scratch.append(pltpu.VMEM((SEQ, shard.shape[1]), jnp.bfloat16))
+        for lead in ((16,), (ZS, 2), (1 if mid else ZS,), (2, ZS, 2 if mid else 1)):
+            scratch.append(pltpu.VMEM(lead + piece, jnp.bfloat16))
+    dma, count = pltpu.SemaphoreType.DMA, len(terms)
+    pairs = ((count, 2), (count, ZS, 2), (count, ZS), (count, 2, ZS, 2))
+    return scratch + [dma(shape) for shape in pairs for _ in range(2)]
+
+
+def back_kernel(*refs):
     refs = list(refs)
 
     def take(n):
@@ -680,7 +1220,81 @@
         del refs[:n]
         return out
 
-    ins = [take(3) for _ in range(count)]
+    lefts, ins = take(2), take(19)
+    results, outs = take(2), take(5)
+    scratch = take(12)
+    bufs = [take(6) for _ in range(2)]
+    sems = take(8)
+    at = Place()
+    at.greet()
+    jobs = [
+        Scatter(at, k, (lefts[k], scratch[k]), results[k], bufs[k], sems) for k in range(2)
+    ]
+    for job in jobs:
+        job.begin(0)
+        job.clear()
+    backward = Backward(at, ins, outs, scratch, jobs)
+    seen = set()
+    for stage, k, part in BACK_ORDER:
+        if k < 0:
+            getattr(backward, BACK_TASKS[stage])(part)
+            continue
+        if k not in seen:
+            jobs[k].ready()
+            seen.add(k)
+        getattr(jobs[k], "stage_" + STAGES[stage])(part)
+    for job in jobs:
+        job.finish()
+
+
+def back_all(lefts, ins, shards):
+    bf16, f32 = jnp.bfloat16, jnp.float32
+    kinds = [
+        ((2, SEQ, D // 2), bf16),
+        ((2, SEQ, 3 * D // 2), bf16),
+        ((SEQ, D), bf16),
+        ((10, 8, D), f32),
+        ((8, 4 * D), f32),
+    ]
+    own = [
+        ((2, SEQ, D // 2), bf16),
+        ((2, SEQ, 2 * D), bf16),
+        ((SEQ, D), f32),
+        ((SEQ, D), f32),
+        ((SEQ, D), bf16),
+        ((SEQ, 3 * D), bf16),
+        ((2, 2, 384, D // 2), bf16),
+        ((2, 384, 2 * D), bf16),
+        ((2, 384, 3 * D // 2), bf16),
+    ]
+    dma = pltpu.SemaphoreType.DMA
+    terms = [(left, None, shard, k in BACK_MID) for k, (left, shard) in enumerate(zip(lefts, shards))]
+    outs = pl.pallas_call(
+        back_kernel,
+        out_shape=[jax.ShapeDtypeStruct(shard.shape, f32) for shard in shards]
+        + [jax.ShapeDtypeStruct(*kind) for kind in kinds],
+        in_specs=[VMEM] * 13 + [ANY] * 8,
+        out_specs=[VMEM] * 7,
+        scratch_shapes=[pltpu.VMEM(*kind) for kind in own]
+        + [dma((2, 2)), dma((2,)), dma((2,))]
+        + scatter_bufs(terms),
+        compiler_params=pltpu.CompilerParams(
+            collective_id=1, has_side_effects=True, vmem_limit_bytes=VMEM_LIMIT
+        ),
+        name="back_all",
+    )(*lefts, *ins)
+    return outs[:2], outs[2:]
+
+
+def scatter_kernel(count, *refs):
+    refs = list(refs)
+
+    def take(n):
+        out = refs[:n]
+        del refs[:n]
+        return out
+
+    ins = [take(2) for _ in range(count)]
     note = take(1)[0]
     results = take(count)
     note_own, note_sib = take(2)
@@ -692,7 +1306,9 @@
     word = Gather(at, 0, note, note_own, note_sib, note_sems)
     whisper = [action for _, action in sorted(word.events(0.0, 1.0), key=lambda item: item[0])]
     for job in jobs:
-        job.begin()
+        job.begin(0)
+        job.begin(1)
+        job.clear()
 
     def speak(n):
         for action in whisper[:n]:
@@ -705,54 +1321,38 @@
         if k not in seen:
             jobs[k].ready()
             seen.add(k)
-        getattr(jobs[k], "stage_" + stage)(part)
-        speak(1)
+        getattr(jobs[k], "stage_" + STAGES[stage])(part)
+        speak(2)
     speak(len(whisper))
     for job in jobs:
         job.finish()
+    word.complete()
     word.finish()
 
 
-def scatter_all(terms, note):
-    count = len(terms)
-    spread = jax.ShapeDtypeStruct((16,) + note.shape, note.dtype)
-    scratch, operands = [], []
-    for left, right, away, shard in terms:
-        operands += [left, right, away]
-        scratch.append(pltpu.VMEM(left.shape, jnp.bfloat16))
-        scratch.append(pltpu.VMEM(right.shape, jnp.bfloat16))
-        mid = shard.shape in MID
-        piece = blocked(shard.shape)
-        for lead in ((16,), (ZS, 2), (1 if mid else ZS,), (2, ZS, 2 if mid else 1)):
-            scratch.append(pltpu.VMEM(lead + piece, jnp.bfloat16))
-    dma = pltpu.SemaphoreType.DMA
-    scratch += [
-        dma((count, 2)),
-        dma((count, 2)),
-        dma((count, ZS, 2)),
-        dma((count, ZS, 2)),
-        dma((count, ZS)),
-        dma((count, ZS)),
-        dma((count, 2, ZS, 2)),
-        dma((count, 2, ZS, 2)),
+def scatter_all(pairs, shards, note):
+    count = len(pairs)
+    spread = jax.ShapeDtypeStruct((16 * note.shape[0], note.shape[1]), note.dtype)
+    terms = [
+        (left, halves, shard, k in MID) for k, ((left, halves), shard) in enumerate(zip(pairs, shards))
     ]
     outs = pl.pallas_call(
         functools.partial(scatter_kernel, count),
-        out_shape=[jax.ShapeDtypeStruct(t[3].shape, jnp.float32) for t in terms]
+        out_shape=[jax.ShapeDtypeStruct(shard.shape, jnp.float32) for shard in shards]
         + [spread, spread],
-        in_specs=[VMEM, VMEM, ANY] * count + [VMEM],
+        in_specs=[VMEM, VMEM] * count + [VMEM],
         out_specs=[VMEM] * count + [ANY, ANY],
-        scratch_shapes=scratch + gather_sems(1),
+        scratch_shapes=scatter_bufs(terms) + gather_sems(1),
         compiler_params=pltpu.CompilerParams(
-            collective_id=1, has_side_effects=True, vmem_limit_bytes=VMEM_LIMIT
+            collective_id=2, has_side_effects=True, vmem_limit_bytes=VMEM_LIMIT
         ),
         name="scatter_all",
-    )(*operands, note)
+    )(*[part for pair in pairs for part in pair], note)
     return outs[:count], outs[count], outs[count + 1]
 
 
 def gather_plain(shards):
-    own = [lax.all_gather(s, "dp", axis=0) for s in shards]
+    own = [lax.all_gather(s, "dp", axis=0, tiled=True) for s in shards]
     pair = [lax.all_gather(g, "fsdp", axis=0) for g in own]
     other = 1 - lax.axis_index("fsdp")
     return own, [lax.dynamic_index_in_dim(p, other, 0, keepdims=False) for p in pair]
@@ -839,13 +1439,29 @@
             jnp.zeros((6, lanes), jnp.float32),
         ]
     )
-    gather = gather_all if fast else gather_plain
-    scatter = scatter_all if fast else scatter_plain
-    own, sib = gather([facts, w_qkv, w_proj, w_fc1, w_fc2])
-    flat = lambda w: w.reshape(-1, w.shape[-1])
-    qkv_own, proj_own, fc1_own, fc2_own = [flat(w) for w in own[1:]]
-    qkv_sib, proj_sib, fc1_sib, fc2_sib = [flat(w) for w in sib[1:]]
-    counts = (jnp.sum(own[0], axis=0) + jnp.sum(sib[0], axis=0))[0, :BINS]
+    shares = [facts, w_qkv, w_proj, w_fc1, w_fc2]
+    bias_qkv = jnp.concatenate([b_query, jnp.zeros_like(b_query), b_value])
+    if fast:
+        row = lambda vector: vector.reshape(1, -1)
+        ins = [
+            tokens.reshape(SEQ, D),
+            jnp.broadcast_to(silu_cond, (16, D)),
+            w_ada,
+            jnp.broadcast_to(b_ada.reshape(6, 1, D), (6, 8, D)),
+            jnp.broadcast_to(valid_keys.astype(jnp.float32), (8, SEQ)),
+            row(bias_qkv),
+            row(b_proj),
+            row(b_fc1),
+            row(b_fc2),
+        ]
+        own, sib, outs = gather_all(shares, ins)
+    else:
+        own, sib = gather_plain(shares)
+        outs = None
+    qkv_own, proj_own, fc1_own, fc2_own = own[1:]
+    qkv_sib, proj_sib, fc1_sib, fc2_sib = sib[1:]
+    own_facts, sib_facts = own[0].reshape(-1, 16, lanes), sib[0].reshape(-1, 16, lanes)
+    counts = (jnp.sum(own_facts, axis=0) + jnp.sum(sib_facts, axis=0))[0, :BINS]
     bin_scale = bin_weights.astype(jnp.float32) * (jnp.sum(counts) / BINS) / counts
     image_scale = jnp.sum(bin_table * bin_scale[None, :], axis=1)
 
@@ -855,112 +1471,134 @@
     def times_t(left, right):
         return lax.dot_general(left, right, LAST_DIMS, preferred_element_type=jnp.float32)
 
-    modul = lax.dot_general(silu_cond, w_ada, LAST_DIMS, preferred_element_type=jnp.float32) + b_ada
-    pieces = [modul[:, None, part_index * D : (part_index + 1) * D] for part_index in range(6)]
-    shift_one, scale_one, gate_one, shift_two, scale_two, gate_two = pieces
-    token_float = tokens.astype(jnp.float32)
-    normed_one, inverse_one = norm_rows(token_float)
-    attn_in = (
-        (normed_one * (1.0 + scale_one) + shift_one).astype(jnp.bfloat16).reshape(row_count, D)
-    )
-    bias_qkv = jnp.concatenate([b_query, jnp.zeros_like(b_query), b_value])
-    qkv_all = (join(times(attn_in, qkv_own), times(attn_in, qkv_sib)) + bias_qkv).astype(
-        jnp.bfloat16
-    )
-    qkv_heads = qkv_all.reshape(images, SEQ, 3, H, HD)
-    query, keys, values = (qkv_heads[:, :, 0], qkv_heads[:, :, 1], qkv_heads[:, :, 2])
-    scores = masked_scores(query, keys, valid_keys)
-    row_max = jnp.max(scores, axis=-1, keepdims=True)
-    exponent = jnp.exp(scores - row_max)
-    row_total = jnp.sum(exponent, axis=-1, keepdims=True)
-    soft_probs = exponent / row_total
-    log_total = row_max + jnp.log(row_total)
-    attended = jnp.einsum(
-        "bhlm,bmhc->blhc",
-        soft_probs.astype(jnp.bfloat16),
-        values,
-        preferred_element_type=jnp.float32,
-    )
-    attended = attended.astype(jnp.bfloat16).reshape(row_count, D)
-    attn_out = (join(times(attended, proj_own), times(attended, proj_sib)) + b_proj).reshape(
-        images, SEQ, D
-    )
-    middle = token_float + gate_one * attn_out
-    normed_two, inverse_two = norm_rows(middle)
-    mlp_in = (normed_two * (1.0 + scale_two) + shift_two).astype(jnp.bfloat16).reshape(row_count, D)
-    bias_own, bias_sib = split(b_fc1)
-    hidden_own = times(mlp_in, fc1_own) + bias_own
-    hidden_sib = times(mlp_in, fc1_sib) + bias_sib
-    active = join(
-        gelu_tanh(hidden_own).astype(jnp.bfloat16), gelu_tanh(hidden_sib).astype(jnp.bfloat16)
-    )
-    branch = (join(times(active, fc2_own), times(active, fc2_sib)) + b_fc2).reshape(
-        images, SEQ, D
-    )
-    result = (middle + gate_two * branch).astype(jnp.bfloat16)
-    grad_out = (
-        cotangent.astype(jnp.float32)
-        * (valid_keys.astype(jnp.float32) * image_scale[:, None])[:, :, None]
-    )
-    d_gate_two = jnp.sum(grad_out * branch, axis=1)
-    d_branch = (gate_two * grad_out).astype(jnp.bfloat16).reshape(row_count, D)
-    d_branch_own, d_branch_sib = split(d_branch)
-    bias_fc2 = jnp.sum(d_branch, axis=0, dtype=jnp.float32)
-    d_active = times_t(d_branch_own, fc2_own) + times_t(d_branch_sib, fc2_sib)
-    d_active_own, d_active_sib = split(d_active)
-    d_hidden_own = jax.vjp(gelu_tanh, hidden_own)[1](d_active_own)[0].astype(jnp.bfloat16)
-    d_hidden_sib = jax.vjp(gelu_tanh, hidden_sib)[1](d_active_sib)[0].astype(jnp.bfloat16)
-    bias_fc1 = join(
-        jnp.sum(d_hidden_own, axis=0, dtype=jnp.float32),
-        jnp.sum(d_hidden_sib, axis=0, dtype=jnp.float32),
-    )
-    d_mlp_in = (times_t(d_hidden_own, fc1_own) + times_t(d_hidden_sib, fc1_sib)).reshape(
-        images, SEQ, D
-    )
-    d_shift_two = jnp.sum(d_mlp_in, axis=1)
-    d_scale_two = jnp.sum(d_mlp_in * normed_two, axis=1)
-    d_middle = grad_out + norm_back(d_mlp_in * (1.0 + scale_two), normed_two, inverse_two)
-    d_gate_one = jnp.sum(d_middle * attn_out, axis=1)
-    d_attn = (gate_one * d_middle).astype(jnp.bfloat16).reshape(row_count, D)
-    d_attn_own, d_attn_sib = split(d_attn)
-    bias_proj = jnp.sum(d_attn, axis=0, dtype=jnp.float32)
-    d_attended = times_t(d_attn_own, proj_own) + times_t(d_attn_sib, proj_sib)
-    d_attended = d_attended.astype(jnp.bfloat16).reshape(images, SEQ, H, HD)
-    soft_again = jnp.exp(masked_scores(query, keys, valid_keys) - log_total)
-    grad_values = jnp.einsum(
-        "bhlm,blhc->bmhc",
-        soft_again.astype(jnp.bfloat16),
-        d_attended,
-        preferred_element_type=jnp.float32,
-    )
-    d_probs = jnp.einsum("blhc,bmhc->bhlm", d_attended, values, preferred_element_type=jnp.float32)
-    d_scores = soft_again * (d_probs - jnp.sum(soft_again * d_probs, axis=-1, keepdims=True))
-    d_scores = jnp.where(valid_keys[:, None, None, :], d_scores, 0.0).astype(jnp.bfloat16)
-    grad_query = jnp.einsum(
-        "bhlm,bmhc->blhc", d_scores, keys, preferred_element_type=jnp.float32
-    ) * HD ** (-0.5)
-    grad_keys = jnp.einsum(
-        "bhlm,blhc->bmhc", d_scores, query, preferred_element_type=jnp.float32
-    ) * HD ** (-0.5)
-    d_qkv = (
-        jnp.stack([grad_query, grad_keys, grad_values], axis=2)
-        .astype(jnp.bfloat16)
-        .reshape(row_count, 3 * D)
-    )
-    d_qkv_own, d_qkv_sib = split(d_qkv)
-    bias_query = jnp.sum(d_qkv[:, :D], axis=0, dtype=jnp.float32)
-    bias_value = jnp.sum(d_qkv[:, 2 * D :], axis=0, dtype=jnp.float32)
-    d_attn_in = (times_t(d_qkv_own, qkv_own) + times_t(d_qkv_sib, qkv_sib)).reshape(
-        images, SEQ, D
-    )
-    d_shift_one = jnp.sum(d_attn_in, axis=1)
-    d_scale_one = jnp.sum(d_attn_in * normed_one, axis=1)
-    grad_tokens = (
-        d_middle + norm_back(d_attn_in * (1.0 + scale_one), normed_one, inverse_one)
-    ).astype(jnp.bfloat16)
-    d_modul = jnp.concatenate(
-        [d_shift_one, d_scale_one, d_gate_one, d_shift_two, d_scale_two, d_gate_two], axis=1
-    ).astype(jnp.bfloat16)
+    if fast:
+        modul, attn_in_t, qkv_all, lse, attended_t, attn_out, middle = outs[:7]
+        mlp_in_t, hidden, active_t, branch, result = outs[7:]
+        weight = valid_keys.astype(jnp.float32) * image_scale[:, None]
+        ins_back = [
+            modul,
+            jnp.broadcast_to(weight.reshape(SEQ, 1), (SEQ, lanes)),
+            cotangent.reshape(SEQ, D),
+            branch,
+            hidden,
+            middle,
+            attn_out,
+            lse,
+            qkv_all,
+            ins[4],
+            tokens.reshape(SEQ, D),
+        ]
+        (grad_fc2, grad_fc1), outs = back_all(
+            [active_t, mlp_in_t], ins_back + list(own[1:]) + list(sib[1:]), [w_fc2, w_fc1]
+        )
+        d_attn, d_split, grad_tokens, sums, sums_fc1 = outs
+        sums = jnp.sum(sums, axis=1)
+        bias_query, bias_value, bias_proj, bias_fc2 = sums[6], sums[7], sums[8], sums[9]
+        bias_fc1 = jnp.sum(sums_fc1, axis=0)
+        d_modul = sums[:6].reshape(1, 6 * D).astype(jnp.bfloat16)
+        result, grad_tokens = result.reshape(tokens.shape), grad_tokens.reshape(tokens.shape)
+    else:
+        token_float = tokens.astype(jnp.float32)
+        normed_one, inverse_one = norm_rows(token_float)
+        modul = (
+            lax.dot_general(silu_cond, w_ada, LAST_DIMS, preferred_element_type=jnp.float32) + b_ada
+        )
+        pieces = [modul[:, None, part_index * D : (part_index + 1) * D] for part_index in range(6)]
+        shift_one, scale_one, gate_one, shift_two, scale_two, gate_two = pieces
+        attn_in = (
+            (normed_one * (1.0 + scale_one) + shift_one).astype(jnp.bfloat16).reshape(row_count, D)
+        )
+        qkv_all = (join(times(attn_in, qkv_own), times(attn_in, qkv_sib)) + bias_qkv).astype(
+            jnp.bfloat16
+        )
+        qkv_heads = qkv_all.reshape(images, SEQ, 3, H, HD)
+        query, keys, values = (qkv_heads[:, :, 0], qkv_heads[:, :, 1], qkv_heads[:, :, 2])
+        scores = masked_scores(query, keys, valid_keys)
+        row_max = jnp.max(scores, axis=-1, keepdims=True)
+        exponent = jnp.exp(scores - row_max)
+        row_total = jnp.sum(exponent, axis=-1, keepdims=True)
+        soft_probs = exponent / row_total
+        log_total = row_max + jnp.log(row_total)
+        attended = jnp.einsum(
+            "bhlm,bmhc->blhc",
+            soft_probs.astype(jnp.bfloat16),
+            values,
+            preferred_element_type=jnp.float32,
+        )
+        attended = attended.astype(jnp.bfloat16).reshape(row_count, D)
+        attn_out = (join(times(attended, proj_own), times(attended, proj_sib)) + b_proj).reshape(
+            images, SEQ, D
+        )
+        middle = token_float + gate_one * attn_out
+        normed_two, inverse_two = norm_rows(middle)
+        mlp_in = (
+            (normed_two * (1.0 + scale_two) + shift_two).astype(jnp.bfloat16).reshape(row_count, D)
+        )
+        hidden = join(times(mlp_in, fc1_own), times(mlp_in, fc1_sib)) + b_fc1
+        active = gelu_tanh(hidden).astype(jnp.bfloat16)
+        branch = (join(times(active, fc2_own), times(active, fc2_sib)) + b_fc2).reshape(
+            images, SEQ, D
+        )
+        result = (middle + gate_two * branch).astype(jnp.bfloat16)
+        grad_out = (
+            cotangent.astype(jnp.float32)
+            * (valid_keys.astype(jnp.float32) * image_scale[:, None])[:, :, None]
+        )
+        d_gate_two = jnp.sum(grad_out * branch, axis=1)
+        d_branch = (gate_two * grad_out).astype(jnp.bfloat16).reshape(row_count, D)
+        d_branch_own, d_branch_sib = split(d_branch)
+        bias_fc2 = jnp.sum(d_branch, axis=0, dtype=jnp.float32)
+        d_active = times_t(d_branch_own, fc2_own) + times_t(d_branch_sib, fc2_sib)
+        d_hidden = jax.vjp(gelu_tanh, hidden)[1](d_active)[0].astype(jnp.bfloat16)
+        d_hidden_own, d_hidden_sib = split(d_hidden)
+        bias_fc1 = jnp.sum(d_hidden, axis=0, dtype=jnp.float32)
+        d_mlp_in = (times_t(d_hidden_own, fc1_own) + times_t(d_hidden_sib, fc1_sib)).reshape(
+            images, SEQ, D
+        )
+        d_shift_two = jnp.sum(d_mlp_in, axis=1)
+        d_scale_two = jnp.sum(d_mlp_in * normed_two, axis=1)
+        d_middle = grad_out + norm_back(d_mlp_in * (1.0 + scale_two), normed_two, inverse_two)
+        d_gate_one = jnp.sum(d_middle * attn_out, axis=1)
+        d_attn = (gate_one * d_middle).astype(jnp.bfloat16).reshape(row_count, D)
+        d_attn_own, d_attn_sib = split(d_attn)
+        bias_proj = jnp.sum(d_attn, axis=0, dtype=jnp.float32)
+        d_attended = times_t(d_attn_own, proj_own) + times_t(d_attn_sib, proj_sib)
+        d_attended = d_attended.astype(jnp.bfloat16).reshape(images, SEQ, H, HD)
+        soft_again = jnp.exp(masked_scores(query, keys, valid_keys) - log_total)
+        grad_values = jnp.einsum(
+            "bhlm,blhc->bmhc",
+            soft_again.astype(jnp.bfloat16),
+            d_attended,
+            preferred_element_type=jnp.float32,
+        )
+        d_probs = jnp.einsum("blhc,bmhc->bhlm", d_attended, values, preferred_element_type=jnp.float32)
+        d_scores = soft_again * (d_probs - jnp.sum(soft_again * d_probs, axis=-1, keepdims=True))
+        d_scores = jnp.where(valid_keys[:, None, None, :], d_scores, 0.0).astype(jnp.bfloat16)
+        grad_query = jnp.einsum(
+            "bhlm,bmhc->blhc", d_scores, keys, preferred_element_type=jnp.float32
+        ) * HD ** (-0.5)
+        grad_keys = jnp.einsum(
+            "bhlm,blhc->bmhc", d_scores, query, preferred_element_type=jnp.float32
+        ) * HD ** (-0.5)
+        d_qkv = (
+            jnp.stack([grad_query, grad_keys, grad_values], axis=2)
+            .astype(jnp.bfloat16)
+            .reshape(row_count, 3 * D)
+        )
+        d_qkv_own, d_qkv_sib = split(d_qkv)
+        bias_query = jnp.sum(d_qkv[:, :D], axis=0, dtype=jnp.float32)
+        bias_value = jnp.sum(d_qkv[:, 2 * D :], axis=0, dtype=jnp.float32)
+        d_attn_in = (times_t(d_qkv_own, qkv_own) + times_t(d_qkv_sib, qkv_sib)).reshape(
+            images, SEQ, D
+        )
+        d_shift_one = jnp.sum(d_attn_in, axis=1)
+        d_scale_one = jnp.sum(d_attn_in * normed_one, axis=1)
+        grad_tokens = (
+            d_middle + norm_back(d_attn_in * (1.0 + scale_one), normed_one, inverse_one)
+        ).astype(jnp.bfloat16)
+        d_modul = jnp.concatenate(
+            [d_shift_one, d_scale_one, d_gate_one, d_shift_two, d_scale_two, d_gate_two], axis=1
+        ).astype(jnp.bfloat16)
     silu_pull = jax.vjp(jax.nn.silu, cond_float)[1]
     grad_condition = silu_pull(jnp.dot(d_modul, w_ada, preferred_element_type=jnp.float32))[0]
     biases = [bias_query, bias_value, bias_proj, bias_fc1, bias_fc2]
@@ -968,14 +1606,22 @@
         biases + [d_modul.astype(jnp.float32).reshape(-1), jnp.zeros((2 * lanes,), jnp.float32)]
     ).reshape(-1, lanes)
 
-    terms = [
-        (attended.T, d_attn_own, d_attn_sib, w_proj),
-        (active.T, d_branch_own, d_branch_sib, w_fc2),
-        (attn_in.T, d_qkv_own, d_qkv_sib, w_qkv),
-        (mlp_in.T, d_hidden_own, d_hidden_sib, w_fc1),
-    ]
-    (grad_proj, grad_fc2, grad_qkv, grad_fc1), note_own, note_sib = scatter(terms, note)
-    total_note = (jnp.sum(note_own, axis=0) + jnp.sum(note_sib, axis=0)).reshape(-1)
+    if fast:
+        pairs = [(attn_in_t, d_split), (attended_t, d_attn)]
+        (grad_qkv, grad_proj), note_own, note_sib = scatter_all(pairs, [w_qkv, w_proj], note)
+    else:
+        terms = [
+            (attended.T, d_attn_own, d_attn_sib, w_proj),
+            (active.T, d_branch_own, d_branch_sib, w_fc2),
+            (attn_in.T, d_qkv_own, d_qkv_sib, w_qkv),
+            (mlp_in.T, d_hidden_own, d_hidden_sib, w_fc1),
+        ]
+        summed_grads, note_own, note_sib = scatter_plain(terms, note)
+        grad_proj, grad_fc2, grad_qkv, grad_fc1 = summed_grads
+    stacked = (-1,) + note.shape
+    total_note = (
+        jnp.sum(note_own.reshape(stacked), axis=0) + jnp.sum(note_sib.reshape(stacked), axis=0)
+    ).reshape(-1)
     summed, start = [], 0
     for vector in biases + [b_ada]:
         summed.append(total_note[start : start + vector.shape[0]])
@@ -984,7 +1630,7 @@
     share_rows = 6 * D // lax.axis_size(("dp", "fsdp"))
     own_start = first + lax.axis_index(("dp", "fsdp")) * share_rows
     notes = jnp.concatenate([note_own, note_sib]).reshape(-1, note.size)
-    silus = jnp.concatenate([own[0], sib[0]])[:, 1:10].reshape(-1, D)
+    silus = jnp.concatenate([own_facts, sib_facts])[:, 1:10].reshape(-1, D)
     columns = lax.dynamic_slice_in_dim(notes, own_start, share_rows, 1)
     grad_ada = lax.dot_general(
         columns.astype(jnp.bfloat16),

time: 478 us -> 436 us (0.912)
  matrix products: 104 us -> 10.5 us
  Pallas kernels: 293 us -> 382 us
  other arithmetic: 30.2 us -> 11.9 us
  local copies, waits for them, and re-layouts: 41 us -> 26.1 us
    pallas_call x0 -> x1, Pallas kernels: none -> 143 us  [back_all(): pl.pallas_call(back_kernel, out_shape=[jax.ShapeDtypeStruct(shard.shape,...]
    dot_general x23 -> x0, matrix products: 94.2 us -> none  [the longest x8 29.9 us: times(): return jnp.dot(left, right, preferred_element_type=jnp.float32)]
    pallas_call x1, Pallas kernels: 160 us -> 80 us  [scatter_all(): pl.pallas_call(functools.partial(scatter_kernel, count), out_shape=[jax.S...]
    pallas_call x1, Pallas kernels: 132 us -> 159 us  [gather_all(): pl.pallas_call(functools.partial(gather_kernel, count), out_shape=spread...]
    unnamed x250 -> x39, local copies, waits for them, and re-layouts: 29.5 us -> 12.2 us
    reduce_sum x13 -> x6, other arithmetic: 11.5 us -> 4 us  [the longest x2 1.85 us: shards(): counts = (jnp.sum(own_facts, axis=0) + jnp.sum(sib_facts, axis=0))[0, :BINS]]
    select_n x5 -> x0, other arithmetic: 6.25 us -> none  [the longest x1 5.4 us: join(): jnp.where(core == 0, jnp.concatenate([own, sib], axis=-1), jnp.concatenat...]
    reshape x0 -> x5, local copies, waits for them, and re-layouts: none -> 5.83 us  [the longest x4 4.54 us: shards(): row = lambda vector: vector.reshape(1, -1)]
where the time goes in v3:
time: 436 us; the launch traced here: 434 us
  Pallas kernels  382 us (88%)
  local copies, waits for them, and re-layouts  26.1 us (6%)
  other arithmetic  11.9 us (3%)
  matrix products  10.5 us (2%)
    pallas_call x1, Pallas kernels, gather_all(): pl.pallas_call(functools.partial(gather_kernel, count), out_shape=spread...  159 us
    pallas_call x1, Pallas kernels, back_all(): pl.pallas_call(back_kernel, out_shape=[jax.ShapeDtypeStruct(shard.shape,...  143 us
    pallas_call x1, Pallas kernels, scatter_all(): pl.pallas_call(functools.partial(scatter_kernel, count), out_shape=[jax.S...  80 us
    unnamed x39, local copies, waits for them, and re-layouts  12.2 us

profile of v3, /device:TPU:16, one launch (start us, length us, event | category | flops | bytes accessed | tf_op | source)
XLA Modules:
  0.0 434.3 jit_solution(6896200022642836485)
XLA Ops:
  0.6 1.3 fusion.10
  10.1 1.3 reshape.144.refs_12_
  11.5 1.3 reshape.143.refs_11_
  12.8 1.3 reshape.145.refs_13_
  14.1 158.8 %gather_all.1 = (f32[256,128]{1,0:T(8,128)}, bf16[1152,1728]{1,0:T(8,128)(2,1)}, bf16[1152,576]{1,0:T(8,128)(2,1)}, bf16[1152,2304]{1,0:T(8,128)(2,1)}, bf16[460...) custom-call(f32[16,128]{1,0:T(8,128)} %maximum_maximum_fusion.refs_0, ...), custom_call_target="tpu_custom_call" | custom-call | tf_op jit(solution)/shard_map/gather_all/pallas_call | solution.py:723
  172.9 0.9 reduce_sum.76
  173.8 0.9 reduce_sum.77
  178.0 143.4 %back_all.1 = (f32[288,576]{1,0:T(8,128)}, f32[72,2304]{1,0:T(8,128)}, bf16[2,256,576]{2,1,0:T(8,128)(2,1)}, bf16[2,256,1728]{2,1,0:T(8,128)(2,1)}, bf16[256,115...) custom-call(bf16[4608,256]{1,0:T(8,128)(2,1)} %get-tuple-element.48.refs_0_, ...), custom_call_target="tpu_custom_call" | custom-call | tf_op jit(solution)/shard_map/back_all/pallas_call | solution.py:1272
  321.4 1.1 reduce_sum.80
  322.6 1.3 constant_dynamic-update-slice_fusion.5
  323.9 1.3 constant_dynamic-update-slice_fusion.4
  325.2 1.3 constant_dynamic-update-slice_fusion.3
  326.5 1.0 reduce_sum.81
  327.5 1.4 constant_dynamic-update-slice_fusion.2
  328.8 1.3 constant_dynamic-update-slice_fusion.1
  330.2 1.4 convert_dynamic-update-slice_fusion
  331.6 1.3 constant_dynamic-update-slice_fusion
  332.9 80.0 %scatter_all.1 = (f32[72,1728]{1,0:T(8,128)}, f32[72,576]{1,0:T(8,128)}, f32[2048,128]{1,0:T(8,128)}, f32[2048,128]{1,0:T(8,128)}) custom-call(bf16[1152,256]{1,0:T(8,128)(2,1)} %get-tuple-element.69.refs_0_, bf16[2,256,1728]{2,1,0:T(8,128)(2,1)} %get-tuple-element.70.refs_1_, bf16[1152,256]{1,0:T(8,128)(2,1)} %get-tuple-element.71.refs_2_, ...), custom_call_target="tpu_custom_call" | custom-call | tf_op jit(solution)/shard_map/scatter_all/pallas_call | solution.py:1339
  412.9 1.8 pad_maximum_fusion
  414.7 1.3 reshape.154
  416.1 2.1 fusion
  421.0 8.4 %fusion.4 = f32[1,1152]{1,0:T(1,128)} fusion(f32[1,1152]{1,0:T(1,128)S(1)} %get-tuple-element.85, bf16[1,1152]{1,0:T(2,128)(2,1)S(1)} %copy-done.11, bf16[6912,1]{0,1:T(2,128)(2,1)S(1)} %bitcast.56, bf16[6912,1152]{1,0:T(8,128)(2,1)} %refs_7_.1), kind=kOutput, calls=%fused_computation.18 | convolution fusion | flops 15933312 | bytes 15950592 | tf_op jit(solution)/shard_map/dot_general | solution.py:1603
  432.6 0.8 copy.55
  433.4 0.9 copy.56
  (63 shorter events, 14.9 us)
Async XLA Ops:
  14.1 161.9 %copy-start.12 = (s32[16]{0:T(128)S(1)}, s32[16]{0:T(128)}, u32[]{:S(2)}) copy-start(s32[16]{0:T(128)} %param.22) | copy-start | bytes 196
  322.5 7.6 %copy-start.9 = (f32[10,1152]{1,0:T(8,128)}, f32[10,1152]{1,0:T(8,128)S(1)}, u32[]{:S(2)}) copy-start(f32[10,1152]{1,0:T(8,128)S(1)} %reduce_sum.80) | copy-start | bytes 138244
  412.9 3.1 copy-start.6
  412.9 3.1 copy-start.7
  412.9 5.3 %copy-start.1 = (f32[2048,128]{1,0:T(8,128)S(1)}, f32[2048,128]{1,0:T(8,128)}, u32[]{:S(2)}) copy-start(f32[2048,128]{1,0:T(8,128)} %get-tuple-element.75) | copy-start | bytes 3145732
  412.9 5.4 %copy-start = (f32[2048,128]{1,0:T(8,128)S(1)}, f32[2048,128]{1,0:T(8,128)}, u32[]{:S(2)}) copy-start(f32[2048,128]{1,0:T(8,128)} %get-tuple-element.76) | copy-start | bytes 3145732
  412.9 8.1 %copy-start.11 = (bf16[1,1152]{1,0:T(2,128)(2,1)S(1)}, bf16[1,1152]{1,0:T(2,128)(2,1)}, u32[]{:S(2)}) copy-start(bf16[1,1152]{1,0:T(2,128)(2,1)} %param.18) | copy-start | bytes 6916
  421.0 8.5 %copy-start.4 = (bf16[256,1152]{1,0:T(8,128)(2,1)S(1)}, bf16[256,1152]{1,0:T(8,128)(2,1)}, u32[]{:S(2)}) copy-start(bf16[256,1152]{1,0:T(8,128)(2,1)} %get-tuple-element.47) | copy-start | bytes 1769476
  421.0 9.3 %copy-start.5 = (bf16[256,1152]{1,0:T(8,128)(2,1)S(1)}, bf16[256,1152]{1,0:T(8,128)(2,1)}, u32[]{:S(2)}) copy-start(bf16[256,1152]{1,0:T(8,128)(2,1)} %get-tuple-element.67) | copy-start | bytes 1769476
  421.0 10.1 %copy-start.8 = (f32[72,1728]{1,0:T(8,128)S(1)}, f32[72,1728]{1,0:T(8,128)}, u32[]{:S(2)}) copy-start(f32[72,1728]{1,0:T(8,128)} %get-tuple-element.111) | copy-start | bytes 1492996
  421.0 10.9 %copy-start.10 = (f32[72,576]{1,0:T(8,128)S(1)}, f32[72,576]{1,0:T(8,128)}, u32[]{:S(2)}) copy-start(f32[72,576]{1,0:T(8,128)} %get-tuple-element.114) | copy-start | bytes 497668
  429.5 3.1 copy-start.3
  429.5 3.9 copy-start.2

commit v4 on v3

--- a/solution.py
+++ b/solution.py
@@ -458,6 +458,11 @@
     return over
 
 
+def valid_row(facts):
+    count = jnp.sum(facts[0:1, :], axis=1, keepdims=True)
+    return lax.broadcasted_iota(jnp.int32, (1, SEQ), 1).astype(jnp.float32) < count
+
+
 def flip(source, out):
     @pl.loop(0, source.shape[-1] // 128)
     def _(t):
@@ -481,17 +486,9 @@
 class Forward:
     def __init__(self, at, ins, outs, scratch, jobs):
         self.at, self.jobs = at, jobs
-        (
-            self.tokens,
-            self.silu,
-            self.w_ada,
-            self.b_ada,
-            self.valid,
-            self.b_qkv,
-            self.b_proj,
-            self.b_fc1,
-            self.b_fc2,
-        ) = ins
+        self.tokens, self.condition, self.w_ada, self.bias = ins
+        self.facts = jobs[0].shard
+        self.b_proj, self.b_fc2 = self.bias.at[3:4], self.bias.at[8:9]
         (
             self.modul,
             self.attn_in_t,
@@ -509,7 +506,8 @@
         self.ada, self.loose = scratch[:2]
         self.weights = dict(zip(WEIGHTS, scratch[2:6]))
         self.attn_in, self.attended, self.mlp_in, self.active = scratch[6:10]
-        self.ada_sem, self.load_sem = scratch[10:]
+        self.silu, self.b_qkv, self.b_fc1 = scratch[10:13]
+        self.ada_sem, self.load_sem = scratch[13:]
 
     def ada_copy(self, part):
         slot = part % 2
@@ -522,6 +520,12 @@
         self.ada_copy(0).start()
         self.lse[...] = jnp.zeros(self.lse.shape, jnp.float32)
         self.attended[...] = jnp.zeros(self.attended.shape, jnp.bfloat16)
+        silu = jax.nn.silu(self.condition[...].astype(jnp.float32))
+        self.silu[...] = jnp.broadcast_to(silu, self.silu.shape).astype(jnp.bfloat16)
+        for flat, first in ((self.b_qkv, 0), (self.b_fc1, 4)):
+            for part in range(flat.shape[1] // D):
+                value = self.bias[first + part : first + part + 1, :]
+                flat[:, part * D : (part + 1) * D] = jnp.broadcast_to(value, (8, D))
 
     def mod(self, half):
         @pl.loop(half * 3, half * 3 + 3)
@@ -534,7 +538,7 @@
                 LAST_DIMS,
                 preferred_element_type=jnp.float32,
             )
-            self.modul[part] = value[:8] + self.b_ada[part]
+            self.modul[part] = value[:8] + self.bias[pl.ds(9 + part, 1), :]
 
     def piece(self, index):
         return self.modul[index, 0:1, :]
@@ -598,6 +602,8 @@
         self.product(self.attn_in, "qkv", half, self.qkv, self.b_qkv)
 
     def attend(self, part):
+        is_valid = valid_row(self.facts)
+
         @pl.loop(part * 4, part * 4 + 4)
         def _(head):
             begin = head * HD
@@ -613,7 +619,7 @@
             scores = lax.dot_general(
                 query.astype(jnp.bfloat16), keys, LAST_DIMS, preferred_element_type=jnp.float32
             ) * HD ** (-0.5)
-            scores = jnp.where(self.valid[0:1, :] > 0.5, scores, NEG_FILL)
+            scores = jnp.where(is_valid, scores, NEG_FILL)
             row_max = jnp.max(scores, axis=1, keepdims=True)
             exponent = jnp.exp(scores - row_max)
             row_total = jnp.sum(exponent, axis=1, keepdims=True)
@@ -686,9 +692,9 @@
         del refs[:n]
         return out
 
-    shards, ins = take(count), take(9)
+    shards, ins = take(count), take(4)
     own, sib, outs = take(count), take(count), take(12)
-    sems, scratch = take(6), take(12)
+    sems, scratch = take(6), take(15)
     at = Place()
     at.greet()
     jobs = [
@@ -723,12 +729,14 @@
     outs = pl.pallas_call(
         functools.partial(gather_kernel, count),
         out_shape=spread + spread + [jax.ShapeDtypeStruct(*kind) for kind in kinds],
-        in_specs=[VMEM] * count + [VMEM, VMEM, ANY] + [VMEM] * 6,
+        in_specs=[VMEM] * count + [VMEM, VMEM, ANY, VMEM],
         out_specs=[ANY] * (2 * count) + [VMEM] * len(kinds),
         scratch_shapes=gather_sems(count)
         + [pltpu.VMEM((2, D, D), jnp.bfloat16), pltpu.VMEM((SEQ, 1792), jnp.float32)]
         + [pltpu.VMEM((2,) + s.shape, s.dtype) for s in spread[1:]]
         + [pltpu.VMEM((SEQ, width), jnp.bfloat16) for width in (D, D, D, 4 * D)]
+        + [pltpu.VMEM((16, D), jnp.bfloat16)]
+        + [pltpu.VMEM((8, width), jnp.float32) for width in (3 * D, 4 * D)]
         + [dma((2,)), dma((4, 2))],
         compiler_params=pltpu.CompilerParams(
             collective_id=0, has_side_effects=True, vmem_limit_bytes=VMEM_LIMIT
@@ -1001,7 +1009,9 @@
         self.at, self.jobs = at, jobs
         (
             self.modul,
-            self.weight,
+            self.facts,
+            self.facts_own,
+            self.facts_sib,
             self.cotangent,
             self.branch,
             self.hidden,
@@ -1009,11 +1019,10 @@
             self.attn_out,
             self.lse,
             self.qkv,
-            self.valid,
             self.tokens,
-        ) = ins[:11]
-        self.own, self.sib = ins[11:15], ins[15:19]
-        self.d_attn, self.d_split, self.grad_tokens, self.sums, self.sums_fc1 = outs
+        ) = ins[:12]
+        self.own, self.sib = ins[12:16], ins[16:20]
+        self.d_attn, self.d_split, self.grad_tokens, self.note = outs
         (
             self.d_branch,
             self.d_hidden,
@@ -1021,6 +1030,9 @@
             self.d_middle,
             self.d_attended,
             self.d_qkv,
+            self.sums,
+            self.sums_fc1,
+            self.weight,
             self.slim,
             self.wide,
             self.long,
@@ -1062,6 +1074,21 @@
         self.fetch(0, 0)
         self.sums[...] = jnp.zeros(self.sums.shape, jnp.float32)
         self.d_qkv[...] = jnp.zeros(self.d_qkv.shape, jnp.bfloat16)
+        shape = self.facts_own.shape
+        is_count = lax.broadcasted_iota(jnp.int32, shape, 0) % 16 == 0
+        counts = jnp.sum(
+            jnp.where(is_count, self.facts_own[...] + self.facts_sib[...], 0.0),
+            axis=0,
+            keepdims=True,
+        )
+        is_bin = lax.broadcasted_iota(jnp.int32, counts.shape, 1) < BINS
+        mean = jnp.sum(counts, axis=1, keepdims=True) / BINS
+        bin_scale = self.facts[10:11, :] * mean / jnp.where(is_bin, counts, 1.0)
+        mine = self.facts[0:1, :]
+        scale = jnp.sum(jnp.where(mine > 0.0, bin_scale, 0.0), axis=1, keepdims=True)
+        tokens = jnp.sum(mine, axis=1, keepdims=True)
+        row = lax.broadcasted_iota(jnp.int32, shape, 0).astype(jnp.float32)
+        self.weight[...] = jnp.where(row < tokens, scale, 0.0)
 
         @spread_rows(SEQ)
         def _(rows):
@@ -1124,6 +1151,8 @@
             )
 
     def attend(self, part):
+        is_valid = valid_row(self.facts)
+
         @pl.loop(part * 4, part * 4 + 4)
         def _(head):
             begin = head * HD
@@ -1146,7 +1175,6 @@
             log_total = jnp.sum(
                 jnp.where(column == head, self.lse[...], 0.0), axis=1, keepdims=True
             )
-            is_valid = self.valid[0:1, :] > 0.5
             scores = lax.dot_general(
                 query, keys, LAST_DIMS, preferred_element_type=jnp.float32
             ) * HD ** (-0.5)
@@ -1198,6 +1226,17 @@
                 self.d_middle[rows, :] + norm_back(d_in * (1.0 + self.piece(1)), normed, inverse)
             ).astype(jnp.bfloat16)
 
+        for index in range(10):
+            row = jnp.sum(self.sums[index], axis=0, keepdims=True)
+            if index < 6:
+                row = row.astype(jnp.bfloat16).astype(jnp.float32)
+            self.note[index : index + 1, :] = row
+        for index in range(4):
+            self.note[10 + index : 11 + index, :] = jnp.sum(
+                self.sums_fc1[:, index * D : (index + 1) * D], axis=0, keepdims=True
+            )
+        self.note[14:16, :] = jnp.zeros((2, D), jnp.float32)
+
 
 def scatter_bufs(terms):
     scratch = []
@@ -1220,9 +1259,9 @@
         del refs[:n]
         return out
 
-    lefts, ins = take(2), take(19)
-    results, outs = take(2), take(5)
-    scratch = take(12)
+    lefts, ins = take(2), take(20)
+    results, outs = take(2), take(4)
+    scratch = take(15)
     bufs = [take(6) for _ in range(2)]
     sems = take(8)
     at = Place()
@@ -1253,8 +1292,7 @@
         ((2, SEQ, D // 2), bf16),
         ((2, SEQ, 3 * D // 2), bf16),
         ((SEQ, D), bf16),
-        ((10, 8, D), f32),
-        ((8, 4 * D), f32),
+        ((16, D), f32),
     ]
     own = [
         ((2, SEQ, D // 2), bf16),
@@ -1263,6 +1301,9 @@
         ((SEQ, D), f32),
         ((SEQ, D), bf16),
         ((SEQ, 3 * D), bf16),
+        ((10, 8, D), f32),
+        ((8, 4 * D), f32),
+        ((SEQ, 128), f32),
         ((2, 2, 384, D // 2), bf16),
         ((2, 384, 2 * D), bf16),
         ((2, 384, 3 * D // 2), bf16),
@@ -1273,8 +1314,8 @@
         back_kernel,
         out_shape=[jax.ShapeDtypeStruct(shard.shape, f32) for shard in shards]
         + [jax.ShapeDtypeStruct(*kind) for kind in kinds],
-        in_specs=[VMEM] * 13 + [ANY] * 8,
-        out_specs=[VMEM] * 7,
+        in_specs=[VMEM] * 14 + [ANY] * 8,
+        out_specs=[VMEM] * 6,
         scratch_shapes=[pltpu.VMEM(*kind) for kind in own]
         + [dma((2, 2)), dma((2,)), dma((2,))]
         + scatter_bufs(terms),
@@ -1295,11 +1336,25 @@
         return out
 
     ins = [take(2) for _ in range(count)]
-    note = take(1)[0]
+    note, w_ada = take(2)
     results = take(count)
-    note_own, note_sib = take(2)
+    note_own, note_sib, d_silu = take(3)
     bufs = [take(6) for _ in range(count)]
     sems, note_sems = take(8), take(6)
+    ada, ada_sem = take(2)
+
+    def ada_copy(part):
+        rows = pl.ds(part * D, D)
+        return pltpu.make_async_copy(w_ada.at[rows], ada.at[part % 2], ada_sem.at[part % 2])
+
+    def silu_part(part):
+        if part < 5:
+            ada_copy(part + 1).start()
+        ada_copy(part).wait()
+        row = jnp.broadcast_to(note[part : part + 1, :], (16, D)).astype(jnp.bfloat16)
+        value = jnp.dot(row, ada[part % 2], preferred_element_type=jnp.float32)
+        d_silu[...] = value if part == 0 else d_silu[...] + value
+
     at = Place()
     at.greet()
     jobs = [Scatter(at, k, ins[k], results[k], bufs[k], sems) for k in range(count)]
@@ -1315,14 +1370,17 @@
             action()
         del whisper[:n]
 
+    ada_copy(0).start()
     speak(1)
     seen = set()
-    for stage, k, part in ORDER:
+    for turn, (stage, k, part) in enumerate(ORDER):
         if k not in seen:
             jobs[k].ready()
             seen.add(k)
         getattr(jobs[k], "stage_" + STAGES[stage])(part)
         speak(2)
+        if turn % 2 and turn < 12:
+            silu_part(turn // 2)
     speak(len(whisper))
     for job in jobs:
         job.finish()
@@ -1330,25 +1388,28 @@
     word.finish()
 
 
-def scatter_all(pairs, shards, note):
+def scatter_all(pairs, shards, note, w_ada):
     count = len(pairs)
     spread = jax.ShapeDtypeStruct((16 * note.shape[0], note.shape[1]), note.dtype)
+    dma = pltpu.SemaphoreType.DMA
     terms = [
         (left, halves, shard, k in MID) for k, ((left, halves), shard) in enumerate(zip(pairs, shards))
     ]
     outs = pl.pallas_call(
         functools.partial(scatter_kernel, count),
         out_shape=[jax.ShapeDtypeStruct(shard.shape, jnp.float32) for shard in shards]
-        + [spread, spread],
-        in_specs=[VMEM, VMEM] * count + [VMEM],
-        out_specs=[VMEM] * count + [ANY, ANY],
-        scratch_shapes=scatter_bufs(terms) + gather_sems(1),
+        + [spread, spread, jax.ShapeDtypeStruct((16, D), jnp.float32)],
+        in_specs=[VMEM, VMEM] * count + [VMEM, ANY],
+        out_specs=[VMEM] * count + [ANY, ANY, VMEM],
+        scratch_shapes=scatter_bufs(terms)
+        + gather_sems(1)
+        + [pltpu.VMEM((2, D, D), jnp.bfloat16), dma((2,))],
         compiler_params=pltpu.CompilerParams(
             collective_id=2, has_side_effects=True, vmem_limit_bytes=VMEM_LIMIT
         ),
         name="scatter_all",
-    )(*[part for pair in pairs for part in pair], note)
-    return outs[:count], outs[count], outs[count + 1]
+    )(*[part for pair in pairs for part in pair], note, w_ada)
+    return outs[:count], outs[count], outs[count + 1], outs[count + 2]
 
 
 def gather_plain(shards):
@@ -1436,24 +1497,17 @@
         [
             head,
             silu_cond.astype(jnp.float32).reshape(-1, lanes),
-            jnp.zeros((6, lanes), jnp.float32),
+            jnp.pad(bin_weights.astype(jnp.float32), (0, lanes - BINS))[None],
+            jnp.zeros((5, lanes), jnp.float32),
         ]
     )
     shares = [facts, w_qkv, w_proj, w_fc1, w_fc2]
     bias_qkv = jnp.concatenate([b_query, jnp.zeros_like(b_query), b_value])
     if fast:
-        row = lambda vector: vector.reshape(1, -1)
-        ins = [
-            tokens.reshape(SEQ, D),
-            jnp.broadcast_to(silu_cond, (16, D)),
-            w_ada,
-            jnp.broadcast_to(b_ada.reshape(6, 1, D), (6, 8, D)),
-            jnp.broadcast_to(valid_keys.astype(jnp.float32), (8, SEQ)),
-            row(bias_qkv),
-            row(b_proj),
-            row(b_fc1),
-            row(b_fc2),
-        ]
+        bias = jnp.concatenate(
+            [bias_qkv, b_proj, b_fc1, b_fc2, b_ada, jnp.zeros((D,), jnp.float32)]
+        ).reshape(16, D)
+        ins = [tokens.reshape(SEQ, D), condition, w_ada, bias]
         own, sib, outs = gather_all(shares, ins)
     else:
         own, sib = gather_plain(shares)
@@ -1461,10 +1515,6 @@
     qkv_own, proj_own, fc1_own, fc2_own = own[1:]
     qkv_sib, proj_sib, fc1_sib, fc2_sib = sib[1:]
     own_facts, sib_facts = own[0].reshape(-1, 16, lanes), sib[0].reshape(-1, 16, lanes)
-    counts = (jnp.sum(own_facts, axis=0) + jnp.sum(sib_facts, axis=0))[0, :BINS]
-    bin_scale = bin_weights.astype(jnp.float32) * (jnp.sum(counts) / BINS) / counts
-    image_scale = jnp.sum(bin_table * bin_scale[None, :], axis=1)
-
     def times(left, right):
         return jnp.dot(left, right, preferred_element_type=jnp.float32)
 
@@ -1474,10 +1524,11 @@
     if fast:
         modul, attn_in_t, qkv_all, lse, attended_t, attn_out, middle = outs[:7]
         mlp_in_t, hidden, active_t, branch, result = outs[7:]
-        weight = valid_keys.astype(jnp.float32) * image_scale[:, None]
         ins_back = [
             modul,
-            jnp.broadcast_to(weight.reshape(SEQ, 1), (SEQ, lanes)),
+            facts,
+            own[0],
+            sib[0],
             cotangent.reshape(SEQ, D),
             branch,
             hidden,
@@ -1485,19 +1536,22 @@
             attn_out,
             lse,
             qkv_all,
-            ins[4],
             tokens.reshape(SEQ, D),
         ]
         (grad_fc2, grad_fc1), outs = back_all(
             [active_t, mlp_in_t], ins_back + list(own[1:]) + list(sib[1:]), [w_fc2, w_fc1]
         )
-        d_attn, d_split, grad_tokens, sums, sums_fc1 = outs
-        sums = jnp.sum(sums, axis=1)
-        bias_query, bias_value, bias_proj, bias_fc2 = sums[6], sums[7], sums[8], sums[9]
-        bias_fc1 = jnp.sum(sums_fc1, axis=0)
-        d_modul = sums[:6].reshape(1, 6 * D).astype(jnp.bfloat16)
+        d_attn, d_split, grad_tokens, note = outs
+        pairs = [(attn_in_t, d_split), (attended_t, d_attn)]
+        (grad_qkv, grad_proj), note_own, note_sib, d_silu = scatter_all(
+            pairs, [w_qkv, w_proj], note, w_ada
+        )
+        d_silu = d_silu[0:1]
         result, grad_tokens = result.reshape(tokens.shape), grad_tokens.reshape(tokens.shape)
     else:
+        counts = (jnp.sum(own_facts, axis=0) + jnp.sum(sib_facts, axis=0))[0, :BINS]
+        bin_scale = bin_weights.astype(jnp.float32) * (jnp.sum(counts) / BINS) / counts
+        image_scale = jnp.sum(bin_table * bin_scale[None, :], axis=1)
         token_float = tokens.astype(jnp.float32)
         normed_one, inverse_one = norm_rows(token_float)
         modul = (
@@ -1599,17 +1653,12 @@
         d_modul = jnp.concatenate(
             [d_shift_one, d_scale_one, d_gate_one, d_shift_two, d_scale_two, d_gate_two], axis=1
         ).astype(jnp.bfloat16)
-    silu_pull = jax.vjp(jax.nn.silu, cond_float)[1]
-    grad_condition = silu_pull(jnp.dot(d_modul, w_ada, preferred_element_type=jnp.float32))[0]
-    biases = [bias_query, bias_value, bias_proj, bias_fc1, bias_fc2]
-    note = jnp.concatenate(
-        biases + [d_modul.astype(jnp.float32).reshape(-1), jnp.zeros((2 * lanes,), jnp.float32)]
-    ).reshape(-1, lanes)
-
-    if fast:
-        pairs = [(attn_in_t, d_split), (attended_t, d_attn)]
-        (grad_qkv, grad_proj), note_own, note_sib = scatter_all(pairs, [w_qkv, w_proj], note)
-    else:
+        d_silu = jnp.dot(d_modul, w_ada, preferred_element_type=jnp.float32)
+        note = jnp.concatenate(
+            [d_modul.astype(jnp.float32).reshape(-1)]
+            + [bias_query, bias_value, bias_proj, bias_fc2, bias_fc1]
+            + [jnp.zeros((2 * D,), jnp.float32)]
+        ).reshape(16, D)
         terms = [
             (attended.T, d_attn_own, d_attn_sib, w_proj),
             (active.T, d_branch_own, d_branch_sib, w_fc2),
@@ -1618,20 +1667,16 @@
         ]
         summed_grads, note_own, note_sib = scatter_plain(terms, note)
         grad_proj, grad_fc2, grad_qkv, grad_fc1 = summed_grads
-    stacked = (-1,) + note.shape
-    total_note = (
-        jnp.sum(note_own.reshape(stacked), axis=0) + jnp.sum(note_sib.reshape(stacked), axis=0)
-    ).reshape(-1)
-    summed, start = [], 0
-    for vector in biases + [b_ada]:
-        summed.append(total_note[start : start + vector.shape[0]])
-        start += vector.shape[0]
-    first = start - b_ada.shape[0]
+    grad_condition = jax.vjp(jax.nn.silu, cond_float)[1](d_silu)[0]
+    note_own, note_sib = note_own.reshape(-1, 16, D), note_sib.reshape(-1, 16, D)
+    summed = jnp.sum(note_own, axis=0) + jnp.sum(note_sib, axis=0)
     share_rows = 6 * D // lax.axis_size(("dp", "fsdp"))
-    own_start = first + lax.axis_index(("dp", "fsdp")) * share_rows
-    notes = jnp.concatenate([note_own, note_sib]).reshape(-1, note.size)
+    own_start = lax.axis_index(("dp", "fsdp")) * share_rows
+    notes = lax.dynamic_slice_in_dim(
+        jnp.concatenate([note_own, note_sib]), own_start // D, 2, 1
+    ).reshape(-1, 2 * D)
     silus = jnp.concatenate([own_facts, sib_facts])[:, 1:10].reshape(-1, D)
-    columns = lax.dynamic_slice_in_dim(notes, own_start, share_rows, 1)
+    columns = lax.dynamic_slice_in_dim(notes, own_start % D, share_rows, 1)
     grad_ada = lax.dot_general(
         columns.astype(jnp.bfloat16),
         silus.astype(jnp.bfloat16),
@@ -1643,16 +1688,16 @@
         grad_tokens,
         grad_condition,
         grad_qkv,
-        summed[0],
-        summed[1],
+        summed[6],
+        summed[7],
         grad_proj,
-        summed[2],
+        summed[8],
         grad_fc1,
-        summed[3],
+        summed[10:14].reshape(-1),
         grad_fc2,
-        summed[4],
+        summed[9],
         grad_ada,
-        summed[5],
+        summed[:6].reshape(-1),
     )
 
 

time: 436 us -> 408 us (0.936)
  local copies, waits for them, and re-layouts: 26.1 us -> 13.1 us
  matrix products: 10.5 us -> 1.36 us
  other arithmetic: 11.9 us -> 5.63 us
    dot_general x1 -> x0, matrix products: 8.43 us -> none  [shards(): jnp.dot(d_modul, w_ada, preferred_element_type=jnp.float32)]
    reduce_sum x8 -> x2, other arithmetic: 5.21 us -> 0.13 us  [shards(): summed = jnp.sum(note_own, axis=0) + jnp.sum(note_sib, axis=0)]
    unnamed x39 -> x36, local copies, waits for them, and re-layouts: 12.2 us -> 9.16 us
where the time goes in v4:
time: 408 us; the launch traced here: 407 us
  Pallas kernels  385 us (94%)
  local copies, waits for them, and re-layouts  13.1 us (3%)
  other arithmetic  5.63 us (1%)
    pallas_call x1, Pallas kernels, gather_all(): pl.pallas_call(functools.partial(gather_kernel, count), out_shape=spread...  159 us
    pallas_call x1, Pallas kernels, back_all(): pl.pallas_call(back_kernel, out_shape=[jax.ShapeDtypeStruct(shard.shape,...  144 us
    pallas_call x1, Pallas kernels, scatter_all(): pl.pallas_call(functools.partial(scatter_kernel, count), out_shape=[jax.S...  82.2 us
    unnamed x36, local copies, waits for them, and re-layouts  9.16 us

profile of v4, /device:TPU:16, one launch (start us, length us, event | category | flops | bytes accessed | tf_op | source)
XLA Modules:
  0.0 407.5 jit_solution(10201475291729978863)
XLA Ops:
  0.6 1.3 fusion.7
  3.9 0.7 convert_element_type.28
  4.6 0.7 convert_reduce_fusion
  5.4 0.7 maximum_maximum_fusion.refs_0_.refs_3_
  6.1 0.7 constant_dynamic-update-slice_fusion.7
  6.8 0.7 constant_dynamic-update-slice_fusion.5
  7.5 0.7 constant_dynamic-update-slice_fusion.4
  8.2 0.7 constant_dynamic-update-slice_fusion.3
  8.9 0.7 constant_dynamic-update-slice_fusion.2
  9.6 0.8 constant_dynamic-update-slice_fusion.1
  10.4 0.6 reshape.93.refs_8_
  11.0 158.7 %gather_all.1 = (f32[256,128]{1,0:T(8,128)}, bf16[1152,1728]{1,0:T(8,128)(2,1)}, bf16[1152,576]{1,0:T(8,128)(2,1)}, bf16[1152,2304]{1,0:T(8,128)(2,1)}, bf16[460...) custom-call(f32[16,128]{1,0:T(8,128)} %maximum_maximum_fusion.refs_0, ...), custom_call_target="tpu_custom_call" | custom-call | tf_op jit(solution)/shard_map/gather_all/pallas_call | solution.py:729
  169.7 143.7 %back_all.1 = (f32[288,576]{1,0:T(8,128)}, f32[72,2304]{1,0:T(8,128)}, bf16[2,256,576]{2,1,0:T(8,128)(2,1)}, bf16[2,256,1728]{2,1,0:T(8,128)(2,1)}, bf16[256,1152]{1,0:T(8,128)(2,1)}, /*index=5*/f32[16,1152]{1,0:T(8,128)}) custom-call(bf16[4608,256]{1,0:T(8,128)(2,1)} %get-tuple-element.48.refs_0_, bf16[1152,256]{1,0:T(8,128)(2,1)} %get-tuple-element.49.refs_1_, ...), custom_call_target="tpu_custom_call" | custom-call | tf_op jit(solution)/shard_map/back_all/pallas_call | solution.py:1313
  313.4 82.2 %scatter_all.1 = (f32[72,1728]{1,0:T(8,128)}, f32[72,576]{1,0:T(8,128)}, f32[256,1152]{1,0:T(8,128)}, f32[256,1152]{1,0:T(8,128)}, f32[16,1152]{1,0:T(8,128)}) custom-call(bf16[1152,256]{1,0:T(8,128)(2,1)} %get-tuple-element.68.refs_0_, bf16[2,256,1728]{2,1,0:T(8,128)(2,1)} %get-tuple-element.69.refs_1_, bf16[1152,256]{1,0:T(8,128)(2,1)} %get-tuple-element.70.refs_2_, ...), custom_call_target="tpu_custom_call" | custom-call | tf_op jit(solution)/shard_map/scatter_all/pallas_call | solution.py:1398
  395.7 2.0 fusion
  397.8 1.4 fusion.1
  400.7 0.6 slice_reduce_fusion
  401.3 1.4 fusion.5
  402.7 0.8 copy.52
  403.5 0.8 copy.53
  404.3 0.8 copy.54
  405.1 0.7 copy.55
  405.8 0.8 copy.56
  406.6 0.9 copy.57
  (40 shorter events, 1.6 us)
Async XLA Ops:
  395.6 2.1 copy-start.7
  395.6 2.1 copy-start.6
  395.7 3.5 copy-start.1
  397.7 1.6 copy-start
  399.2 2.1 copy-start.10
  399.2 3.5 copy-start.4
  399.3 4.2 %copy-start.5 = (bf16[256,1152]{1,0:T(8,128)(2,1)S(1)}, bf16[256,1152]{1,0:T(8,128)(2,1)}, u32[]{:S(2)}) copy-start(bf16[256,1152]{1,0:T(8,128)(2,1)} %get-tuple-element.67) | copy-start | bytes 1769476
  399.3 5.0 %copy-start.8 = (f32[72,1728]{1,0:T(8,128)S(1)}, f32[72,1728]{1,0:T(8,128)}, u32[]{:S(2)}) copy-start(f32[72,1728]{1,0:T(8,128)} %get-tuple-element.107) | copy-start | bytes 1492996
  400.0 5.1 %copy-start.9 = (f32[72,576]{1,0:T(8,128)S(1)}, f32[72,576]{1,0:T(8,128)}, u32[]{:S(2)}) copy-start(f32[72,576]{1,0:T(8,128)} %get-tuple-element.110) | copy-start | bytes 497668
  402.7 3.1 copy-start.3
  403.5 3.1 copy-start.2

commit v5 on v4

--- a/solution.py
+++ b/solution.py
@@ -48,55 +48,108 @@
 VMEM = pl.BlockSpec(memory_space=pltpu.VMEM)
 ZS = 4
 TILE = 256
-MID = (1,)
+PARTS = (
+    (0, 0, 72, 0, 1152, False),
+    (0, 0, 72, 1152, 1152, False),
+    (1, 0, 72, 0, 896, True),
+    (1, 0, 72, 896, 832, False),
+    (2, 0, 72, 0, 576, True),
+)
 ORDER = (
+    (0, 4, 0),
+    (0, 4, 1),
+    (0, 2, 0),
+    (0, 0, 0),
+    (0, 2, 1),
+    (2, 4, 3),
+    (2, 4, 0),
+    (0, 3, 0),
+    (2, 4, 4),
+    (2, 2, 0),
     (0, 1, 0),
-    (0, 0, 0),
+    (2, 2, 3),
+    (2, 2, 4),
+    (2, 4, 1),
+    (2, 2, 5),
+    (2, 4, 5),
+    (0, 1, 1),
+    (1, 1, 0),
+    (2, 4, 2),
+    (2, 2, 1),
+    (1, 3, 0),
+    (0, 3, 1),
+    (1, 0, 0),
+    (2, 1, 3),
+    (1, 1, 1),
+    (0, 0, 1),
+    (2, 3, 3),
+    (2, 1, 4),
     (2, 1, 0),
-    (1, 0, 0),
-    (0, 0, 1),
-    (0, 1, 1),
+    (2, 2, 2),
+    (2, 1, 5),
     (2, 0, 0),
+    (2, 3, 0),
+    (1, 3, 1),
+    (2, 1, 1),
     (1, 0, 1),
-    (2, 1, 1),
+    (1, 4, 0),
     (2, 1, 2),
+    (2, 3, 1),
+    (2, 0, 3),
     (2, 0, 1),
-    (1, 1, 0),
+    (2, 3, 2),
+    (2, 3, 4),
+    (2, 0, 4),
+    (1, 2, 0),
+    (2, 3, 5),
+    (3, 4, 0),
     (2, 0, 2),
     (3, 1, 0),
+    (2, 0, 5),
+    (3, 2, 0),
+    (3, 3, 0),
     (3, 0, 0),
 )
-BACK_MID = ()
+BACK_PARTS = (
+    (0, 0, 144, 0, 576, False),
+    (0, 144, 144, 0, 576, False),
+)
 BACK_ORDER = (
     (0, -1, 0),
     (1, -1, 0),
+    (0, 1, 0),
+    (1, -1, 1),
     (0, 0, 0),
+    (1, -1, 2),
     (0, 0, 1),
-    (1, -1, 1),
-    (1, -1, 2),
     (2, -1, 0),
-    (0, 1, 0),
+    (1, 1, 0),
     (3, -1, 0),
     (4, -1, 0),
+    (1, 0, 0),
     (5, -1, 0),
+    (0, 1, 1),
+    (2, 1, 0),
     (5, -1, 1),
-    (1, 0, 0),
+    (5, -1, 2),
     (1, 0, 1),
-    (5, -1, 2),
-    (1, 1, 0),
-    (0, 1, 1),
     (2, 0, 0),
+    (1, 1, 1),
     (2, 0, 1),
+    (2, 1, 3),
     (5, -1, 3),
-    (1, 1, 1),
-    (2, 1, 0),
+    (2, 1, 1),
     (6, -1, 0),
+    (2, 1, 2),
+    (2, 0, 3),
+    (2, 0, 4),
+    (7, -1, 0),
+    (2, 1, 4),
+    (8, -1, 0),
+    (2, 0, 5),
     (2, 0, 2),
     (3, 0, 0),
-    (2, 1, 1),
-    (2, 1, 2),
-    (7, -1, 0),
-    (8, -1, 0),
+    (2, 1, 5),
     (3, 1, 0),
 )
 BACK_TASKS = ("seed", "widen", "mix", "centre", "project", "attend", "part", "query", "leave")
@@ -758,17 +811,44 @@
     return out
 
 
+class Swap:
+    def __init__(self, at, w, ins, bufs, sems):
+        self.left, halves = ins
+        self.right, away = halves.at[at.c], halves.at[1 - at.c]
+        self.left_sib, self.right_sib = bufs
+        send, recv = sems
+        pairs = ((self.left, self.left_sib), (away, self.right_sib))
+        self.copies = lambda: [
+            remote(src, dst, send.at[w, s], recv.at[w, s], at.i, 1 - at.c)
+            for s, (src, dst) in enumerate(pairs)
+        ]
+        self.arrived = False
+
+    def begin(self, part):
+        self.copies()[part].start()
+
+    def ready(self):
+        if not self.arrived:
+            for copy in self.copies():
+                copy.wait_recv()
+        self.arrived = True
+
+    def finish(self):
+        for copy in self.copies():
+            copy.wait_send()
+
+
 class Scatter:
-    def __init__(self, at, k, ins, result, bufs, sems):
-        self.at, self.k = at, k
-        self.left, halves = ins
-        self.right, self.away = halves.at[at.c], halves.at[1 - at.c]
-        self.result = result
-        self.left_sib, self.right_sib, self.held, self.near, self.far, self.line = bufs
+    def __init__(self, at, k, swap, part, result, bufs, sems):
+        self.at, self.k, self.swap = at, k, swap
+        _, self.first_row, rows, self.first_column, columns, _ = part
+        self.rows = rows
+        self.result = result.at[
+            pl.ds(self.first_row, rows), pl.ds(self.first_column, columns)
+        ]
+        self.held, self.near, self.far, self.line = bufs
         self.mid = self.line.shape[2] == 2
         (
-            self.swap_send,
-            self.swap_recv,
             self.near_send,
             self.near_recv,
             self.far_send,
@@ -776,16 +856,6 @@
             self.line_send,
             self.line_recv,
         ) = sems
-
-    def swaps(self):
-        at, k = self.at, self.k
-        pairs = ((self.left, self.left_sib), (self.away, self.right_sib))
-        return [
-            remote(
-                src, dst, self.swap_send.at[k, s], self.swap_recv.at[k, s], at.i, 1 - at.c
-            )
-            for s, (src, dst) in enumerate(pairs)
-        ]
 
     def near_copies(self, level):
         at, k = self.at, self.k
@@ -840,9 +910,6 @@
             else:
                 pl.when(self.at.z < ZS - 1)(copy.wait_recv)
 
-    def begin(self, part):
-        self.swaps()[part].start()
-
     def clear(self):
         zeros = jnp.zeros(self.line.shape[3:], self.line.dtype)
 
@@ -861,39 +928,39 @@
                     self.line[1, level, slot] = zeros
 
     def multiply(self, level):
-        cols = self.held.shape[-1]
-        rows = self.left.shape[0] // 16
-        group = max(1, 288 // rows)
+        cols, rows, swap = self.held.shape[-1], self.rows, self.swap
+        whole = swap.left.shape[0] // 16
+        group = max(1, 288 // rows) if rows == whole else 1
         height = group * rows
         wide = cols // TILE
 
-        def block(part, columns):
-            where = pl.ds(pl.multiple_of((level * 4 + part * group) * rows, 32), height)
+        def block(part, start, width):
+            where = pl.ds(
+                pl.multiple_of((level * 4 + part * group) * whole + self.first_row, 16), height
+            )
+            columns = pl.ds(pl.multiple_of(self.first_column + start, 128), width)
             value = jnp.dot(
-                self.left[where, :], self.right[:, columns], preferred_element_type=jnp.float32
+                swap.left[where, :], swap.right[:, columns], preferred_element_type=jnp.float32
             ) + jnp.dot(
-                self.left_sib[where, :],
-                self.right_sib[:, columns],
+                swap.left_sib[where, :],
+                swap.right_sib[:, columns],
                 preferred_element_type=jnp.float32,
             )
+            spot = pl.ds(pl.multiple_of(start, 128), width)
             for g in range(group):
                 piece = value[g * rows : (g + 1) * rows]
                 if len(self.held.shape) == 4:
                     piece = piece.reshape((rows // 8, 8, piece.shape[-1]))
-                self.held[level * 4 + part * group + g, ..., columns] = piece.astype(jnp.bfloat16)
+                self.held[level * 4 + part * group + g, ..., spot] = piece.astype(jnp.bfloat16)
 
         @pl.loop(0, 4 // group)
         def _(part):
             @pl.loop(0, wide)
             def _(t):
-                block(part, pl.ds(pl.multiple_of(t * TILE, TILE), TILE))
+                block(part, t * TILE, TILE)
 
             if cols % TILE:
-                block(part, pl.ds(wide * TILE, cols % TILE))
-
-    def ready(self):
-        for copy in self.swaps():
-            copy.wait_recv()
+                block(part, wide * TILE, cols % TILE)
 
     def stage_near(self, pair):
         @pl.loop(0, 2)
@@ -948,12 +1015,11 @@
             self.held[j] = total(*values).astype(jnp.bfloat16)
             copy.start()
 
-    def stage_line(self, back):
-        z = self.at.z
-        if back < ZS - 1:
-            up, down = ZS - 1 - back, back
-            pl.when(z < up)(lambda: self.pass_on(0, up))
-            pl.when(z > down)(lambda: self.pass_on(1, down))
+    def stage_line(self, part):
+        way, back = part // 3, part % 3
+        level = back if way else ZS - 1 - back
+        beyond = self.at.z > level if way else self.at.z < level
+        pl.when(beyond)(lambda: self.pass_on(way, level))
 
     def stage_own(self, _):
         z = self.at.z
@@ -973,8 +1039,6 @@
 
     def finish(self):
         z = self.at.z
-        for copy in self.swaps():
-            copy.wait_send()
 
         if self.mid:
             self.far_copy(z).wait_send()
@@ -1022,10 +1086,9 @@
             self.tokens,
         ) = ins[:12]
         self.own, self.sib = ins[12:16], ins[16:20]
-        self.d_attn, self.d_split, self.grad_tokens, self.note = outs
+        self.d_attn, self.d_split, self.grad_tokens, self.note, self.d_hidden = outs
         (
             self.d_branch,
-            self.d_hidden,
             self.flow,
             self.d_middle,
             self.d_attended,
@@ -1114,7 +1177,6 @@
             self.sums_fc1[:, columns] = fold(d_hidden.astype(jnp.float32))
 
         if part == 2:
-            self.jobs[1].begin(1)
             self.fetch(1, 0)
 
     def mix(self, _):
@@ -1238,17 +1300,30 @@
         self.note[14:16, :] = jnp.zeros((2, D), jnp.float32)
 
 
-def scatter_bufs(terms):
+def scatter_bufs(pairs, parts):
     scratch = []
-    for left, halves, shard, mid in terms:
-        piece = blocked(shard.shape)
+    for left, halves in pairs:
         scratch.append(pltpu.VMEM(left.shape, jnp.bfloat16))
-        scratch.append(pltpu.VMEM((SEQ, shard.shape[1]), jnp.bfloat16))
+        scratch.append(pltpu.VMEM(halves[1:], jnp.bfloat16))
+    for _, _, rows, _, columns, mid in parts:
+        piece = blocked((rows, columns))
         for lead in ((16,), (ZS, 2), (1 if mid else ZS,), (2, ZS, 2 if mid else 1)):
             scratch.append(pltpu.VMEM(lead + piece, jnp.bfloat16))
-    dma, count = pltpu.SemaphoreType.DMA, len(terms)
-    pairs = ((count, 2), (count, ZS, 2), (count, ZS), (count, 2, ZS, 2))
-    return scratch + [dma(shape) for shape in pairs for _ in range(2)]
+    dma, count = pltpu.SemaphoreType.DMA, len(parts)
+    kinds = ((len(pairs), 2), (count, ZS, 2), (count, ZS), (count, 2, ZS, 2))
+    return scratch + [dma(shape) for shape in kinds for _ in range(2)]
+
+
+def scatter_jobs(at, ins, results, take, parts):
+    bufs = [take(2) for _ in ins]
+    pieces = [take(4) for _ in parts]
+    swap_sems, sems = take(2), take(6)
+    swaps = [Swap(at, w, ins[w], bufs[w], swap_sems) for w in range(len(ins))]
+    jobs = [
+        Scatter(at, k, swaps[part[0]], part, results[part[0]], pieces[k], sems)
+        for k, part in enumerate(parts)
+    ]
+    return swaps, jobs
 
 
 def back_kernel(*refs):
@@ -1259,30 +1334,23 @@
         del refs[:n]
         return out
 
-    lefts, ins = take(2), take(20)
-    results, outs = take(2), take(4)
-    scratch = take(15)
-    bufs = [take(6) for _ in range(2)]
-    sems = take(8)
+    lefts, ins = take(1), take(20)
+    results, outs = take(1), take(5)
+    scratch = take(14)
     at = Place()
     at.greet()
-    jobs = [
-        Scatter(at, k, (lefts[k], scratch[k]), results[k], bufs[k], sems) for k in range(2)
-    ]
+    swaps, jobs = scatter_jobs(at, [(lefts[0], scratch[0])], results, take, BACK_PARTS)
+    swaps[0].begin(0)
     for job in jobs:
-        job.begin(0)
         job.clear()
-    backward = Backward(at, ins, outs, scratch, jobs)
-    seen = set()
+    backward = Backward(at, ins, outs, scratch, swaps)
     for stage, k, part in BACK_ORDER:
         if k < 0:
             getattr(backward, BACK_TASKS[stage])(part)
             continue
-        if k not in seen:
-            jobs[k].ready()
-            seen.add(k)
+        jobs[k].swap.ready()
         getattr(jobs[k], "stage_" + STAGES[stage])(part)
-    for job in jobs:
+    for job in swaps + jobs:
         job.finish()
 
 
@@ -1293,10 +1361,10 @@
         ((2, SEQ, 3 * D // 2), bf16),
         ((SEQ, D), bf16),
         ((16, D), f32),
+        ((2, SEQ, 2 * D), bf16),
     ]
     own = [
         ((2, SEQ, D // 2), bf16),
-        ((2, SEQ, 2 * D), bf16),
         ((SEQ, D), f32),
         ((SEQ, D), f32),
         ((SEQ, D), bf16),
@@ -1309,22 +1377,22 @@
         ((2, 384, 3 * D // 2), bf16),
     ]
     dma = pltpu.SemaphoreType.DMA
-    terms = [(left, None, shard, k in BACK_MID) for k, (left, shard) in enumerate(zip(lefts, shards))]
+    pairs = [(lefts[0], (2, SEQ, D // 2))]
     outs = pl.pallas_call(
         back_kernel,
         out_shape=[jax.ShapeDtypeStruct(shard.shape, f32) for shard in shards]
         + [jax.ShapeDtypeStruct(*kind) for kind in kinds],
-        in_specs=[VMEM] * 14 + [ANY] * 8,
+        in_specs=[VMEM] * 13 + [ANY] * 8,
         out_specs=[VMEM] * 6,
         scratch_shapes=[pltpu.VMEM(*kind) for kind in own]
         + [dma((2, 2)), dma((2,)), dma((2,))]
-        + scatter_bufs(terms),
+        + scatter_bufs(pairs, BACK_PARTS),
         compiler_params=pltpu.CompilerParams(
             collective_id=1, has_side_effects=True, vmem_limit_bytes=VMEM_LIMIT
         ),
         name="back_all",
     )(*lefts, *ins)
-    return outs[:2], outs[2:]
+    return outs[:1], outs[1:]
 
 
 def scatter_kernel(count, *refs):
@@ -1339,8 +1407,10 @@
     note, w_ada = take(2)
     results = take(count)
     note_own, note_sib, d_silu = take(3)
-    bufs = [take(6) for _ in range(count)]
-    sems, note_sems = take(8), take(6)
+    at = Place()
+    at.greet()
+    swaps, jobs = scatter_jobs(at, ins, results, take, PARTS)
+    note_sems = take(6)
     ada, ada_sem = take(2)
 
     def ada_copy(part):
@@ -1355,14 +1425,12 @@
         value = jnp.dot(row, ada[part % 2], preferred_element_type=jnp.float32)
         d_silu[...] = value if part == 0 else d_silu[...] + value
 
-    at = Place()
-    at.greet()
-    jobs = [Scatter(at, k, ins[k], results[k], bufs[k], sems) for k in range(count)]
     word = Gather(at, 0, note, note_own, note_sib, note_sems)
     whisper = [action for _, action in sorted(word.events(0.0, 1.0), key=lambda item: item[0])]
+    for swap in swaps:
+        swap.begin(0)
+        swap.begin(1)
     for job in jobs:
-        job.begin(0)
-        job.begin(1)
         job.clear()
 
     def speak(n):
@@ -1372,17 +1440,14 @@
 
     ada_copy(0).start()
     speak(1)
-    seen = set()
     for turn, (stage, k, part) in enumerate(ORDER):
-        if k not in seen:
-            jobs[k].ready()
-            seen.add(k)
+        jobs[k].swap.ready()
         getattr(jobs[k], "stage_" + STAGES[stage])(part)
-        speak(2)
+        speak(1)
         if turn % 2 and turn < 12:
             silu_part(turn // 2)
     speak(len(whisper))
-    for job in jobs:
+    for job in swaps + jobs:
         job.finish()
     word.complete()
     word.finish()
@@ -1392,16 +1457,14 @@
     count = len(pairs)
     spread = jax.ShapeDtypeStruct((16 * note.shape[0], note.shape[1]), note.dtype)
     dma = pltpu.SemaphoreType.DMA
-    terms = [
-        (left, halves, shard, k in MID) for k, ((left, halves), shard) in enumerate(zip(pairs, shards))
-    ]
+    shapes = [(left, halves.shape) for left, halves in pairs]
     outs = pl.pallas_call(
         functools.partial(scatter_kernel, count),
         out_shape=[jax.ShapeDtypeStruct(shard.shape, jnp.float32) for shard in shards]
         + [spread, spread, jax.ShapeDtypeStruct((16, D), jnp.float32)],
         in_specs=[VMEM, VMEM] * count + [VMEM, ANY],
         out_specs=[VMEM] * count + [ANY, ANY, VMEM],
-        scratch_shapes=scatter_bufs(terms)
+        scratch_shapes=scatter_bufs(shapes, PARTS)
         + gather_sems(1)
         + [pltpu.VMEM((2, D, D), jnp.bfloat16), dma((2,))],
         compiler_params=pltpu.CompilerParams(
@@ -1538,13 +1601,13 @@
             qkv_all,
             tokens.reshape(SEQ, D),
         ]
-        (grad_fc2, grad_fc1), outs = back_all(
-            [active_t, mlp_in_t], ins_back + list(own[1:]) + list(sib[1:]), [w_fc2, w_fc1]
-        )
-        d_attn, d_split, grad_tokens, note = outs
-        pairs = [(attn_in_t, d_split), (attended_t, d_attn)]
-        (grad_qkv, grad_proj), note_own, note_sib, d_silu = scatter_all(
-            pairs, [w_qkv, w_proj], note, w_ada
+        (grad_fc2,), outs = back_all(
+            [active_t], ins_back + list(own[1:]) + list(sib[1:]), [w_fc2]
+        )
+        d_attn, d_split, grad_tokens, note, d_hidden = outs
+        pairs = [(mlp_in_t, d_hidden), (attn_in_t, d_split), (attended_t, d_attn)]
+        (grad_fc1, grad_qkv, grad_proj), note_own, note_sib, d_silu = scatter_all(
+            pairs, [w_fc1, w_qkv, w_proj], note, w_ada
         )
         d_silu = d_silu[0:1]
         result, grad_tokens = result.reshape(tokens.shape), grad_tokens.reshape(tokens.shape)

time: 408 us -> 398 us (0.975)
  Pallas kernels: 385 us -> 373 us
    pallas_call x1, Pallas kernels: 144 us -> 97.9 us  [back_all(): pl.pallas_call(back_kernel, out_shape=[jax.ShapeDtypeStruct(shard.shape,...]
    pallas_call x1, Pallas kernels: 82.2 us -> 116 us  [scatter_all(): pl.pallas_call(functools.partial(scatter_kernel, count), out_shape=[jax.S...]
where the time goes in v5:
time: 398 us; the launch traced here: 396 us
  Pallas kernels  373 us (94%)
  local copies, waits for them, and re-layouts  13.1 us (3%)
  other arithmetic  5.63 us (1%)
    pallas_call x1, Pallas kernels, gather_all(): pl.pallas_call(functools.partial(gather_kernel, count), out_shape=spread...  159 us
    pallas_call x1, Pallas kernels, scatter_all(): pl.pallas_call(functools.partial(scatter_kernel, count), out_shape=[jax.S...  116 us
    pallas_call x1, Pallas kernels, back_all(): pl.pallas_call(back_kernel, out_shape=[jax.ShapeDtypeStruct(shard.shape,...  97.9 us
    unnamed x36, local copies, waits for them, and re-layouts  9.16 us

profile of v5, /device:TPU:16, one launch (start us, length us, event | category | flops | bytes accessed | tf_op | source)
XLA Modules:
  0.0 395.9 jit_solution(3683288010019061202)
XLA Ops:
  0.6 1.3 fusion.7
  3.9 0.7 convert_element_type.28
  4.6 0.7 convert_reduce_fusion
  5.4 0.7 maximum_maximum_fusion.refs_0_.refs_2_
  6.1 0.7 constant_dynamic-update-slice_fusion.7
  6.8 0.7 constant_dynamic-update-slice_fusion.5
  7.5 0.7 constant_dynamic-update-slice_fusion.4
  8.2 0.7 constant_dynamic-update-slice_fusion.3
  8.9 0.7 constant_dynamic-update-slice_fusion.2
  9.6 0.8 constant_dynamic-update-slice_fusion.1
  10.4 0.6 reshape.93.refs_8_
  11.0 158.7 %gather_all.1 = (f32[256,128]{1,0:T(8,128)}, bf16[1152,1728]{1,0:T(8,128)(2,1)}, bf16[1152,576]{1,0:T(8,128)(2,1)}, bf16[1152,2304]{1,0:T(8,128)(2,1)}, bf16[460...) custom-call(f32[16,128]{1,0:T(8,128)} %maximum_maximum_fusion.refs_0, ...), custom_call_target="tpu_custom_call" | custom-call | tf_op jit(solution)/shard_map/gather_all/pallas_call | solution.py:782
  169.8 97.9 %back_all.1 = (f32[288,576]{1,0:T(8,128)}, bf16[2,256,576]{2,1,0:T(8,128)(2,1)}, bf16[2,256,1728]{2,1,0:T(8,128)(2,1)}, bf16[256,1152]{1,0:T(8,128)(2,1)}, f32[1...) custom-call(bf16[4608,256]{1,0:T(8,128)(2,1)} %get-tuple-element.49.refs_0_, f32[6,8,1152]{2,1,0:T(8,128)} %get-tuple-element.50.refs_1_, ...), custom_call_target="tpu_custom_call" | custom-call | tf_op jit(solution)/shard_map/back_all/pallas_call | solution.py:1381
  267.7 116.3 %scatter_all.1 = (f32[72,2304]{1,0:T(8,128)}, f32[72,1728]{1,0:T(8,128)}, f32[72,576]{1,0:T(8,128)}, f32[256,1152]{1,0:T(8,128)}, f32[256,1152]{1,0:T(8,128)}, /*index=5*/f32[16,1152]{1,0:T(8,128)}) custom-call(bf16[1152,256]{1,0:T(8,128)(2,1)} %get-tuple-element.68.refs_0_, bf16[2,256,2304]{2,1,0:T(8,128)(2,1)} %get-tuple-element.69.refs_1_, ...), custom_call_target="tpu_custom_call" | custom-call | tf_op jit(solution)/shard_map/scatter_all/pallas_call | solution.py:1461
  384.1 2.0 fusion
  386.3 1.4 fusion.1
  389.1 0.6 slice_reduce_fusion
  389.7 1.4 fusion.5
  391.1 0.8 copy.52
  391.9 0.8 copy.53
  392.8 0.8 copy.54
  393.5 0.7 copy.55
  394.2 0.8 copy.56
  395.1 0.9 copy.57
  (40 shorter events, 1.6 us)
Async XLA Ops:
  384.1 2.1 copy-start.7
  384.1 2.1 copy-start.6
  384.1 3.5 copy-start.1
  386.1 1.6 copy-start
  387.6 2.1 copy-start.10
  387.6 3.5 copy-start.4
  387.7 4.2 %copy-start.5 = (bf16[256,1152]{1,0:T(8,128)(2,1)S(1)}, bf16[256,1152]{1,0:T(8,128)(2,1)}, u32[]{:S(2)}) copy-start(bf16[256,1152]{1,0:T(8,128)(2,1)} %get-tuple-element.67) | copy-start | bytes 1769476
  387.7 5.0 %copy-start.8 = (f32[72,1728]{1,0:T(8,128)S(1)}, f32[72,1728]{1,0:T(8,128)}, u32[]{:S(2)}) copy-start(f32[72,1728]{1,0:T(8,128)} %get-tuple-element.109) | copy-start | bytes 1492996
  388.5 5.1 %copy-start.9 = (f32[72,576]{1,0:T(8,128)S(1)}, f32[72,576]{1,0:T(8,128)}, u32[]{:S(2)}) copy-start(f32[72,576]{1,0:T(8,128)} %get-tuple-element.112) | copy-start | bytes 497668
  391.1 3.1 copy-start.3
  391.9 3.1 copy-start.2
